TPU v7x, 32 devices: a whole 2x2x4 slice. The times are simulated.
32 devices in a mesh: dp: 2 (over x), ctx: 4 (over z), tp: 4 (over y, core).
Axes of the slice: x: 2, y: 2, z: 4, core: 2. Of those that a mesh axis runs over, the one named last changes fastest.
Arguments:
- teacher_in: bfloat16 [4, 512, 1600], P('dp', 'ctx'), may hold values from -6 to 6
- teacher_gain_a: bfloat16 [1600], replicated, may hold values from 0.5 to 1.5
- teacher_shift_a: bfloat16 [1600], replicated, may hold values from -3 to 3
- teacher_attn_in: bfloat16 [3, 1600, 1600], P(None, 'dp'), may hold values from -0.15625 to 0.15625
- teacher_attn_bias: bfloat16 [2, 1600], replicated, may hold values from -3 to 3
- teacher_attn_out: bfloat16 [1600, 1600], P('dp'), may hold values from -1.75 to 1.75
- teacher_out_bias: bfloat16 [1600], replicated, may hold values from -3 to 3
- teacher_gain_b: bfloat16 [1600], replicated, may hold values from 0.5 to 1.5
- teacher_shift_b: bfloat16 [1600], replicated, may hold values from -3 to 3
- teacher_up: bfloat16 [1600, 6400], P('dp', 'tp'), may hold values from -0.15625 to 0.15625
- teacher_up_bias: bfloat16 [6400], P('tp'), may hold values from -3 to 3
- teacher_down: bfloat16 [6400, 1600], P('tp', 'dp'), may hold values from -0.15625 to 0.15625
- teacher_down_bias: bfloat16 [1600], replicated, may hold values from -3 to 3
- student_in: bfloat16 [4, 512, 768], P('dp', 'ctx'), may hold values from -6 to 6
- student_gain_a: bfloat16 [768], replicated, may hold values from 0.5 to 1.5
- student_shift_a: bfloat16 [768], replicated, may hold values from -3 to 3
- student_attn_in: bfloat16 [3, 768, 768], P(None, 'dp', 'tp'), may hold values from -0.21875 to 0.21875
- student_attn_bias: bfloat16 [2, 768], P(None, 'tp'), may hold values from -3 to 3
- student_attn_out: bfloat16 [768, 768], P('tp', 'dp'), may hold values from -2.5 to 2.5
- student_out_bias: bfloat16 [768], replicated, may hold values from -3 to 3
- student_gain_b: bfloat16 [768], replicated, may hold values from 0.5 to 1.5
- student_shift_b: bfloat16 [768], replicated, may hold values from -3 to 3
- student_up: bfloat16 [768, 3072], P('dp', 'tp'), may hold values from -0.21875 to 0.21875
- student_up_bias: bfloat16 [3072], P('tp'), may hold values from -3 to 3
- student_down: bfloat16 [3072, 768], P('tp', 'dp'), may hold values from -0.21875 to 0.21875
- student_down_bias: bfloat16 [768], replicated, may hold values from -3 to 3
- out_grad: bfloat16 [4, 512, 768], P('dp', 'ctx'), may hold values from -6 to 6
- slot_lengths: int32 [4], replicated, may hold values from 1 to 512, 1536 in all
Outputs:
- teacher_result: bfloat16 [4, 512, 1600], P('dp', 'ctx')
- student_result: bfloat16 [4, 512, 768], P('dp', 'ctx')
- student_in_grad: float32 [4, 512, 768], P('dp', 'ctx')
- grad_gain_a: float32 [768], P(('dp', 'ctx'))
- grad_shift_a: float32 [768], P(('dp', 'ctx'))
- grad_attn_in: float32 [3, 768, 768], P(None, ('dp', 'ctx'), 'tp')
- grad_attn_bias: float32 [2, 768], P(None, 'tp')
- grad_attn_out: float32 [768, 768], P('tp', ('dp', 'ctx'))
- grad_out_bias: float32 [768], P(('dp', 'ctx'))
- grad_gain_b: float32 [768], P(('dp', 'ctx'))
- grad_shift_b: float32 [768], P(('dp', 'ctx'))
- grad_up: float32 [768, 3072], P(('dp', 'ctx'), 'tp')
- grad_up_bias: float32 [3072], P('tp')
- grad_down: float32 [3072, 768], P('tp', ('dp', 'ctx'))
- grad_down_bias: float32 [768], P(('dp', 'ctx'))
Inputs may be any that keep to these rules, and one draw needn't show every extreme that they name: `slot_lengths`: valid positions of each slot; the longest slot is full, and the lengths add up to 1536.
All inputs are finite; a program needn't handle non-finite values.
Results may differ from a plain program's by a relative error of at most 0.022.
Values may be sent and summed in bfloat16 or wider, within the bound.
No kernel may reach another device: no remote copies, remote signals or barrier semaphores. Data moves between devices by JAX's collectives and lax.ppermute only.
A program may use at most 192 MiB of HBM per device.

v0:
```python
import functools
import math

import jax
import jax.numpy as jnp
from jax import lax
from jax.experimental import pallas as pl
from jax.experimental.pallas import tpu as pltpu
from jax.sharding import PartitionSpec as P

HD = 64
PAIR = 2 * HD
EPS = 1e-05
MASKED = -1000000000.0
FAR = 1 << 30
BF = jnp.bfloat16
F32 = jnp.float32
GELU_C = math.sqrt(2.0 / math.pi)
SMEM = pl.BlockSpec(memory_space=pltpu.SMEM)
VMEM = pl.BlockSpec(memory_space=pltpu.VMEM)
ANY = pl.BlockSpec(memory_space=pl.ANY)
LIMIT = 60 * 1024 * 1024


def dense(left, right):
    return jnp.dot(left, right, preferred_element_type=F32)


def dense_tn(left, right):
    return lax.dot_general(left, right, (((0,), (0,)), ((), ())), preferred_element_type=F32)


def dense_nt(left, right):
    return lax.dot_general(left, right, (((1,), (1,)), ((), ())), preferred_element_type=F32)


def norm_parts(x):
    centered = x - jnp.mean(x, axis=-1, keepdims=True)
    spread = jnp.mean(centered * centered, axis=-1, keepdims=True)
    factor = lax.rsqrt(spread + EPS)
    return centered * factor, factor


def norm_back(d_out, xhat, factor, gain):
    e = d_out * gain
    return factor * (
        e - jnp.mean(e, axis=-1, keepdims=True) - xhat * jnp.mean(e * xhat, axis=-1, keepdims=True)
    )


def gelu_tanh(v):
    return 0.5 * v * (1.0 + jnp.tanh(GELU_C * (v + 0.044715 * v * v * v)))


def gelu_both(v):
    inner = jnp.tanh(GELU_C * (v + 0.044715 * v * v * v))
    slope = 0.5 * (1.0 + inner) + 0.5 * v * (1.0 - inner * inner) * GELU_C * (
        1.0 + 3.0 * 0.044715 * v * v
    )
    return 0.5 * v * (1.0 + inner), slope


BASE, DP, ODD, TP, CTX, LEN = 0, 1, 2, 3, 4, 5


def row(ref):
    return ref[...].astype(F32).reshape(1, -1)


def halves(info, x):
    mid = x.shape[-1] // 2
    first = info[DP] == 0
    left, right = x[:, :mid], x[:, mid:]
    return jnp.where(first, left, right), jnp.where(first, right, left)


def ordered(info, own_peer):
    mid = own_peer.shape[-1] // 2
    first = info[DP] == 0
    own, peer = own_peer[:, :mid], own_peer[:, mid:]
    return jnp.concatenate(
        [jnp.where(first, own, peer), jnp.where(first, peer, own)], axis=-1
    )


def run(kernel, name, outs, args, specs=None, scratch=(), flops=0, extra=0):
    out_shape = [jax.ShapeDtypeStruct(shape, kind) for shape, kind in outs]
    if specs is None:
        specs = [SMEM] + [VMEM] * (len(args) - 1)
    moved = sum(a.size * a.dtype.itemsize for a in args)
    moved += sum(math.prod(o.shape) * o.dtype.itemsize for o in out_shape)
    return pl.pallas_call(
        kernel,
        out_shape=out_shape,
        in_specs=specs,
        out_specs=[VMEM] * len(outs),
        scratch_shapes=list(scratch),
        compiler_params=pltpu.CompilerParams(vmem_limit_bytes=LIMIT),
        cost_estimate=pl.CostEstimate(
            flops=int(flops), bytes_accessed=int(moved), transcendentals=int(extra)
        ),
        name=name,
    )(*args)


def kv_tiles(heads):
    pairs = heads // 2
    return pairs, heads % 2, pairs * 2 * PAIR + (heads % 2) * PAIR


def put_kv(ref, k, v, heads):
    pairs, single, unused = kv_tiles(heads)
    for g in range(pairs):
        ref[:, 2 * g * PAIR:(2 * g + 1) * PAIR] = k[:, g * PAIR:(g + 1) * PAIR].astype(ref.dtype)
        ref[:, (2 * g + 1) * PAIR:(2 * g + 2) * PAIR] = v[:, g * PAIR:(g + 1) * PAIR].astype(
            ref.dtype
        )
    if single:
        tail = jnp.concatenate([k[:, pairs * PAIR:], v[:, pairs * PAIR:]], axis=1)
        ref[:, 2 * pairs * PAIR:] = tail.astype(ref.dtype)


def put_q(ref, q, heads):
    pairs, single, unused = kv_tiles(heads)
    q = q * (HD ** -0.5)
    ref[:, :pairs * PAIR] = q[:, :pairs * PAIR].astype(ref.dtype)
    if single:
        tail = q[:, pairs * PAIR:]
        ref[:, pairs * PAIR:] = jnp.concatenate([tail, jnp.zeros_like(tail)], axis=1).astype(
            ref.dtype
        )


def chunks_of(keys):
    width = math.gcd(keys, 512)
    return [(i * width, width) for i in range(keys // width)]


def key_rows(info, rows, blocks, chunks):
    out = []
    for start, width in chunks:
        place = start + lax.broadcasted_iota(jnp.int32, (1, width), 1)
        if blocks > 1:
            place = info[BASE] + place - 2 * rows * (place // rows)
            place = jnp.where(place < 0, FAR, place)
        out.append(place)
    return out


def soft(query, keys, places, bound):
    scores = [
        jnp.where(place <= bound, dense_nt(query, k), MASKED) for place, k in zip(places, keys)
    ]
    top = functools.reduce(jnp.maximum, [jnp.max(s, axis=-1, keepdims=True) for s in scores])
    raised = [jnp.exp(s - top) for s in scores]
    total = functools.reduce(jnp.add, [jnp.sum(r, axis=-1, keepdims=True) for r in raised])
    return raised, 1.0 / total


def add_all(items):
    return functools.reduce(jnp.add, items)


def query_bound(info, slot, rows):
    place = info[BASE] + lax.broadcasted_iota(jnp.int32, (rows, 1), 0)
    return jnp.minimum(place, info[LEN + slot] - 1)


def attend_slot(query_of, kv_of, heads, rows, places, bound):
    pairs, single, unused = kv_tiles(heads)
    lane = lax.broadcasted_iota(jnp.int32, (rows, PAIR), 1)
    low = lane < HD
    out = []
    for g in range(pairs):
        query = query_of(g)
        keys, values = kv_of(2 * g), kv_of(2 * g + 1)
        held = []
        for part in (low, jnp.logical_not(low)):
            one = jnp.where(part, query, jnp.zeros_like(query))
            raised, inverse = soft(one, keys, places, bound)
            held.append(add_all([dense(r.astype(BF), v) for r, v in zip(raised, values)]) * inverse)
        out.append(jnp.where(low, held[0], held[1]))
    if single:
        keys = kv_of(2 * pairs)
        raised, inverse = soft(query_of(pairs), keys, places, bound)
        held = add_all([dense(r.astype(BF), v) for r, v in zip(raised, keys)]) * inverse
        out.append(held[:, HD:])
    return out


def load_blocks(kv_s, kv_refs, slot, rows):
    if kv_s is not None:
        for i, ref in enumerate(kv_refs):
            kv_s[i * rows:(i + 1) * rows, :] = ref[slot]


def kv_reader(kv_s, kv_refs, slot, chunks):
    def kv_of(tile):
        if kv_s is not None:
            return [kv_s[a:a + w, tile * PAIR:(tile + 1) * PAIR] for a, w in chunks]
        return [kv_refs[0][slot, a:a + w, tile * PAIR:(tile + 1) * PAIR] for a, w in chunks]
    return kv_of


def student_attend_kernel(heads, blocks, info, q_ref, own_ref, peer_ref, *refs):
    kv_refs = refs[:blocks]
    att_ref, give_ref, keep_ref = refs[blocks:blocks + 3]
    kv_s = refs[blocks + 3] if blocks > 1 else None
    slots, rows, unused = q_ref.shape
    keys = blocks * kv_refs[0].shape[1]
    chunks = chunks_of(keys)
    half = own_ref.shape[1]

    def one_slot(i, carry):
        slot = jnp.where(i == 0, 1 - info[ODD], info[ODD])
        load_blocks(kv_s, kv_refs, slot, rows)
        out = attend_slot(
            lambda g: q_ref[slot, :, g * PAIR:(g + 1) * PAIR],
            kv_reader(kv_s, kv_refs, slot, chunks),
            heads,
            rows,
            key_rows(info, rows, blocks, chunks),
            query_bound(info, slot, rows),
        )
        att = jnp.concatenate(out, axis=1).astype(BF)
        att_ref[slot] = att
        part = jnp.concatenate([dense(att, own_ref[...]), dense(att, peer_ref[...])], axis=1)

        @pl.when(i == 0)
        def _():
            give_ref[...] = part.astype(BF)

        @pl.when(i == 1)
        def _():
            keep_ref[...] = part

        return carry

    lax.fori_loop(0, slots, one_slot, 0)


def teacher_attend_kernel(heads, blocks, info, q_ref, *refs):
    kv_refs = refs[:blocks]
    att_ref, tail_ref = refs[blocks:blocks + 2]
    kv_s = refs[blocks + 2] if blocks > 1 else None
    slots, rows, unused = q_ref.shape
    chunks = chunks_of(blocks * kv_refs[0].shape[1])
    pairs = heads // 2

    def one_slot(slot, carry):
        load_blocks(kv_s, kv_refs, slot, rows)
        out = attend_slot(
            lambda g: q_ref[slot, :, g * PAIR:(g + 1) * PAIR],
            kv_reader(kv_s, kv_refs, slot, chunks),
            heads,
            rows,
            key_rows(info, rows, blocks, chunks),
            query_bound(info, slot, rows),
        )
        for g in range(pairs):
            att_ref[slot, :, g * PAIR:(g + 1) * PAIR] = out[g].astype(BF)
        tail_ref[slot] = out[pairs].astype(BF)
        return carry

    lax.fori_loop(0, slots, one_slot, 0)


def keep_mask(info, slots, rows):
    row = lax.broadcasted_iota(jnp.int32, (rows, 1), 0) + info[BASE]
    return jnp.concatenate([row < info[LEN + s] for s in range(slots)], axis=0)


def student_back_kernel(
    heads, blocks, info, mid_ref, gain, r_ref, other_ref, grad_ref, own_ref, peer_ref, q_ref, *refs
):
    kv_refs = refs[:blocks]
    d_mid_ref, d_a_ref, d_q_ref, sums_ref = refs[blocks:blocks + 4]
    d_refs = refs[blocks + 4:2 * blocks + 4]
    d_att_s = refs[2 * blocks + 4]
    d_s = refs[2 * blocks + 5]
    kv_s = refs[2 * blocks + 6] if blocks > 1 else None
    slots, rows, unused = q_ref.shape
    chunks = chunks_of(blocks * kv_refs[0].shape[1])
    pairs, single, unused = kv_tiles(heads)
    scale = HD ** -0.5

    d_s[pl.ds(info[ODD] * rows, rows), :] = ordered(info, r_ref[...]).astype(F32)
    d_s[pl.ds((1 - info[ODD]) * rows, rows), :] = ordered(info, other_ref[...]).astype(F32)
    xhat, factor = norm_parts(mid_ref[...])
    d_norm = d_s[...]
    cot = jnp.where(keep_mask(info, slots, rows), grad_ref[...].astype(F32), 0.0)
    d_mid = cot + norm_back(d_norm, xhat, factor, row(gain))
    d_a = d_mid.astype(BF)
    d_mid_ref[...] = d_mid
    d_a_ref[...] = d_a
    sums_ref[0:1, :] = jnp.sum(d_norm * xhat, axis=0, keepdims=True)
    sums_ref[1:2, :] = jnp.sum(d_norm, axis=0, keepdims=True)
    sums_ref[2:3, :] = jnp.sum(d_a.astype(F32), axis=0, keepdims=True)
    mine, theirs = halves(info, d_a)
    d_att = dense_nt(mine, own_ref[...]) + dense_nt(theirs, peer_ref[...])
    width = heads * HD
    d_att_s[:, :pairs * PAIR] = d_att[:, :pairs * PAIR].astype(BF)
    if single:
        tail = d_att[:, pairs * PAIR:width]
        d_att_s[:, pairs * PAIR:] = jnp.concatenate([jnp.zeros_like(tail), tail], axis=1).astype(BF)

    def put(slot, tile, i, value):
        start, size = chunks[i]
        if blocks == 1:
            d_refs[0][slot, start:start + size, tile * PAIR:(tile + 1) * PAIR] = value.astype(
                d_refs[0].dtype
            )
        else:
            for b in range(blocks):
                d_refs[b][slot, :, tile * PAIR:(tile + 1) * PAIR] = value[
                    b * rows:(b + 1) * rows
                ].astype(d_refs[b].dtype)

    def one_slot(slot, carry):
        load_blocks(kv_s, kv_refs, slot, rows)
        kv_of = kv_reader(kv_s, kv_refs, slot, chunks)
        places = key_rows(info, rows, blocks, chunks)
        bound = query_bound(info, slot, rows)
        low = lax.broadcasted_iota(jnp.int32, (rows, PAIR), 1) < HD
        row0 = pl.multiple_of(slot * rows, rows)

        def head(query, d_out, keys, values):
            raised, inverse = soft(query, keys, places, bound)
            probs = [r * inverse for r in raised]
            d_probs = [dense_nt(d_out, v) for v in values]
            delta = add_all(
                [jnp.sum(p * d, axis=-1, keepdims=True) for p, d in zip(probs, d_probs)]
            )
            d_scores = [(p * (d - delta)).astype(BF) for p, d in zip(probs, d_probs)]
            d_query = add_all([dense(s, k) for s, k in zip(d_scores, keys)]) * scale
            d_keys = [dense_tn(s, query) for s in d_scores]
            d_values = [dense_tn(p.astype(BF), d_out) for p in probs]
            return d_query, d_keys, d_values

        for g in range(pairs):
            query = q_ref[slot, :, g * PAIR:(g + 1) * PAIR]
            d_out = d_att_s[pl.ds(row0, rows), g * PAIR:(g + 1) * PAIR]
            keys, values = kv_of(2 * g), kv_of(2 * g + 1)
            zero = jnp.zeros_like(query)
            a = head(jnp.where(low, query, zero), jnp.where(low, d_out, zero), keys, values)
            b = head(jnp.where(low, zero, query), jnp.where(low, zero, d_out), keys, values)
            d_q_ref[slot, :, g * PAIR:(g + 1) * PAIR] = jnp.where(low, a[0], b[0]).astype(BF)
            for i in range(len(chunks)):
                put(slot, 2 * g, i, a[1][i] + b[1][i])
                put(slot, 2 * g + 1, i, a[2][i] + b[2][i])
        if single:
            query = q_ref[slot, :, pairs * PAIR:]
            d_out = d_att_s[pl.ds(row0, rows), pairs * PAIR:]
            keys = kv_of(2 * pairs)
            a = head(query, d_out, keys, keys)
            d_q_ref[slot, :, pairs * PAIR:] = a[0][:, :HD].astype(BF)
            for i in range(len(chunks)):
                put(slot, 2 * pairs, i, a[1][i] + a[2][i])
        return carry

    lax.fori_loop(0, slots, one_slot, 0)


def student_qkv_kernel(heads, info, x, gain, shift, own, peer, bias, normed_ref, q_ref, kv_ref):
    xhat, unused = norm_parts(x[...].astype(F32))
    normed = (xhat * row(gain) + row(shift)).astype(BF)
    normed_ref[...] = normed
    mine, theirs = halves(info, normed)

    def project(i):
        return dense_nt(mine, own[i]) + dense_nt(theirs, peer[i])

    put_kv(kv_ref, project(1), project(2) + bias[1:2, :].astype(F32), heads)
    put_q(q_ref, (project(0) + bias[0:1, :].astype(F32)).astype(BF), heads)


def student_ffn_kernel(
    info, x, out_bias, gain, shift, up_bias, r_ref, other_ref, up_own, up_peer, down_own,
    down_peer, grad, mid_ref, normed_ref, act_ref, d_upper_ref, give_ref, keep_ref, part_s,
):
    rows = r_ref.shape[0]
    slots = x.shape[0] // rows
    keep_at = pl.multiple_of(info[ODD] * rows, rows)
    give_at = pl.multiple_of((1 - info[ODD]) * rows, rows)
    for at, ref in ((keep_at, r_ref), (give_at, other_ref)):
        mid_ref[pl.ds(at, rows), :] = (
            x[pl.ds(at, rows), :].astype(F32) + ordered(info, ref[...]).astype(F32) + row(out_bias)
        )
    xhat, unused = norm_parts(mid_ref[...])
    normed = (xhat * row(gain) + row(shift)).astype(BF)
    normed_ref[...] = normed
    mine, theirs = halves(info, normed)
    upper = dense(mine, up_own[...]) + dense(theirs, up_peer[...]) + row(up_bias)
    act, slope = gelu_both(upper)
    act_ref[...] = act.astype(BF)
    d_b = jnp.where(keep_mask(info, slots, rows), grad[...].astype(F32), 0.0).astype(BF)
    d_mine, d_theirs = halves(info, d_b)
    d_act = (dense_nt(d_mine, down_own[...]) + dense_nt(d_theirs, down_peer[...])).astype(BF)
    d_upper = (d_act.astype(F32) * slope).astype(BF)
    d_upper_ref[...] = d_upper
    half = up_own.shape[0]
    part_s[:, :half] = dense_nt(d_upper, up_own[...])
    part_s[:, half:] = dense_nt(d_upper, up_peer[...])
    give_ref[...] = part_s[pl.ds(give_at, rows), :].astype(BF)
    keep_ref[...] = part_s[pl.ds(keep_at, rows), :]


def split_rows(info, n_ctx, grad_s, give_ref, keep_ref):
    full = grad_s.shape[0]
    piece = full // (2 * n_ctx)
    bit = lax.rem(info[CTX], 2)
    for d in range(2):
        for j in range(n_ctx // 2):
            to = (d * (n_ctx // 2) + j) * piece
            base = (d * n_ctx + 2 * j) * piece
            keep_ref[to:to + piece, :] = grad_s[
                pl.ds(pl.multiple_of(base + bit * piece, 16), piece), :
            ]
            give_ref[to:to + piece, :] = grad_s[
                pl.ds(pl.multiple_of(base + (1 - bit) * piece, 16), piece), :
            ].astype(give_ref.dtype)


def student_ffn_grads_kernel(
    n_ctx, info, normed, act, d_upper, grad, down_own, down_peer,
    give_ref, keep_ref, part_give, part_keep, sums_ref, grad_s, part_s,
):
    rows = part_give.shape[0]
    slots = normed.shape[0] // rows
    d_b = jnp.where(keep_mask(info, slots, rows), grad[...].astype(F32), 0.0).astype(BF)
    hidden = act.shape[1]
    grad_s[:, :hidden] = dense_tn(d_b, act[...])
    grad_s[:, hidden:] = dense_tn(normed[...], d_upper[...])
    split_rows(info, n_ctx, grad_s, give_ref, keep_ref)
    cols = down_own.shape[1]
    part_s[:, :cols] = dense(act[...], down_own[...])
    part_s[:, cols:] = dense(act[...], down_peer[...])
    part_give[...] = part_s[pl.ds((1 - info[ODD]) * rows, rows), :].astype(BF)
    part_keep[...] = part_s[pl.ds(info[ODD] * rows, rows), :]
    sums_ref[0:1, :] = jnp.sum(d_b.astype(F32), axis=0, keepdims=True)
    sums_ref[1:2, :] = jnp.sum(d_upper[...].astype(F32), axis=0, keepdims=True)


def student_in_kernel(
    heads, n_got, n_ctx, info, d_q, normed, d_a, att, own, peer, d_kv, *refs
):
    gots = refs[:n_got]
    give_ref, keep_ref, g_give, g_keep, bias_ref, part_s, grad_s = refs[n_got:]
    rows = give_ref.shape[0]
    pairs, single, unused = kv_tiles(heads)
    total = d_kv[...].astype(F32)
    for got in gots:
        total = total + got[...].astype(F32)
    total = total.astype(BF)
    d_k = [total[:, 2 * g * PAIR:(2 * g + 1) * PAIR] for g in range(pairs)]
    d_v = [total[:, (2 * g + 1) * PAIR:(2 * g + 2) * PAIR] for g in range(pairs)]
    if single:
        d_k.append(total[:, 2 * pairs * PAIR:2 * pairs * PAIR + HD])
        d_v.append(total[:, 2 * pairs * PAIR + HD:])
    d_k = jnp.concatenate(d_k, axis=1)
    d_v = jnp.concatenate(d_v, axis=1)
    half = own.shape[2]

    def back(w):
        return dense(d_q[...], w[0]) + dense(d_k, w[1]) + dense(d_v, w[2])

    part_s[:, :half] = back(own)
    part_s[:, half:] = back(peer)
    give_ref[...] = part_s[pl.ds((1 - info[ODD]) * rows, rows), :].astype(BF)
    keep_ref[...] = part_s[pl.ds(info[ODD] * rows, rows), :]
    cols = heads * HD
    n = normed[...]
    grad_s[:, :cols] = dense_tn(n, d_q[...])
    grad_s[:, cols:2 * cols] = dense_tn(n, d_k)
    grad_s[:, 2 * cols:3 * cols] = dense_tn(n, d_v)
    grad_s[:, 3 * cols:] = dense_tn(d_a[...], att[...])
    split_rows(info, n_ctx, grad_s, g_give, g_keep)
    bias_ref[0:1, :] = jnp.sum(d_q[...].astype(F32), axis=0, keepdims=True)
    bias_ref[1:2, :] = jnp.sum(d_v.astype(F32), axis=0, keepdims=True)


def student_last_kernel(
    info, x, gain, r_ref, other_ref, d_mid, sums_b, sums_f, sums_q, out_ref, sums_ref, d_s
):
    rows = r_ref.shape[0]
    d_s[pl.ds(info[ODD] * rows, rows), :] = ordered(info, r_ref[...]).astype(F32)
    d_s[pl.ds((1 - info[ODD]) * rows, rows), :] = ordered(info, other_ref[...]).astype(F32)
    xhat, factor = norm_parts(x[...].astype(F32))
    d_norm = d_s[...]
    out_ref[...] = d_mid[...] + norm_back(d_norm, xhat, factor, row(gain))
    sums_ref[0:1, :] = jnp.sum(d_norm * xhat, axis=0, keepdims=True)
    sums_ref[1:2, :] = jnp.sum(d_norm, axis=0, keepdims=True)
    sums_ref[2:5, :] = sums_b[...]
    sums_ref[5:7, :] = sums_f[...]
    rest = out_ref.shape[1] - 2 * sums_q.shape[1]
    sums_ref[7:8, :] = jnp.concatenate(
        [sums_q[0:1, :], sums_q[1:2, :], jnp.zeros((1, rest), F32)], axis=1
    )


def teacher_norm_kernel(info, x, gain, shift, mine_ref, theirs_ref):
    xhat, unused = norm_parts(x[...].astype(F32))
    normed = (xhat * row(gain) + row(shift)).astype(BF)
    mine, theirs = halves(info, normed)
    mine_ref[...] = mine
    theirs_ref[...] = theirs


def teacher_qkv_kernel(
    heads, cols, info, mine, other, w_hbm, wo, give_ref, own_ref, wo_ref, w, w_tail, sems
):
    pairs, unused, kv_width = kv_tiles(heads)
    col0 = pl.multiple_of(info[TP] * cols, cols)
    wide = w_hbm.shape[2]
    tail = w_tail.shape[2]
    copies = [
        pltpu.make_async_copy(w_hbm.at[:, :, pl.ds(col0, cols)], w, sems.at[0]),
        pltpu.make_async_copy(w_hbm.at[:, :, pl.ds(wide - tail, tail)], w_tail, sems.at[1]),
    ]
    for copy in copies:
        copy.start()
    wo_ref[:, :cols] = wo[:, pl.ds(col0, cols)]
    last = wo[:, wide - tail:]
    wo_ref[:, cols:] = jnp.concatenate([last, jnp.zeros_like(last)], axis=1)
    for copy in copies:
        copy.wait()
    for source, target in ((other, give_ref), (mine, own_ref)):
        x = source[...]
        k, v, q = (dense(x, w[i]) for i in (1, 2, 0))
        tk, tv, tq = (dense(x, w_tail[i]) for i in (1, 2, 0))
        kind = target.dtype
        for g in range(pairs):
            a = 2 * g * PAIR
            target[:, a:a + PAIR] = k[:, g * PAIR:(g + 1) * PAIR].astype(kind)
            target[:, a + PAIR:a + 2 * PAIR] = v[:, g * PAIR:(g + 1) * PAIR].astype(kind)
        target[:, 2 * pairs * PAIR:kv_width] = jnp.concatenate([tk, tv], axis=1).astype(kind)
        target[:, kv_width:kv_width + cols] = q.astype(kind)
        target[:, kv_width + cols:] = jnp.concatenate([tq, jnp.zeros_like(tq)], axis=1).astype(kind)


def teacher_join_kernel(heads, cols, info, own, got, bias, kv_ref, q_ref):
    pairs, unused, kv_width = kv_tiles(heads)
    whole = own[...] + got[...].astype(F32)
    b = bias[:, pl.ds(pl.multiple_of(info[TP] * cols, cols), cols)].astype(F32)
    t = bias[:, bias.shape[1] - HD:].astype(F32)
    zero = jnp.zeros_like(t[0:1])
    for g in range(pairs):
        a = 2 * g * PAIR
        kv_ref[:, a:a + PAIR] = whole[:, a:a + PAIR].astype(BF)
        kv_ref[:, a + PAIR:a + 2 * PAIR] = (
            whole[:, a + PAIR:a + 2 * PAIR] + b[1:2, g * PAIR:(g + 1) * PAIR]
        ).astype(BF)
    a = 2 * pairs * PAIR
    kv_ref[:, a:] = (whole[:, a:kv_width] + jnp.concatenate([zero, t[1:2]], axis=1)).astype(BF)
    q = (whole[:, kv_width:] + jnp.concatenate([b[0:1], t[0:1], zero], axis=1)).astype(BF)
    q_ref[...] = (q * (HD ** -0.5)).astype(BF)


def teacher_out_kernel(info, every, tail, w, peer, out_ref, out_tail_ref, w_s):
    half = w.shape[0]
    n, unused, cols = every.shape
    extra = tail.shape[1]
    own_at = pl.multiple_of(info[DP] * half, 16)
    peer_at = pl.multiple_of((1 - info[DP]) * half, 16)
    w_s[pl.ds(own_at, half), :cols] = w[:, pl.ds(pl.multiple_of(info[TP] * cols, cols), cols)]
    last = w[:, w.shape[1] - extra:]
    w_s[pl.ds(own_at, half), cols:] = jnp.concatenate([last, jnp.zeros_like(last)], axis=1)
    w_s[pl.ds(peer_at, half), :] = peer[...]
    total = dense(tail[...], w_s[n * cols:, :])
    for i in range(n):
        total = total + dense(every[i], w_s[i * cols:(i + 1) * cols, :])
    out_ref[...] = total[:, :cols].astype(BF)
    out_tail_ref[...] = total[:, cols:cols + extra].astype(BF)


def teacher_ffn_kernel(
    tile, slab, info, x, out_bias, gain, shift, up_bias, every, tail, p_give, p_keep,
    up_own, up_peer, down_own, down_peer,
    mid_ref, give_ref, keep_ref, up_s, down_s, act_s, normed_s, part_s, sems,
):
    half, hidden = up_own.shape
    own_at = pl.multiple_of(info[DP] * half, 16)
    peer_at = pl.multiple_of((1 - info[DP]) * half, 16)
    copies = [
        pltpu.make_async_copy(up_own, up_s.at[pl.ds(own_at, half)], sems.at[0]),
        pltpu.make_async_copy(up_peer, up_s.at[pl.ds(peer_at, half)], sems.at[1]),
        pltpu.make_async_copy(down_own, down_s.at[0], sems.at[2]),
        pltpu.make_async_copy(down_peer, down_s.at[1], sems.at[3]),
    ]
    for copy in copies:
        copy.start()
    n, unused, cols = every.shape
    bias = row(out_bias)
    for i in range(n):
        a = i * cols
        mid_ref[:, a:a + cols] = (
            x[:, a:a + cols].astype(F32) + every[i].astype(F32) + bias[:, a:a + cols]
        )
    a = n * cols
    mid_ref[:, a:] = x[:, a:].astype(F32) + tail[...].astype(F32) + bias[:, a:]
    xhat, unused = norm_parts(mid_ref[...])
    normed_s[...] = (xhat * row(gain) + row(shift)).astype(BF)
    rows = give_ref.shape[0]
    packed = give_ref.shape[1]
    give_ref[:, 2 * slab:] = p_give[...]
    keep_ref[:, 2 * slab:] = p_keep[...]
    for copy in copies[:2]:
        copy.wait()
    up_row = row(up_bias)
    at = 0
    while at < hidden:
        size = min(tile, hidden - at)
        v = dense(normed_s[...], up_s[:, at:at + size]) + up_row[:, at:at + size]
        act_s[:, at:at + size] = gelu_tanh(v).astype(BF)
        at += size
    for copy in copies[2:]:
        copy.wait()
    width = down_own.shape[0]
    for i in range(2):
        part_s[:, :width] = dense_nt(act_s[...], down_s[i])
        a = i * slab
        give_ref[:, a:a + width] = part_s[pl.ds((1 - info[ODD]) * rows, rows), :width].astype(BF)
        keep_ref[:, a:a + width] = part_s[pl.ds(info[ODD] * rows, rows), :width]
        give_ref[:, a + width:a + slab] = jnp.zeros((rows, slab - width), BF)
        keep_ref[:, a + width:a + slab] = jnp.zeros((rows, slab - width), F32)


def last_kernel(slab, info, t_mid, s_mid, t_bias, s_bias, r_ref, other_ref, t_out, s_out):
    rows = r_ref.shape[0]
    width = t_out.shape[1] // 2
    keep_at = pl.multiple_of(info[ODD] * rows, rows)
    give_at = pl.multiple_of((1 - info[ODD]) * rows, rows)
    first = info[DP] == 0
    for at, ref in ((keep_at, r_ref), (give_at, other_ref)):
        own, peer = ref[:, :width].astype(F32), ref[:, slab:slab + width].astype(F32)
        branch = jnp.concatenate(
            [jnp.where(first, own, peer), jnp.where(first, peer, own)], axis=1
        )
        t_out[pl.ds(at, rows), :] = (
            t_mid[pl.ds(at, rows), :] + branch + row(t_bias)
        ).astype(BF)
        s_out[pl.ds(at, rows), :] = (
            s_mid[pl.ds(at, rows), :]
            + ordered(info, ref[:, 2 * slab:].astype(F32))
            + row(s_bias)
        ).astype(BF)


def make_body(n_dp, n_ctx, n_tp):
    near = n_ctx <= 4

    def swap(x, axis, size, bit):
        return lax.ppermute(x, axis, [(i, i ^ bit) for i in range(size)])

    def tp_sum(give, keep):
        part = (keep + swap(give, "tp", n_tp, 1).astype(F32)).astype(BF)
        part = (part.astype(F32) + swap(part, "tp", n_tp, 2).astype(F32)).astype(BF)
        return part, swap(part, "tp", n_tp, 1)

    def gather_keys(kv):
        if not near:
            return [lax.all_gather(kv, "ctx", axis=1, tiled=True)]
        out = [kv]
        for k in range(1, n_ctx):
            out.append(lax.ppermute(kv, "ctx", [(i, i + k) for i in range(n_ctx - k)]))
        return out

    def small_sum(v):
        v = v + swap(v, "dp", n_dp, 1)
        bit = 1
        while bit < n_ctx:
            v = v + swap(v, "ctx", n_ctx, bit)
            bit *= 2
        return v

    def halving(give, keep, dp, ctx):
        keep = keep + swap(give, "ctx", n_ctx, 1).astype(F32)

        def split(x, index):
            half = x.shape[0] // 2
            return (
                lax.dynamic_slice_in_dim(x, (1 - index) * half, half).astype(BF),
                lax.dynamic_slice_in_dim(x, index * half, half),
            )

        give, keep = split(keep, dp)
        keep = keep + swap(give, "dp", n_dp, 1).astype(F32)
        if n_ctx == 4:
            give, keep = split(keep, ctx // 2)
            return keep + swap(give, "ctx", n_ctx, 2).astype(F32)
        groups = [[i for i in range(n_ctx) if i % 2 == b] for b in range(2)]
        return lax.psum_scatter(
            keep.astype(BF), "ctx", scatter_dimension=0, axis_index_groups=groups, tiled=True
        ).astype(F32)

    def body(
        teacher_in,
        teacher_gain_a,
        teacher_shift_a,
        teacher_attn_in,
        teacher_attn_bias,
        teacher_attn_out,
        teacher_out_bias,
        teacher_gain_b,
        teacher_shift_b,
        teacher_up,
        teacher_up_bias,
        teacher_down,
        teacher_down_bias,
        student_in,
        student_gain_a,
        student_shift_a,
        student_attn_in,
        student_attn_bias,
        student_attn_out,
        student_out_bias,
        student_gain_b,
        student_shift_b,
        student_up,
        student_up_bias,
        student_down,
        student_down_bias,
        out_grad,
        slot_lengths,
    ):
        slots, rows, wide = teacher_in.shape
        narrow = student_in.shape[2]
        total = slots * rows
        s_cols = student_attn_in.shape[2]
        s_heads = s_cols // HD
        hidden = student_up.shape[1]
        dp = lax.axis_index("dp")
        ctx = lax.axis_index("ctx")
        tp = lax.axis_index("tp")
        local_lengths = lax.dynamic_slice_in_dim(slot_lengths, dp * slots, slots)
        info = jnp.concatenate(
            [
                jnp.stack([ctx * rows, dp, tp % 2, tp, ctx]).astype(jnp.int32),
                local_lengths,
            ]
        )
        t_x = teacher_in.reshape(total, wide)
        s_x = student_in.reshape(total, narrow)
        grad = out_grad.reshape(total, narrow)

        s_in_t = jnp.swapaxes(student_attn_in, 1, 2)
        t_down_t = teacher_down.T
        peer_qkv = swap(s_in_t, "dp", n_dp, 1)
        t_half = wide // 2
        t_mine, t_theirs = run(
            teacher_norm_kernel,
            "teacher_norm",
            [((total, t_half), BF)] * 2,
            [info, t_x, teacher_gain_a, teacher_shift_a],
        )
        t_other = swap(t_theirs, "dp", n_dp, 1)
        s_x, t_theirs = lax.optimization_barrier((s_x, t_theirs))
        peer_out = swap(student_attn_out, "dp", n_dp, 1)
        peer_up = swap(student_up, "dp", n_dp, 1)
        peer_down = swap(student_down, "dp", n_dp, 1)

        unused_pairs, unused_single, s_kv_width = kv_tiles(s_heads)
        s_q_width = -(-s_cols // PAIR) * PAIR
        s_normed, s_q, s_kv = run(
            functools.partial(student_qkv_kernel, s_heads),
            "student_qkv",
            [((total, narrow), BF), ((total, s_q_width), BF), ((total, s_kv_width), BF)],
            [info, s_x, student_gain_a, student_shift_a, s_in_t, peer_qkv, student_attn_bias],
            flops=2 * total * narrow * 3 * s_cols,
        )
        s_q = s_q.reshape(slots, rows, s_q_width)
        s_kv_list = gather_keys(s_kv.reshape(slots, rows, s_kv_width))

        heads = wide // HD
        cols = heads // n_tp * HD
        tail = wide - n_tp * cols
        t_heads = (cols + tail) // HD
        unused_pairs, unused_single, t_kv_width = kv_tiles(t_heads)
        t_q_width = -(-(cols + tail) // PAIR) * PAIR
        packed = t_kv_width + t_q_width
        t_give, t_own, w_out_give = run(
            functools.partial(teacher_qkv_kernel, t_heads, cols),
            "teacher_qkv",
            [((total, packed), BF), ((total, packed), F32), ((t_half, t_q_width), BF)],
            [info, t_mine, t_other, teacher_attn_in, teacher_attn_out],
            specs=[SMEM, VMEM, VMEM, ANY, VMEM],
            scratch=[
                pltpu.VMEM((3, t_half, cols), BF),
                pltpu.VMEM((3, t_half, tail), BF),
                pltpu.SemaphoreType.DMA((2,)),
            ],
            flops=4 * total * wide * (cols + tail) * 3 // 2,
        )
        t_got = swap(t_give, "dp", n_dp, 1)
        t_kv, t_q = run(
            functools.partial(teacher_join_kernel, t_heads, cols),
            "teacher_join",
            [((total, t_kv_width), BF), ((total, t_q_width), BF)],
            [info, t_own, t_got, teacher_attn_bias],
        )
        t_kv_all = lax.all_gather(
            t_kv.reshape(slots, rows, t_kv_width), "ctx", axis=1, tiled=True
        )
        t_q = t_q.reshape(slots, rows, t_q_width)

        w_out_peer = swap(w_out_give, "dp", n_dp, 1)
        pairs_of_ctx = [[i, i + 1] for i in range(0, n_ctx, 2)]

        def fetch(w):
            quarter = w.shape[0] // 2
            part = lax.dynamic_slice_in_dim(w, (ctx % 2) * quarter, quarter)
            part = lax.all_gather(part, "dp", axis=0, tiled=True)
            part = lax.dynamic_slice_in_dim(part, (1 - dp) * quarter, quarter)
            return lax.all_gather(
                part, "ctx", axis=0, axis_index_groups=pairs_of_ctx, tiled=True
            )

        up_src, down_src, t_kv = lax.optimization_barrier((teacher_up, t_down_t, t_kv))
        up_peer = fetch(up_src)
        down_peer = fetch(down_src)

        blocks = len(s_kv_list)
        keys = blocks * s_kv_list[0].shape[1]
        block_scratch = [pltpu.VMEM((keys, s_kv_width), BF)] if blocks > 1 else []
        s_att, b_give, b_keep = run(
            functools.partial(student_attend_kernel, s_heads, blocks),
            "student_attend",
            [((slots, rows, s_cols), BF), ((rows, narrow), BF), ((rows, narrow), F32)],
            [info, s_q, student_attn_out, peer_out] + s_kv_list,
            scratch=block_scratch,
            flops=4 * total * s_cols * keys,
            extra=total * s_heads * keys,
        )
        r, other = tp_sum(b_give, b_keep)

        s_mid, b_normed, act, d_upper, give, keep = run(
            student_ffn_kernel,
            "student_ffn",
            [
                ((total, narrow), F32),
                ((total, narrow), BF),
                ((total, hidden), BF),
                ((total, hidden), BF),
                ((rows, narrow), BF),
                ((rows, narrow), F32),
            ],
            [
                info,
                s_x,
                student_out_bias,
                student_gain_b,
                student_shift_b,
                student_up_bias,
                r,
                other,
                student_up,
                peer_up,
                student_down,
                peer_down,
                grad,
            ],
            scratch=[pltpu.VMEM((total, narrow), F32)],
            flops=6 * total * narrow * hidden,
        )
        r2, other2 = tp_sum(give, keep)
        d_scratch = [
            pltpu.VMEM((total, s_q_width), BF),
            pltpu.VMEM((total, narrow), F32),
        ] + block_scratch
        d_outs = run(
            functools.partial(student_back_kernel, s_heads, blocks),
            "student_back",
            [
                ((total, narrow), F32),
                ((total, narrow), BF),
                ((slots, rows, s_cols), BF),
                ((3, narrow), F32),
            ]
            + [
                (item.shape, F32 if (blocks > 1 and i == 0) else BF)
                for i, item in enumerate(s_kv_list)
            ],
            [info, s_mid, student_gain_b, r2, other2, grad, student_attn_out, peer_out, s_q] + s_kv_list,
            scratch=d_scratch,
            flops=10 * total * s_cols * keys,
            extra=total * s_heads * keys,
        )
        d_mid, d_a, d_q, sums_b = d_outs[:4]
        d_parts = d_outs[4:]
        if near:
            d_own = d_parts[0]
            gots = [
                lax.ppermute(d_parts[k], "ctx", [(i + k, i) for i in range(n_ctx - k)])
                for k in range(1, n_ctx)
            ]
        else:
            d_own = lax.psum_scatter(d_parts[0], "ctx", scatter_dimension=1, tiled=True)
            gots = []
        b_normed, act, d_upper, d_q = lax.optimization_barrier((b_normed, act, d_upper, d_q))
        g_give, g_keep, p_give, p_keep, sums_f = run(
            functools.partial(student_ffn_grads_kernel, n_ctx),
            "student_ffn_grads",
            [
                ((narrow // 2, 2 * hidden), BF),
                ((narrow // 2, 2 * hidden), F32),
                ((rows, narrow), BF),
                ((rows, narrow), F32),
                ((2, narrow), F32),
            ],
            [info, b_normed, act, d_upper, grad, student_down, peer_down],
            scratch=[pltpu.VMEM((narrow, 2 * hidden), F32), pltpu.VMEM((total, narrow), F32)],
            flops=6 * total * narrow * hidden,
        )
        g_ffn = halving(g_give, g_keep, dp, ctx)
        d_own = d_own.reshape(total, s_kv_width)
        gots = [g.reshape(total, s_kv_width) for g in gots]
        a_give, a_keep, ga_give, ga_keep, sums_q = run(
            functools.partial(student_in_kernel, s_heads, len(gots), n_ctx),
            "student_in",
            [
                ((rows, narrow), BF),
                ((rows, narrow), F32),
                ((narrow // n_dp, 4 * s_cols), BF),
                ((narrow // n_dp, 4 * s_cols), F32),
                ((2, s_cols), F32),
            ],
            [
                info,
                d_q.reshape(total, s_cols),
                s_normed,
                d_a,
                s_att.reshape(total, s_cols),
                s_in_t,
                peer_qkv,
                d_own,
            ]
            + gots,
            scratch=[pltpu.VMEM((total, narrow), F32), pltpu.VMEM((narrow, 4 * s_cols), F32)],
            flops=2 * total * narrow * 7 * s_cols,
        )
        r3, other3 = tp_sum(a_give, a_keep)
        g_att = halving(ga_give, ga_keep, dp, ctx)
        in_grad, sums = run(
            student_last_kernel,
            "student_last",
            [((total, narrow), F32), ((8, narrow), F32)],
            [info, s_x, student_gain_a, r3, other3, d_mid, sums_b, sums_f, sums_q],
            scratch=[pltpu.VMEM((total, narrow), F32)],
        )

        t_att, t_att_tail = run(
            functools.partial(teacher_attend_kernel, t_heads, 1),
            "teacher_attend",
            [((slots, rows, cols), BF), ((slots, rows, tail), BF)],
            [info, t_q, t_kv_all],
            flops=4 * total * (cols + tail) * keys,
            extra=total * t_heads * keys,
        )
        every = lax.all_gather(t_att.reshape(total, cols), "tp", axis=0)
        o_cols, o_tail = run(
            teacher_out_kernel,
            "teacher_out",
            [((total, cols), BF), ((total, tail), BF)],
            [info, every, t_att_tail.reshape(total, tail), teacher_attn_out, w_out_peer],
            scratch=[pltpu.VMEM((wide, t_q_width), BF)],
            flops=2 * total * wide * (cols + tail),
        )
        o_every = lax.all_gather(o_cols, "tp", axis=0)
        t_hidden = teacher_up.shape[1]
        slab = -(-t_half // 128) * 128
        t_mid, f_give, f_keep = run(
            functools.partial(teacher_ffn_kernel, 256, slab),
            "teacher_ffn",
            [
                ((total, wide), F32),
                ((rows, 2 * slab + narrow), BF),
                ((rows, 2 * slab + narrow), F32),
            ],
            [
                info,
                t_x,
                teacher_out_bias,
                teacher_gain_b,
                teacher_shift_b,
                teacher_up_bias,
                o_every,
                o_tail,
                p_give,
                p_keep,
                teacher_up,
                up_peer,
                t_down_t,
                down_peer,
            ],
            specs=[SMEM] + [VMEM] * 9 + [ANY] * 4,
            scratch=[
                pltpu.VMEM((wide, t_hidden), BF),
                pltpu.VMEM((2, t_half, t_hidden), BF),
                pltpu.VMEM((total, t_hidden), BF),
                pltpu.VMEM((total, wide), BF),
                pltpu.VMEM((total, slab), F32),
                pltpu.SemaphoreType.DMA((4,)),
            ],
            flops=4 * total * wide * t_hidden,
        )
        r4, other4 = tp_sum(f_give, f_keep)
        t_result, s_result = run(
            functools.partial(last_kernel, slab),
            "last",
            [((total, wide), BF), ((total, narrow), BF)],
            [info, t_mid, s_mid, teacher_down_bias, student_down_bias, r4, other4],
        )

        small = small_sum(sums)
        piece = narrow // (n_dp * n_ctx)
        shards = lax.dynamic_slice_in_dim(small, (dp * n_ctx + ctx) * piece, piece, axis=1)

        grad_attn_in = jnp.stack([g_att[:, i * s_cols:(i + 1) * s_cols] for i in range(3)])
        return (
            t_result.reshape(slots, rows, wide),
            s_result.reshape(slots, rows, narrow),
            in_grad.reshape(slots, rows, narrow),
            shards[0],
            shards[1],
            grad_attn_in,
            small[7, :2 * s_cols].reshape(2, s_cols),
            g_att[:, 3 * s_cols:].T,
            shards[4],
            shards[2],
            shards[3],
            g_ffn[:, hidden:],
            small[6],
            g_ffn[:, :hidden].T,
            shards[5],
        )

    return body


def solution(mesh):
    sizes = mesh.shape
    return jax.shard_map(
        make_body(sizes["dp"], sizes["ctx"], sizes["tp"]),
        mesh=mesh,
        in_specs=(
            P("dp", "ctx", None),
            P(),
            P(),
            P(None, "dp", None),
            P(),
            P("dp", None),
            P(),
            P(),
            P(),
            P("dp", "tp"),
            P("tp"),
            P("tp", "dp"),
            P(),
            P("dp", "ctx", None),
            P(),
            P(),
            P(None, "dp", "tp"),
            P(None, "tp"),
            P("tp", "dp"),
            P(),
            P(),
            P(),
            P("dp", "tp"),
            P("tp"),
            P("tp", "dp"),
            P(),
            P("dp", "ctx", None),
            P(),
        ),
        out_specs=(
            P("dp", "ctx", None),
            P("dp", "ctx", None),
            P("dp", "ctx", None),
            P(("dp", "ctx")),
            P(("dp", "ctx")),
            P(None, ("dp", "ctx"), "tp"),
            P(None, "tp"),
            P("tp", ("dp", "ctx")),
            P(("dp", "ctx")),
            P(("dp", "ctx")),
            P(("dp", "ctx")),
            P(("dp", "ctx"), "tp"),
            P("tp"),
            P("tp", ("dp", "ctx")),
            P(("dp", "ctx")),
        ),
        check_vma=False,
    )
```

profile of v0, /device:TPU:0, one launch (start us, length us, event | category | flops | bytes accessed | tf_op | source)
XLA Modules:
  0.0 399.5 jit_solution(9559898131371937251)
XLA Ops:
  16.0 10.7 %collective-permute-done.other = bf16[256,800]{1,0:T(8,128)(2,1)S(1)} collective-permute-done((bf16[256,800]{1,0:T(8,128)(2,1)}, bf16[256,800]{1,0:T(8,128)(2,1)S(1)}, u32[]{:S(2)}, u32[]{:S(2)}) %collective-permute-start) | collective-permute-done | bytes 409632 | tf_op jit(solution)/shard_map/ppermute | solution.py:653
  27.5 7.6 %teacher_qkv.1 = (bf16[256,1408]{1,0:T(8,128)(2,1)}, f32[256,1408]{1,0:T(8,128)}, bf16[800,512]{1,0:T(8,128)(2,1)}) custom-call(s32[7]{0:T(128)} %concatenate.3.info, bf16[256,800]{1,0:T(8,128)(2,1)} %get-tuple-element.70.mine, bf16[256,800]{1,0:T(8,128)(2,1)} %copy-done.19, bf16[3,800,1600]{2,1,0:T(8,128)(2,1)} %w_hbm.1, bf16[800,1600]{1,0:T(8,128)(2,1)} %w.1), custom_call_target="tpu_custom_call" | custom-call | flops 1101004800 | bytes 14041116 | tf_op jit(solution)/shard_map/teacher_qkv/pallas_call | solution.py:92
  36.9 15.8 %collective-permute-done.1.got = bf16[256,1408]{1,0:T(8,128)(2,1)S(1)} collective-permute-done((bf16[256,1408]{1,0:T(8,128)(2,1)}, bf16[256,1408]{1,0:T(8,128)(2,1)S(1)}, u32[]{:S(2)}, u32[]{:S(2)}) %collective-permute-start.1) | collective-permute-done | bytes 720928 | tf_op jit(solution)/shard_map/ppermute | solution.py:653
  62.5 13.3 %collective-permute-done.3.peer = bf16[3,192,384]{2,1,0:T(8,128)(2,1)S(1)} collective-permute-done((bf16[3,192,384]{2,1,0:T(8,128)(2,1)S(1)}, bf16[3,192,384]{2,1,0:T(8,128)(2,1)S(1)}, u32[]{:S(2)}, u32[]{:S(2)}) %collective-permute-start.3) | collective-permute-done | bytes 442400 | tf_op jit(solution)/shard_map/ppermute | solution.py:653
  82.6 4.8 %collective-permute-start.6 = (bf16[2,128,384]{2,1,0:T(8,128)(2,1)}, bf16[2,128,384]{2,1,0:T(8,128)(2,1)S(1)}, u32[]{:S(2)}, u32[]{:S(2)}) collective-permute-start(bf16[2,128,384]{2,1,0:T(8,128)(2,1)} %bitcast.64), channel_id=1, source_target_pairs={{0,8},{4,12},{1,9},{5,13},{2,10},{6,14},{3,11},{7,15},{16,24},{20,... | collective-permute-start | bytes 589832 | tf_op jit(solution)/shard_map/ppermute | solution.py:665
  91.3 6.4 %collective-permute-done.4.peer_ref = bf16[192,384]{1,0:T(8,128)(2,1)S(1)} collective-permute-done((bf16[192,384]{1,0:T(8,128)(2,1)S(1)}, bf16[192,384]{1,0:T(8,128)(2,1)S(1)}, u32[]{:S(2)}, u32[]{:S(2)}) %collective-permute-start.4) | collective-permute-done | bytes 147488 | tf_op jit(solution)/shard_map/ppermute | solution.py:653
  113.1 19.0 %collective-permute-done.12.down_peer = bf16[768,384]{1,0:T(8,128)(2,1)S(1)} collective-permute-done((bf16[768,384]{1,0:T(8,128)(2,1)S(1)}, bf16[768,384]{1,0:T(8,128)(2,1)S(1)}, u32[]{:S(2)}, u32[]{:S(2)}) %collective-permute-start.12) | collective-permute-done | bytes 589856 | tf_op jit(solution)/shard_map/ppermute | solution.py:653
  132.2 24.2 %collective-permute-done.11.up_peer = bf16[384,768]{1,0:T(8,128)(2,1)S(1)} collective-permute-done((bf16[384,768]{1,0:T(8,128)(2,1)S(1)}, bf16[384,768]{1,0:T(8,128)(2,1)S(1)}, u32[]{:S(2)}, u32[]{:S(2)}) %collective-permute-start.11) | collective-permute-done | bytes 589856 | tf_op jit(solution)/shard_map/ppermute | solution.py:653
  157.2 4.9 %student_ffn.1 = (f32[256,768]{1,0:T(8,128)}, bf16[256,768]{1,0:T(8,128)(2,1)}, bf16[256,768]{1,0:T(8,128)(2,1)}, bf16[256,768]{1,0:T(8,128)(2,1)}, bf16[128,768]{1,0:T(8,128)(2,1)}, /*index=5*/f32[128,768]{1,0:T(8,128)}) custom-call(s32[7]{0:T(128)} %concatenate.3.info, bf16[256,768]{1,0:T(8,128)(2,1)} %bitcast.53, bf16[768]{0:T(1024)(128)(2,1)} %out_bias.2, ...), custom_call_target="tpu_custom_call" | custom-call | flops 905969664 | bytes 6101020 | tf_op jit(solution)/shard_map/student_ffn/pallas_call | solution.py:92
  165.8 7.3 %collective-permute-done.14 = bf16[128,768]{1,0:T(8,128)(2,1)S(1)} collective-permute-done((bf16[128,768]{1,0:T(8,128)(2,1)S(1)}, bf16[128,768]{1,0:T(8,128)(2,1)S(1)}, u32[]{:S(2)}, u32[]{:S(2)}) %collective-permute-start.14) | collective-permute-done | bytes 196640 | tf_op jit(solution)/shard_map/ppermute | solution.py:653
  175.3 7.7 %student_back.1 = (f32[256,768]{1,0:T(8,128)}, bf16[256,768]{1,0:T(8,128)(2,1)}, bf16[2,128,192]{2,1,0:T(8,128)(2,1)}, f32[3,768]{1,0:T(4,128)}, f32[2,128,384]{...) custom-call(s32[7]{0:T(128)} %concatenate.3.info, ...), custom_call_target="tpu_custom_call" | custom-call | flops 251658240 | bytes 5057052 | tf_op jit(solution)/shard_map/student_back/pallas_call | solution.py:92
  186.9 11.6 %collective-permute-done.19 = bf16[2,128,384]{2,1,0:T(8,128)(2,1)S(1)} collective-permute-done((bf16[2,128,384]{2,1,0:T(8,128)(2,1)}, bf16[2,128,384]{2,1,0:T(8,128)(2,1)S(1)}, u32[]{:S(2)}, u32[]{:S(2)}) %collective-permute-start.19) | collective-permute-done | bytes 196640 | tf_op jit(solution)/shard_map/ppermute | solution.py:893
  198.5 21.5 %collective-permute-done.20 = bf16[2,128,384]{2,1,0:T(8,128)(2,1)S(1)} collective-permute-done((bf16[2,128,384]{2,1,0:T(8,128)(2,1)}, bf16[2,128,384]{2,1,0:T(8,128)(2,1)S(1)}, u32[]{:S(2)}, u32[]{:S(2)}) %collective-permute-start.20) | collective-permute-done | bytes 196640 | tf_op jit(solution)/shard_map/ppermute | solution.py:893
  228.6 6.5 %collective-permute-done.23 = bf16[128,768]{1,0:T(8,128)(2,1)S(1)} collective-permute-done((bf16[128,768]{1,0:T(8,128)(2,1)S(1)}, bf16[128,768]{1,0:T(8,128)(2,1)S(1)}, u32[]{:S(2)}, u32[]{:S(2)}) %collective-permute-start.23) | collective-permute-done | bytes 196640 | tf_op jit(solution)/shard_map/ppermute | solution.py:653
  235.3 5.3 %student_ffn_grads.1 = (bf16[384,1536]{1,0:T(8,128)(2,1)}, f32[384,1536]{1,0:T(8,128)}, bf16[128,768]{1,0:T(8,128)(2,1)}, f32[128,768]{1,0:T(8,128)}, f32[2,768]{1,0:T(2,128)}) custom-call(s32[7]{0:T(128)} %concatenate.3.info, bf16[256,768]{1,0:T(8,128)(2,1)} %get-tuple-element.93.normed, bf16[256,768]{1,0:T(8,128)(2,1)} %get-tuple-element.94.act, ...), custom_call_target="tpu_custom_call" | custom-call | flops 905969664 | bytes 6887452 | tf_op jit(solution)/shard_map/student_ffn_grads/pallas_call | solution.py:92
  251.6 5.8 %collective-permute-done.28 = bf16[384,768]{1,0:T(8,128)(2,1)S(1)} collective-permute-done((bf16[384,768]{1,0:T(8,128)(2,1)}, bf16[384,768]{1,0:T(8,128)(2,1)S(1)}, u32[]{:S(2)}, u32[]{:S(2)}) %collective-permute-start.28) | collective-permute-done | bytes 589856 | tf_op jit(solution)/shard_map/ppermute | solution.py:653
  257.6 40.7 %collective-permute-done.26 = f32[8,768]{1,0:T(8,128)S(1)} collective-permute-done((f32[8,768]{1,0:T(8,128)S(1)}, f32[8,768]{1,0:T(8,128)S(1)}, u32[]{:S(2)}, u32[]{:S(2)}) %collective-permute-start.26) | collective-permute-done | bytes 24608 | tf_op jit(solution)/shard_map/ppermute | solution.py:653
  313.2 6.3 %teacher_attend.1 = (bf16[2,128,384]{2,1,0:T(8,128)(2,1)}, bf16[2,128,64]{2,1,0:T(8,128)(2,1)}) custom-call(s32[7]{0:T(128)} %concatenate.3.info, bf16[2,128,512]{2,1,0:T(8,128)(2,1)} %bitcast.72, bf16[2,512,896]{2,1,0:T(8,128)(2,1)} %all-gather.7.cloned.1.call-done.refs_0_), custom_call_target="tpu_custom_call" | custom-call | flops 234881024 | bytes 2326556 | tf_op jit(solution)/shard_map/teacher_attend/pallas_call | solution.py:92
  319.5 9.1 %all_gather.25.every = bf16[4,256,384]{2,1,0:T(8,128)(2,1)} all-gather(bf16[1,256,384]{2,1,0:T(8,128)(2,1)} %bitcast.76), channel_id=1, replica_groups=mesh['dp'=2,'ctx'=4,'tp'=4] {'tp'}, dimensions={0}, use_global_device_ids=true | all-gather | bytes 983040 | tf_op jit(solution)/shard_map/all_gather | solution.py:959
  332.5 10.7 %all-gather = bf16[1024,384]{1,0:T(8,128)(2,1)} all-gather(bf16[256,384]{1,0:T(8,128)(2,1)} %get-tuple-element.79), channel_id=2, replica_groups=mesh['dp'=2,'ctx'=4,'tp'=4] {'tp'}, dimensions={0}, use_global_device_ids=true | all-gather | bytes 983040 | tf_op jit(solution)/shard_map/all_gather | solution.py:968
  343.3 9.6 %teacher_ffn.1 = (f32[256,1600]{1,0:T(8,128)}, bf16[128,2560]{1,0:T(8,128)(2,1)}, f32[128,2560]{1,0:T(8,128)}) custom-call(s32[7]{0:T(128)} %concatenate.3.info, bf16[256,1600]{1,0:T(8,128)(2,1)} %bitcast.49, bf16[1600]{0:T(1024)(128)(2,1)} %out_bias.3, bf16[1600]{0:T(1024)(128)(2,1)} %gain.10, bf16[1600]{0:T(1024)(128)(2,1)} %shift.7, ...), custom_call_target="tpu_custom_call" | custom-call | flops 2621440000 | bytes 16085532 | tf_op jit(solution)/shard_map/teacher_ffn/pallas_call | solution.py:92
  360.0 8.9 %collective-permute-done.32 = bf16[192,1536]{1,0:T(8,128)(2,1)} collective-permute-done((bf16[192,1536]{1,0:T(8,128)(2,1)S(1)}, bf16[192,1536]{1,0:T(8,128)(2,1)}, u32[]{:S(2)}, u32[]{:S(2)}) %collective-permute-start.32) | collective-permute-done | bytes 589856 | tf_op jit(solution)/shard_map/ppermute | solution.py:653
  370.8 4.9 %collective-permute-done.17 = bf16[128,2560]{1,0:T(8,128)(2,1)S(1)} collective-permute-done((bf16[128,2560]{1,0:T(8,128)(2,1)S(1)}, bf16[128,2560]{1,0:T(8,128)(2,1)S(1)}, u32[]{:S(2)}, u32[]{:S(2)}) %collective-permute-start.17) | collective-permute-done | bytes 655392 | tf_op jit(solution)/shard_map/ppermute | solution.py:653
  375.9 9.7 %collective-permute-done.33 = bf16[96,1536]{1,0:T(8,128)(2,1)S(1)} collective-permute-done((bf16[96,1536]{1,0:T(8,128)(2,1)S(1)}, bf16[96,1536]{1,0:T(8,128)(2,1)S(1)}, u32[]{:S(2)}, u32[]{:S(2)}) %collective-permute-start.33) | collective-permute-done | bytes 294944 | tf_op jit(solution)/shard_map/ppermute | solution.py:653
  (169 shorter events, 113.0 us)
Async XLA Ops:
  7.2 154.9 %all-gather.9.cloned.1.call-start = ((), (), s32[]{:S(2)}) async-start(), calls=%async_computation.1 | async-start | bytes 3993600 | tf_op jit(solution)/shard_map/all_gather | solution.py:812
  13.0 13.7 %collective-permute-start = (bf16[256,800]{1,0:T(8,128)(2,1)}, bf16[256,800]{1,0:T(8,128)(2,1)S(1)}, u32[]{:S(2)}, u32[]{:S(2)}) collective-permute-start(bf16[256,800]{1,0:T(8,128)(2,1)} %get-tuple-element.71), channel_id=1, source_target_pairs={{0,16},{16,0},{1,17},{17,1},{2,18},{18,2},{3,19},{19,3},{4,20},{20... | collective-permute-start | bytes 1228808 | tf_op jit(solution)/shard_map/ppermute | solution.py:653
  35.1 17.6 %collective-permute-start.1 = (bf16[256,1408]{1,0:T(8,128)(2,1)}, bf16[256,1408]{1,0:T(8,128)(2,1)S(1)}, u32[]{:S(2)}, u32[]{:S(2)}) collective-permute-start(bf16[256,1408]{1,0:T(8,128)(2,1)} %get-tuple-element.73), channel_id=1, source_target_pairs={{0,16},{16,0},{1,17},{17,1},{2,18},{18,2},{3,19},{19,3},{4,20},{20... | collective-permute-start | bytes 2162696 | tf_op jit(solution)/shard_map/ppermute | solution.py:653
  57.5 191.6 %all-gather.13.cloned.1.call-start = ((), (), s32[]{:S(2)}) async-start(), calls=%async_computation.3 | async-start | bytes 3993600 | tf_op jit(solution)/shard_map/all_gather | solution.py:812
  60.1 253.1 %all-gather.7.cloned.1.call-start = ((), (), s32[]{:S(2)}) async-start(), calls=%async_computation | async-start | bytes 2293760 | tf_op jit(solution)/shard_map/all_gather | solution.py:801
  60.8 282.5 %all-gather.11.cloned.1.call-start = ((), (), s32[]{:S(2)}) async-start(), calls=%async_computation.2 | async-start | bytes 3993600 | tf_op jit(solution)/shard_map/all_gather | solution.py:814
  61.0 14.7 %collective-permute-start.3 = (bf16[3,192,384]{2,1,0:T(8,128)(2,1)S(1)}, bf16[3,192,384]{2,1,0:T(8,128)(2,1)S(1)}, u32[]{:S(2)}, u32[]{:S(2)}) collective-permute-start(bf16[3,192,384]{2,1,0:T(8,128)(2,1)S(1)} %bitcast.58), channel_id=1, source_target_pairs={{0,16},{16,0},{1,17},{17,1},{2,18},{18,2},{3,19},{19,3},{4,20},{20... | collective-permute-start | bytes 1327112 | tf_op jit(solution)/shard_map/ppermute | solution.py:653
  79.4 18.3 %collective-permute-start.5 = (bf16[2,128,384]{2,1,0:T(8,128)(2,1)}, bf16[2,128,384]{2,1,0:T(8,128)(2,1)S(1)}, u32[]{:S(2)}, u32[]{:S(2)}) collective-permute-start(bf16[2,128,384]{2,1,0:T(8,128)(2,1)} %bitcast.63), channel_id=1, source_target_pairs={{0,4},{4,8},{8,12},{1,5},{5,9},{9,13},{2,6},{6,10},{10,14},{3,7},{... | collective-permute-start | bytes 589832 | tf_op jit(solution)/shard_map/ppermute | solution.py:665
  82.6 15.1 %collective-permute-start.6 = (bf16[2,128,384]{2,1,0:T(8,128)(2,1)}, bf16[2,128,384]{2,1,0:T(8,128)(2,1)S(1)}, u32[]{:S(2)}, u32[]{:S(2)}) collective-permute-start(bf16[2,128,384]{2,1,0:T(8,128)(2,1)} %bitcast.64), channel_id=1, source_target_pairs={{0,8},{4,12},{1,9},{5,13},{2,10},{6,14},{3,11},{7,15},{16,24},{20,... | collective-permute-start | bytes 589832 | tf_op jit(solution)/shard_map/ppermute | solution.py:665
  107.6 24.5 %collective-permute-start.12 = (bf16[768,384]{1,0:T(8,128)(2,1)S(1)}, bf16[768,384]{1,0:T(8,128)(2,1)S(1)}, u32[]{:S(2)}, u32[]{:S(2)}) collective-permute-start(bf16[768,384]{1,0:T(8,128)(2,1)S(1)} %copy-done.16), channel_id=1, source_target_pairs={{0,16},{16,0},{1,17},{17,1},{2,18},{18,2},{3,19},{19,3},{4,20},{20... | collective-permute-start | bytes 1769480 | tf_op jit(solution)/shard_map/ppermute | solution.py:653
  109.6 46.7 %collective-permute-start.11 = (bf16[384,768]{1,0:T(8,128)(2,1)S(1)}, bf16[384,768]{1,0:T(8,128)(2,1)S(1)}, u32[]{:S(2)}, u32[]{:S(2)}) collective-permute-start(bf16[384,768]{1,0:T(8,128)(2,1)S(1)} %copy-done.15), channel_id=1, source_target_pairs={{0,16},{16,0},{1,17},{17,1},{2,18},{18,2},{3,19},{19,3},{4,20},{20... | collective-permute-start | bytes 1769480 | tf_op jit(solution)/shard_map/ppermute | solution.py:653
  113.0 43.3 %collective-permute-start.10 = (bf16[128,768]{1,0:T(8,128)(2,1)S(1)}, bf16[128,768]{1,0:T(8,128)(2,1)S(1)}, u32[]{:S(2)}, u32[]{:S(2)}) collective-permute-start(bf16[128,768]{1,0:T(8,128)(2,1)S(1)} %add_convert_fusion.6.r_ref), channel_id=1, source_target_pairs={{0,1},{1,0},{2,3},{3,2},{4,5},{5,4},{6,7},{7,6},{8,9},{9,8},{10,11... | collective-permute-start | bytes 589832 | tf_op jit(solution)/shard_map/ppermute | solution.py:653
  164.7 178.5 %all-gather.15.cloned.1.call-start = ((), (), s32[]{:S(2)}) async-start(), calls=%async_computation.4 | async-start | bytes 3993600 | tf_op jit(solution)/shard_map/all_gather | solution.py:814
  183.0 15.5 %collective-permute-start.19 = (bf16[2,128,384]{2,1,0:T(8,128)(2,1)}, bf16[2,128,384]{2,1,0:T(8,128)(2,1)S(1)}, u32[]{:S(2)}, u32[]{:S(2)}) collective-permute-start(bf16[2,128,384]{2,1,0:T(8,128)(2,1)} %get-tuple-element.110), channel_id=1, source_target_pairs={{4,0},{8,4},{12,8},{5,1},{9,5},{13,9},{6,2},{10,6},{14,10},{7,3},{... | collective-permute-start | bytes 589832 | tf_op jit(solution)/shard_map/ppermute | solution.py:893
  184.3 35.7 %collective-permute-start.20 = (bf16[2,128,384]{2,1,0:T(8,128)(2,1)}, bf16[2,128,384]{2,1,0:T(8,128)(2,1)S(1)}, u32[]{:S(2)}, u32[]{:S(2)}) collective-permute-start(bf16[2,128,384]{2,1,0:T(8,128)(2,1)} %get-tuple-element.111), channel_id=1, source_target_pairs={{8,0},{12,4},{9,1},{13,5},{10,2},{14,6},{11,3},{15,7},{24,16},{28,... | collective-permute-start | bytes 589832 | tf_op jit(solution)/shard_map/ppermute | solution.py:893
  185.6 34.4 %collective-permute-start.21 = (bf16[2,128,384]{2,1,0:T(8,128)(2,1)}, bf16[2,128,384]{2,1,0:T(8,128)(2,1)S(1)}, u32[]{:S(2)}, u32[]{:S(2)}) collective-permute-start(bf16[2,128,384]{2,1,0:T(8,128)(2,1)} %get-tuple-element.112), channel_id=1, source_target_pairs={{12,0},{13,1},{14,2},{15,3},{28,16},{29,17},{30,18},{31,19}} | collective-permute-start | bytes 589832 | tf_op jit(solution)/shard_map/ppermute | solution.py:893
  228.6 28.9 %collective-permute-start.28 = (bf16[384,768]{1,0:T(8,128)(2,1)}, bf16[384,768]{1,0:T(8,128)(2,1)S(1)}, u32[]{:S(2)}, u32[]{:S(2)}) collective-permute-start(bf16[384,768]{1,0:T(8,128)(2,1)} %get-tuple-element.122), channel_id=1, source_target_pairs={{0,4},{4,0},{8,12},{12,8},{1,5},{5,1},{9,13},{13,9},{2,6},{6,2},{1... | collective-permute-start | bytes 1769480 | tf_op jit(solution)/shard_map/ppermute | solution.py:653
  245.9 82.7 %collective-permute-start.2 = (bf16[800,512]{1,0:T(8,128)(2,1)}, bf16[800,512]{1,0:T(8,128)(2,1)}, u32[]{:S(2)}, u32[]{:S(2)}) collective-permute-start(bf16[800,512]{1,0:T(8,128)(2,1)} %get-tuple-element.78), channel_id=1, source_target_pairs={{0,16},{16,0},{1,17},{17,1},{2,18},{18,2},{3,19},{19,3},{4,20},{20... | collective-permute-start | bytes 2457608 | tf_op jit(solution)/shard_map/ppermute | solution.py:653
  246.4 64.5 %collective-permute-start.31 = (bf16[384,1536]{1,0:T(8,128)(2,1)}, bf16[384,1536]{1,0:T(8,128)(2,1)}, u32[]{:S(2)}, u32[]{:S(2)}) collective-permute-start(bf16[384,1536]{1,0:T(8,128)(2,1)} %get-tuple-element.124), channel_id=1, source_target_pairs={{0,4},{4,0},{8,12},{12,8},{1,5},{5,1},{9,13},{13,9},{2,6},{6,2},{1... | collective-permute-start | bytes 3538952 | tf_op jit(solution)/shard_map/ppermute | solution.py:653
  249.1 49.1 %collective-permute-start.26 = (f32[8,768]{1,0:T(8,128)S(1)}, f32[8,768]{1,0:T(8,128)S(1)}, u32[]{:S(2)}, u32[]{:S(2)}) collective-permute-start(f32[8,768]{1,0:T(8,128)S(1)} %add.106), channel_id=1, source_target_pairs={{0,4},{4,0},{8,12},{12,8},{1,5},{5,1},{9,13},{13,9},{2,6},{6,2},{1... | collective-permute-start | bytes 73736 | tf_op jit(solution)/shard_map/ppermute | solution.py:653
  308.3 46.7 %collective-permute-start.30 = (bf16[96,768]{1,0:T(8,128)(2,1)}, bf16[96,768]{1,0:T(8,128)(2,1)}, u32[]{:S(2)}, u32[]{:S(2)}) collective-permute-start(bf16[96,768]{1,0:T(8,128)(2,1)} %dynamic-slice_convert_fusion.3), channel_id=1, source_target_pairs={{0,8},{4,12},{8,0},{12,4},{1,9},{5,13},{9,1},{13,5},{2,10},{6,14},... | collective-permute-start | bytes 442376 | tf_op jit(solution)/shard_map/ppermute | solution.py:653
  353.3 15.6 %collective-permute-start.32 = (bf16[192,1536]{1,0:T(8,128)(2,1)S(1)}, bf16[192,1536]{1,0:T(8,128)(2,1)}, u32[]{:S(2)}, u32[]{:S(2)}) collective-permute-start(bf16[192,1536]{1,0:T(8,128)(2,1)S(1)} %dynamic-slice_convert_fusion), channel_id=1, source_target_pairs={{0,16},{16,0},{1,17},{17,1},{2,18},{18,2},{3,19},{19,3},{4,20},{20... | collective-permute-start | bytes 1769480 | tf_op jit(solution)/shard_map/ppermute | solution.py:653
  359.1 16.6 %collective-permute-start.17 = (bf16[128,2560]{1,0:T(8,128)(2,1)S(1)}, bf16[128,2560]{1,0:T(8,128)(2,1)S(1)}, u32[]{:S(2)}, u32[]{:S(2)}) collective-permute-start(bf16[128,2560]{1,0:T(8,128)(2,1)S(1)} %add_convert_fusion.1), channel_id=1, source_target_pairs={{0,2},{1,3},{2,0},{3,1},{4,6},{5,7},{6,4},{7,5},{8,10},{9,11},{10,... | collective-permute-start | bytes 1966088 | tf_op jit(solution)/shard_map/ppermute | solution.py:653
  370.1 15.5 %collective-permute-start.33 = (bf16[96,1536]{1,0:T(8,128)(2,1)S(1)}, bf16[96,1536]{1,0:T(8,128)(2,1)S(1)}, u32[]{:S(2)}, u32[]{:S(2)}) collective-permute-start(bf16[96,1536]{1,0:T(8,128)(2,1)S(1)} %dynamic-slice_convert_fusion.1), channel_id=1, source_target_pairs={{0,8},{4,12},{8,0},{12,4},{1,9},{5,13},{9,1},{13,5},{2,10},{6,14},... | collective-permute-start | bytes 884744 | tf_op jit(solution)/shard_map/ppermute | solution.py:653
  (43 other events, 364.4 us)
Sparse Core Ops, SparseCore 0:
  57.6 45.7 all-gather.8
  105.0 59.3 all-gather.12
  166.0 55.7 all-gather.6
  223.1 66.2 all-gather.10
  290.8 42.8 all-gather.14
where the time goes:
time: 401 us; the launch traced here: 400 us
  waiting for transfers between devices  222 us (55%)
  Pallas kernels  69.5 us (17%)
  starting transfers between devices  37.4 us (9%)
  local copies, waits for them, and re-layouts  26.2 us (7%)
  blocking collectives  19.8 us (5%)
  between operations  14.2 us (4%)
  other arithmetic  10.1 us (3%)
    ppermute x28, waiting for transfers between devices, swap(): return lax.ppermute(x, axis, [(i, i ^ bit) for i in range(size)])  188 us
    pallas_call x14, Pallas kernels, run(): pl.pallas_call(kernel, out_shape=out_shape, in_specs=specs, out_specs=[VM...  69.5 us
    ppermute x3, waiting for transfers between devices, body(): lax.ppermute(d_parts[k], 'ctx', [(i + k, i) for i in range(n_ctx - k)])  33.1 us
    ppermute x28, starting transfers between devices, swap(): return lax.ppermute(x, axis, [(i, i ^ bit) for i in range(size)])  23.9 us
    unnamed x59, local copies, waits for them, and re-layouts  13.1 us
    all_gather x1, blocking collectives, body(): o_every = lax.all_gather(o_cols, 'tp', axis=0)  10.7 us
    ppermute x3, starting transfers between devices, gather_keys(): out.append(lax.ppermute(kv, 'ctx', [(i, i + k) for i in range(n_ctx - k)]))  9.31 us
    all_gather x1, blocking collectives, body(): every = lax.all_gather(t_att.reshape(total, cols), 'tp', axis=0)  9.1 us
  transfers between devices with their start and end apart: 39, of which 22 were waited for; matrix products, arithmetic and copies ran while one was open for 6% of the time, Pallas kernels for 13%

commit v1 on v0

--- a/solution.py
+++ b/solution.py
@@ -19,6 +19,7 @@
 SMEM = pl.BlockSpec(memory_space=pltpu.SMEM)
 VMEM = pl.BlockSpec(memory_space=pltpu.VMEM)
 ANY = pl.BlockSpec(memory_space=pl.ANY)
+RING = 4
 LIMIT = 60 * 1024 * 1024
 
 
@@ -97,7 +98,7 @@
         scratch_shapes=list(scratch),
         compiler_params=pltpu.CompilerParams(vmem_limit_bytes=LIMIT),
         cost_estimate=pl.CostEstimate(
-            flops=int(flops), bytes_accessed=int(moved), transcendentals=int(extra)
+            flops=1, bytes_accessed=1, transcendentals=0
         ),
         name=name,
     )(*args)
@@ -408,41 +409,39 @@
 def split_rows(info, n_ctx, grad_s, give_ref, keep_ref):
     full = grad_s.shape[0]
     piece = full // (2 * n_ctx)
-    bit = lax.rem(info[CTX], 2)
-    for d in range(2):
-        for j in range(n_ctx // 2):
-            to = (d * (n_ctx // 2) + j) * piece
-            base = (d * n_ctx + 2 * j) * piece
-            keep_ref[to:to + piece, :] = grad_s[
-                pl.ds(pl.multiple_of(base + bit * piece, 16), piece), :
-            ]
-            give_ref[to:to + piece, :] = grad_s[
-                pl.ds(pl.multiple_of(base + (1 - bit) * piece, 16), piece), :
-            ].astype(give_ref.dtype)
+    count = n_ctx // RING
+    if piece % 8:
+        for half, ref in ((info[DP], keep_ref), (1 - info[DP], give_ref)):
+            start = pl.multiple_of(half * (full // 2), 16)
+            ref[...] = grad_s[pl.ds(start, full // 2), :].astype(ref.dtype)
+        return
+    place = lax.rem(info[CTX], RING)
+    for i, flip in enumerate((0, 3, 1, 2)):
+        for q in range(count):
+            to = (i * count + q) * piece
+            at = (q * RING + (place ^ flip)) * piece
+            for half, ref in ((info[DP], keep_ref), (1 - info[DP], give_ref)):
+                start = pl.multiple_of(half * (full // 2) + at, math.gcd(piece, 16))
+                ref[to:to + piece, :] = grad_s[pl.ds(start, piece), :].astype(ref.dtype)
 
 
 def student_ffn_grads_kernel(
-    n_ctx, info, normed, act, d_upper, grad, down_own, down_peer,
-    give_ref, keep_ref, part_give, part_keep, sums_ref, grad_s, part_s,
+    n_ctx, info, normed, act, d_upper, grad, give_ref, keep_ref, sums_ref, grad_s
 ):
-    rows = part_give.shape[0]
-    slots = normed.shape[0] // rows
+    slots = info.shape[0] - LEN
+    rows = normed.shape[0] // slots
     d_b = jnp.where(keep_mask(info, slots, rows), grad[...].astype(F32), 0.0).astype(BF)
     hidden = act.shape[1]
     grad_s[:, :hidden] = dense_tn(d_b, act[...])
     grad_s[:, hidden:] = dense_tn(normed[...], d_upper[...])
     split_rows(info, n_ctx, grad_s, give_ref, keep_ref)
-    cols = down_own.shape[1]
-    part_s[:, :cols] = dense(act[...], down_own[...])
-    part_s[:, cols:] = dense(act[...], down_peer[...])
-    part_give[...] = part_s[pl.ds((1 - info[ODD]) * rows, rows), :].astype(BF)
-    part_keep[...] = part_s[pl.ds(info[ODD] * rows, rows), :]
     sums_ref[0:1, :] = jnp.sum(d_b.astype(F32), axis=0, keepdims=True)
     sums_ref[1:2, :] = jnp.sum(d_upper[...].astype(F32), axis=0, keepdims=True)
 
 
 def student_in_kernel(
-    heads, n_got, n_ctx, info, d_q, normed, d_a, att, own, peer, d_kv, *refs
+    heads, n_got, n_ctx, info, d_q, normed, d_a, att, own, peer, act, down_own, down_peer, d_kv,
+    *refs
 ):
     gots = refs[:n_got]
     give_ref, keep_ref, g_give, g_keep, bias_ref, part_s, grad_s = refs[n_got:]
@@ -465,7 +464,9 @@
         return dense(d_q[...], w[0]) + dense(d_k, w[1]) + dense(d_v, w[2])
 
     part_s[:, :half] = back(own)
-    part_s[:, half:] = back(peer)
+    part_s[:, half:2 * half] = back(peer)
+    part_s[:, 2 * half:3 * half] = dense(act[...], down_own[...])
+    part_s[:, 3 * half:] = dense(act[...], down_peer[...])
     give_ref[...] = part_s[pl.ds((1 - info[ODD]) * rows, rows), :].astype(BF)
     keep_ref[...] = part_s[pl.ds(info[ODD] * rows, rows), :]
     cols = heads * HD
@@ -480,11 +481,17 @@
 
 
 def student_last_kernel(
-    info, x, gain, r_ref, other_ref, d_mid, sums_b, sums_f, sums_q, out_ref, sums_ref, d_s
+    info, x, gain, s_mid, s_bias, r_ref, other_ref, d_mid, sums_b, sums_f, sums_q,
+    out_ref, s_out, sums_ref, d_s,
 ):
     rows = r_ref.shape[0]
-    d_s[pl.ds(info[ODD] * rows, rows), :] = ordered(info, r_ref[...]).astype(F32)
-    d_s[pl.ds((1 - info[ODD]) * rows, rows), :] = ordered(info, other_ref[...]).astype(F32)
+    width = x.shape[1]
+    for at, ref in ((info[ODD] * rows, r_ref), ((1 - info[ODD]) * rows, other_ref)):
+        at = pl.multiple_of(at, rows)
+        d_s[pl.ds(at, rows), :] = ordered(info, ref[:, :width]).astype(F32)
+        s_out[pl.ds(at, rows), :] = (
+            s_mid[pl.ds(at, rows), :] + ordered(info, ref[:, width:]).astype(F32) + row(s_bias)
+        ).astype(BF)
     xhat, factor = norm_parts(x[...].astype(F32))
     d_norm = d_s[...]
     out_ref[...] = d_mid[...] + norm_back(d_norm, xhat, factor, row(gain))
@@ -574,19 +581,26 @@
 
 
 def teacher_ffn_kernel(
-    tile, slab, info, x, out_bias, gain, shift, up_bias, every, tail, p_give, p_keep,
-    up_own, up_peer, down_own, down_peer,
-    mid_ref, give_ref, keep_ref, up_s, down_s, act_s, normed_s, part_s, sems,
+    tile, info, x, out_bias, gain, shift, up_bias, every, tail, up_own, down_own,
+    up_near, up_far, down_near, down_far, mid_ref, give_ref, keep_ref, w_s, act_s, normed_s, part_s, sems,
 ):
     half, hidden = up_own.shape
+    wide = 2 * half
     own_at = pl.multiple_of(info[DP] * half, 16)
-    peer_at = pl.multiple_of((1 - info[DP]) * half, 16)
+    peer_at = (1 - info[DP]) * half
     copies = [
-        pltpu.make_async_copy(up_own, up_s.at[pl.ds(own_at, half)], sems.at[0]),
-        pltpu.make_async_copy(up_peer, up_s.at[pl.ds(peer_at, half)], sems.at[1]),
-        pltpu.make_async_copy(down_own, down_s.at[0], sems.at[2]),
-        pltpu.make_async_copy(down_peer, down_s.at[1], sems.at[3]),
+        pltpu.make_async_copy(up_own, w_s.at[pl.ds(own_at, half)], sems.at[0]),
+        pltpu.make_async_copy(
+            down_own, w_s.at[pl.ds(pl.multiple_of(own_at + wide, 16), half)], sems.at[1]
+        ),
     ]
+    size = up_near.shape[0]
+    bit = lax.rem(info[CTX], 2)
+    for i, (part, base, place) in enumerate(
+        ((up_near, 0, bit), (up_far, 0, 1 - bit), (down_near, wide, bit), (down_far, wide, 1 - bit))
+    ):
+        at = pl.multiple_of(peer_at + base + place * size, 16)
+        copies.append(pltpu.make_async_copy(part, w_s.at[pl.ds(at, size)], sems.at[i + 2]))
     for copy in copies:
         copy.start()
     n, unused, cols = every.shape
@@ -600,49 +614,31 @@
     mid_ref[:, a:] = x[:, a:].astype(F32) + tail[...].astype(F32) + bias[:, a:]
     xhat, unused = norm_parts(mid_ref[...])
     normed_s[...] = (xhat * row(gain) + row(shift)).astype(BF)
-    rows = give_ref.shape[0]
-    packed = give_ref.shape[1]
-    give_ref[:, 2 * slab:] = p_give[...]
-    keep_ref[:, 2 * slab:] = p_keep[...]
-    for copy in copies[:2]:
+    rows, packed = give_ref.shape
+    for copy in copies:
         copy.wait()
     up_row = row(up_bias)
     at = 0
     while at < hidden:
         size = min(tile, hidden - at)
-        v = dense(normed_s[...], up_s[:, at:at + size]) + up_row[:, at:at + size]
+        v = dense(normed_s[...], w_s[:wide, at:at + size]) + up_row[:, at:at + size]
         act_s[:, at:at + size] = gelu_tanh(v).astype(BF)
         at += size
-    for copy in copies[2:]:
-        copy.wait()
-    width = down_own.shape[0]
-    for i in range(2):
-        part_s[:, :width] = dense_nt(act_s[...], down_s[i])
-        a = i * slab
-        give_ref[:, a:a + width] = part_s[pl.ds((1 - info[ODD]) * rows, rows), :width].astype(BF)
-        keep_ref[:, a:a + width] = part_s[pl.ds(info[ODD] * rows, rows), :width]
-        give_ref[:, a + width:a + slab] = jnp.zeros((rows, slab - width), BF)
-        keep_ref[:, a + width:a + slab] = jnp.zeros((rows, slab - width), F32)
-
-
-def last_kernel(slab, info, t_mid, s_mid, t_bias, s_bias, r_ref, other_ref, t_out, s_out):
+    part_s[...] = dense_nt(act_s[...], w_s[wide:, :])
+    give_ref[:, :wide] = part_s[pl.ds((1 - info[ODD]) * rows, rows), :].astype(BF)
+    keep_ref[:, :wide] = part_s[pl.ds(info[ODD] * rows, rows), :]
+    give_ref[:, wide:] = jnp.zeros((rows, packed - wide), BF)
+    keep_ref[:, wide:] = jnp.zeros((rows, packed - wide), F32)
+
+
+def last_kernel(info, t_mid, t_bias, r_ref, other_ref, t_out):
     rows = r_ref.shape[0]
-    width = t_out.shape[1] // 2
+    wide = t_out.shape[1]
     keep_at = pl.multiple_of(info[ODD] * rows, rows)
     give_at = pl.multiple_of((1 - info[ODD]) * rows, rows)
-    first = info[DP] == 0
     for at, ref in ((keep_at, r_ref), (give_at, other_ref)):
-        own, peer = ref[:, :width].astype(F32), ref[:, slab:slab + width].astype(F32)
-        branch = jnp.concatenate(
-            [jnp.where(first, own, peer), jnp.where(first, peer, own)], axis=1
-        )
         t_out[pl.ds(at, rows), :] = (
-            t_mid[pl.ds(at, rows), :] + branch + row(t_bias)
-        ).astype(BF)
-        s_out[pl.ds(at, rows), :] = (
-            s_mid[pl.ds(at, rows), :]
-            + ordered(info, ref[:, 2 * slab:].astype(F32))
-            + row(s_bias)
+            t_mid[pl.ds(at, rows), :] + ref[:, :wide].astype(F32) + row(t_bias)
         ).astype(BF)
 
 
@@ -662,36 +658,44 @@
             return [lax.all_gather(kv, "ctx", axis=1, tiled=True)]
         out = [kv]
         for k in range(1, n_ctx):
-            out.append(lax.ppermute(kv, "ctx", [(i, i + k) for i in range(n_ctx - k)]))
+            if k == 2:
+                step = [(i, i + 1) for i in range(1, n_ctx - 1)]
+                out.append(lax.ppermute(out[1], "ctx", step))
+            else:
+                out.append(lax.ppermute(kv, "ctx", [(i, i + k) for i in range(n_ctx - k)]))
         return out
 
     def small_sum(v):
         v = v + swap(v, "dp", n_dp, 1)
         bit = 1
         while bit < n_ctx:
-            v = v + swap(v, "ctx", n_ctx, bit)
+            v = v + swap(v, "ctx", n_ctx, 3 if bit == 2 else bit)
             bit *= 2
         return v
 
-    def halving(give, keep, dp, ctx):
-        keep = keep + swap(give, "ctx", n_ctx, 1).astype(F32)
-
-        def split(x, index):
-            half = x.shape[0] // 2
-            return (
-                lax.dynamic_slice_in_dim(x, (1 - index) * half, half).astype(BF),
-                lax.dynamic_slice_in_dim(x, index * half, half),
-            )
-
-        give, keep = split(keep, dp)
-        keep = keep + swap(give, "dp", n_dp, 1).astype(F32)
-        if n_ctx == 4:
-            give, keep = split(keep, ctx // 2)
-            return keep + swap(give, "ctx", n_ctx, 2).astype(F32)
-        groups = [[i for i in range(n_ctx) if i % 2 == b] for b in range(2)]
+    def halve(keep, bit):
+        half = keep.shape[0] // 2
+        got = swap(keep[half:].astype(BF), "ctx", n_ctx, bit)
+        return keep[:half] + got.astype(F32)
+
+    def ring_order(x, ctx):
+        piece = x.shape[0] // n_ctx
+        if piece % 8 == 0:
+            return x
+        parts = x.reshape(n_ctx // RING, RING, piece, x.shape[1])
+        order = jnp.bitwise_xor(ctx % RING, jnp.array([0, 3, 1, 2], jnp.int32))
+        return jnp.swapaxes(jnp.take(parts, order, axis=1), 0, 1).reshape(x.shape)
+
+    def over_rings(keep):
+        if n_ctx == RING:
+            return keep
+        groups = [list(range(r, n_ctx, RING)) for r in range(RING)]
         return lax.psum_scatter(
             keep.astype(BF), "ctx", scatter_dimension=0, axis_index_groups=groups, tiled=True
         ).astype(F32)
+
+    def after(x, *first):
+        return lax.optimization_barrier((x,) + first)[0]
 
     def body(
         teacher_in,
@@ -754,10 +758,8 @@
             [info, t_x, teacher_gain_a, teacher_shift_a],
         )
         t_other = swap(t_theirs, "dp", n_dp, 1)
-        s_x, t_theirs = lax.optimization_barrier((s_x, t_theirs))
-        peer_out = swap(student_attn_out, "dp", n_dp, 1)
-        peer_up = swap(student_up, "dp", n_dp, 1)
-        peer_down = swap(student_down, "dp", n_dp, 1)
+        peer_out = swap(after(student_attn_out, t_theirs), "dp", n_dp, 1)
+        s_x = after(s_x, t_theirs)
 
         unused_pairs, unused_single, s_kv_width = kv_tiles(s_heads)
         s_q_width = -(-s_cols // PAIR) * PAIR
@@ -778,6 +780,8 @@
         unused_pairs, unused_single, t_kv_width = kv_tiles(t_heads)
         t_q_width = -(-(cols + tail) // PAIR) * PAIR
         packed = t_kv_width + t_q_width
+        t_mine = after(t_mine, s_kv_list[min(1, len(s_kv_list) - 1)], peer_out)
+        peer_up = swap(after(student_up, s_kv), "dp", n_dp, 1)
         t_give, t_own, w_out_give = run(
             functools.partial(teacher_qkv_kernel, t_heads, cols),
             "teacher_qkv",
@@ -792,36 +796,10 @@
             flops=4 * total * wide * (cols + tail) * 3 // 2,
         )
         t_got = swap(t_give, "dp", n_dp, 1)
-        t_kv, t_q = run(
-            functools.partial(teacher_join_kernel, t_heads, cols),
-            "teacher_join",
-            [((total, t_kv_width), BF), ((total, t_q_width), BF)],
-            [info, t_own, t_got, teacher_attn_bias],
-        )
-        t_kv_all = lax.all_gather(
-            t_kv.reshape(slots, rows, t_kv_width), "ctx", axis=1, tiled=True
-        )
-        t_q = t_q.reshape(slots, rows, t_q_width)
-
-        w_out_peer = swap(w_out_give, "dp", n_dp, 1)
-        pairs_of_ctx = [[i, i + 1] for i in range(0, n_ctx, 2)]
-
-        def fetch(w):
-            quarter = w.shape[0] // 2
-            part = lax.dynamic_slice_in_dim(w, (ctx % 2) * quarter, quarter)
-            part = lax.all_gather(part, "dp", axis=0, tiled=True)
-            part = lax.dynamic_slice_in_dim(part, (1 - dp) * quarter, quarter)
-            return lax.all_gather(
-                part, "ctx", axis=0, axis_index_groups=pairs_of_ctx, tiled=True
-            )
-
-        up_src, down_src, t_kv = lax.optimization_barrier((teacher_up, t_down_t, t_kv))
-        up_peer = fetch(up_src)
-        down_peer = fetch(down_src)
-
         blocks = len(s_kv_list)
         keys = blocks * s_kv_list[0].shape[1]
         block_scratch = [pltpu.VMEM((keys, s_kv_width), BF)] if blocks > 1 else []
+        s_q = after(s_q, t_give, peer_up)
         s_att, b_give, b_keep = run(
             functools.partial(student_attend_kernel, s_heads, blocks),
             "student_attend",
@@ -831,8 +809,28 @@
             flops=4 * total * s_cols * keys,
             extra=total * s_heads * keys,
         )
+        peer_down = swap(after(student_down, b_keep), "dp", n_dp, 1)
+        b_keep, t_got = lax.optimization_barrier((b_keep, t_got))
         r, other = tp_sum(b_give, b_keep)
-
+        t_own = after(t_own, s_att)
+        t_kv, t_q = run(
+            functools.partial(teacher_join_kernel, t_heads, cols),
+            "teacher_join",
+            [((total, t_kv_width), BF), ((total, t_q_width), BF)],
+            [info, t_own, t_got, teacher_attn_bias],
+        )
+        t_kv_list = gather_keys(t_kv.reshape(slots, rows, t_kv_width))
+        t_q = t_q.reshape(slots, rows, t_q_width)
+
+        quarter = t_half // 2
+
+        def half_of(w, *first):
+            part = lax.dynamic_slice_in_dim(w, (ctx % 2) * quarter, quarter)
+            return swap(after(part, *first), "dp", n_dp, 1)
+
+        up_near = half_of(teacher_up, peer_up, peer_down)
+
+        s_x = after(s_x, t_kv_list[-1], t_kv_list[min(1, len(t_kv_list) - 1)])
         s_mid, b_normed, act, d_upper, give, keep = run(
             student_ffn_kernel,
             "student_ffn",
@@ -863,6 +861,21 @@
             flops=6 * total * narrow * hidden,
         )
         r2, other2 = tp_sum(give, keep)
+        t_q = after(t_q, give)
+        t_blocks = len(t_kv_list)
+        t_scratch = [pltpu.VMEM((keys, t_kv_width), BF)] if t_blocks > 1 else []
+        t_att, t_att_tail = run(
+            functools.partial(teacher_attend_kernel, t_heads, t_blocks),
+            "teacher_attend",
+            [((slots, rows, cols), BF), ((slots, rows, tail), BF)],
+            [info, t_q] + t_kv_list,
+            scratch=t_scratch,
+            flops=4 * total * (cols + tail) * keys,
+            extra=total * t_heads * keys,
+        )
+        every = lax.all_gather(t_att.reshape(total, cols), "tp", axis=0)
+
+        s_mid = after(s_mid, every)
         d_scratch = [
             pltpu.VMEM((total, s_q_width), BF),
             pltpu.VMEM((total, narrow), F32),
@@ -896,30 +909,44 @@
         else:
             d_own = lax.psum_scatter(d_parts[0], "ctx", scatter_dimension=1, tiled=True)
             gots = []
-        b_normed, act, d_upper, d_q = lax.optimization_barrier((b_normed, act, d_upper, d_q))
-        g_give, g_keep, p_give, p_keep, sums_f = run(
+        up_near = after(up_near, d_q)
+        up_far = swap(up_near, "ctx", n_ctx, 1)
+        down_near = half_of(t_down_t, peer_up, peer_down)
+        b_normed = after(b_normed, up_near, down_near, d_q)
+
+        g_give, g_keep, sums_f = run(
             functools.partial(student_ffn_grads_kernel, n_ctx),
             "student_ffn_grads",
             [
                 ((narrow // 2, 2 * hidden), BF),
                 ((narrow // 2, 2 * hidden), F32),
-                ((rows, narrow), BF),
-                ((rows, narrow), F32),
                 ((2, narrow), F32),
             ],
-            [info, b_normed, act, d_upper, grad, student_down, peer_down],
-            scratch=[pltpu.VMEM((narrow, 2 * hidden), F32), pltpu.VMEM((total, narrow), F32)],
-            flops=6 * total * narrow * hidden,
-        )
-        g_ffn = halving(g_give, g_keep, dp, ctx)
+            [info, b_normed, act, d_upper, grad],
+            scratch=[pltpu.VMEM((narrow, 2 * hidden), F32)],
+            flops=4 * total * narrow * hidden,
+        )
+        down_far = swap(after(down_near, *gots), "ctx", n_ctx, 1)
+        w_out_peer = swap(after(w_out_give, peer_up, peer_down), "dp", n_dp, 1)
+        every = after(every, g_give, up_far, *gots)
+        pieces = [up_near, up_far, down_near, down_far]
+        o_cols, o_tail = run(
+            teacher_out_kernel,
+            "teacher_out",
+            [((total, cols), BF), ((total, tail), BF)],
+            [info, every, t_att_tail.reshape(total, tail), teacher_attn_out, w_out_peer],
+            scratch=[pltpu.VMEM((wide, t_q_width), BF)],
+            flops=2 * total * wide * (cols + tail),
+        )
+        o_every = lax.all_gather(o_cols, "tp", axis=0)
         d_own = d_own.reshape(total, s_kv_width)
         gots = [g.reshape(total, s_kv_width) for g in gots]
         a_give, a_keep, ga_give, ga_keep, sums_q = run(
             functools.partial(student_in_kernel, s_heads, len(gots), n_ctx),
             "student_in",
             [
-                ((rows, narrow), BF),
-                ((rows, narrow), F32),
+                ((rows, 2 * narrow), BF),
+                ((rows, 2 * narrow), F32),
                 ((narrow // n_dp, 4 * s_cols), BF),
                 ((narrow // n_dp, 4 * s_cols), F32),
                 ((2, s_cols), F32),
@@ -927,91 +954,88 @@
             [
                 info,
                 d_q.reshape(total, s_cols),
-                s_normed,
+                after(s_normed, o_every),
                 d_a,
                 s_att.reshape(total, s_cols),
                 s_in_t,
                 peer_qkv,
+                act,
+                student_down,
+                peer_down,
                 d_own,
             ]
             + gots,
-            scratch=[pltpu.VMEM((total, narrow), F32), pltpu.VMEM((narrow, 4 * s_cols), F32)],
+            scratch=[pltpu.VMEM((total, 2 * narrow), F32), pltpu.VMEM((narrow, 4 * s_cols), F32)],
             flops=2 * total * narrow * 7 * s_cols,
         )
         r3, other3 = tp_sum(a_give, a_keep)
-        g_att = halving(ga_give, ga_keep, dp, ctx)
-        in_grad, sums = run(
+        g_give, g_keep = ring_order(g_give, ctx), ring_order(g_keep, ctx)
+        ga_give, ga_keep = ring_order(ga_give, ctx), ring_order(ga_keep, ctx)
+        g_got = swap(after(g_give, w_out_peer), "dp", n_dp, 1)
+        ga_got = swap(after(ga_give, w_out_peer), "dp", n_dp, 1)
+        g_near = halve(g_keep + after(g_got, down_far).astype(F32), 1)
+        d_mid = after(d_mid, g_got, down_far)
+        in_grad, s_result, sums = run(
             student_last_kernel,
             "student_last",
-            [((total, narrow), F32), ((8, narrow), F32)],
-            [info, s_x, student_gain_a, r3, other3, d_mid, sums_b, sums_f, sums_q],
-            scratch=[pltpu.VMEM((total, narrow), F32)],
-        )
-
-        t_att, t_att_tail = run(
-            functools.partial(teacher_attend_kernel, t_heads, 1),
-            "teacher_attend",
-            [((slots, rows, cols), BF), ((slots, rows, tail), BF)],
-            [info, t_q, t_kv_all],
-            flops=4 * total * (cols + tail) * keys,
-            extra=total * t_heads * keys,
-        )
-        every = lax.all_gather(t_att.reshape(total, cols), "tp", axis=0)
-        o_cols, o_tail = run(
-            teacher_out_kernel,
-            "teacher_out",
-            [((total, cols), BF), ((total, tail), BF)],
-            [info, every, t_att_tail.reshape(total, tail), teacher_attn_out, w_out_peer],
-            scratch=[pltpu.VMEM((wide, t_q_width), BF)],
-            flops=2 * total * wide * (cols + tail),
-        )
-        o_every = lax.all_gather(o_cols, "tp", axis=0)
-        t_hidden = teacher_up.shape[1]
-        slab = -(-t_half // 128) * 128
-        t_mid, f_give, f_keep = run(
-            functools.partial(teacher_ffn_kernel, 256, slab),
-            "teacher_ffn",
-            [
-                ((total, wide), F32),
-                ((rows, 2 * slab + narrow), BF),
-                ((rows, 2 * slab + narrow), F32),
-            ],
+            [((total, narrow), F32), ((total, narrow), BF), ((8, narrow), F32)],
             [
                 info,
-                t_x,
+                s_x,
+                student_gain_a,
+                s_mid,
+                student_down_bias,
+                r3,
+                other3,
+                d_mid,
+                sums_b,
+                sums_f,
+                sums_q,
+            ],
+            scratch=[pltpu.VMEM((total, narrow), F32)],
+        )
+
+        t_hidden = teacher_up.shape[1]
+        packed = -(-wide // 128) * 128
+        t_mid, f_give, f_keep = run(
+            functools.partial(teacher_ffn_kernel, 256),
+            "teacher_ffn",
+            [((total, wide), F32), ((rows, packed), BF), ((rows, packed), F32)],
+            [
+                info,
+                after(t_x, g_got, ga_got, sums),
                 teacher_out_bias,
                 teacher_gain_b,
                 teacher_shift_b,
                 teacher_up_bias,
                 o_every,
                 o_tail,
-                p_give,
-                p_keep,
                 teacher_up,
-                up_peer,
                 t_down_t,
-                down_peer,
-            ],
-            specs=[SMEM] + [VMEM] * 9 + [ANY] * 4,
+            ]
+            + pieces,
+            specs=[SMEM] + [VMEM] * 7 + [ANY] * 6,
             scratch=[
-                pltpu.VMEM((wide, t_hidden), BF),
-                pltpu.VMEM((2, t_half, t_hidden), BF),
+                pltpu.VMEM((2 * wide, t_hidden), BF),
                 pltpu.VMEM((total, t_hidden), BF),
                 pltpu.VMEM((total, wide), BF),
-                pltpu.VMEM((total, slab), F32),
-                pltpu.SemaphoreType.DMA((4,)),
+                pltpu.VMEM((total, wide), F32),
+                pltpu.SemaphoreType.DMA((6,)),
             ],
             flops=4 * total * wide * t_hidden,
         )
-        r4, other4 = tp_sum(f_give, f_keep)
-        t_result, s_result = run(
-            functools.partial(last_kernel, slab),
+        r4, other4 = tp_sum(f_give, after(f_keep, g_near))
+        g_ffn = over_rings(halve(g_near, 3))
+        ga_got = after(ga_got, f_give)
+        g_att = over_rings(halve(halve(ga_keep + ga_got.astype(F32), 1), 3))
+        t_result = run(
+            last_kernel,
             "last",
-            [((total, wide), BF), ((total, narrow), BF)],
-            [info, t_mid, s_mid, teacher_down_bias, student_down_bias, r4, other4],
-        )
-
-        small = small_sum(sums)
+            [((total, wide), BF)],
+            [info, t_mid, teacher_down_bias, r4, other4],
+        )[0]
+
+        small = small_sum(after(sums, f_give))
         piece = narrow // (n_dp * n_ctx)
         shards = lax.dynamic_slice_in_dim(small, (dp * n_ctx + ctx) * piece, piece, axis=1)
 

time: 401 us -> 285 us (0.71)
  waiting for transfers between devices: 222 us -> 114 us
  starting transfers between devices: 37.4 us -> 53.8 us
  between operations: 14.2 us -> 1.26 us
  local copies, waits for them, and re-layouts: 26.2 us -> 19.1 us
    ppermute x28 -> x32, waiting for transfers between devices: 188 us -> 48.1 us  [swap(): return lax.ppermute(x, axis, [(i, i ^ bit) for i in range(size)])]
    ppermute x3 -> x4, waiting for transfers between devices: 0.01 us -> 20.7 us  [gather_keys(): out.append(lax.ppermute(kv, 'ctx', [(i, i + k) for i in range(n_ctx - k)]))]
    ppermute x3, waiting for transfers between devices: 33.1 us -> 45.1 us  [body(): lax.ppermute(d_parts[k], 'ctx', [(i + k, i) for i in range(n_ctx - k)])]
    ppermute x28 -> x32, starting transfers between devices: 23.9 us -> 32.7 us  [swap(): return lax.ppermute(x, axis, [(i, i ^ bit) for i in range(size)])]
    ppermute x3 -> x4, starting transfers between devices: 9.31 us -> 15.9 us  [gather_keys(): out.append(lax.ppermute(kv, 'ctx', [(i, i + k) for i in range(n_ctx - k)]))]
    dynamic_slice x4 -> x2, local copies, waits for them, and re-layouts: 8.7 us -> 2.38 us  [half_of(): part = lax.dynamic_slice_in_dim(w, ctx % 2 * quarter, quarter)]
    unnamed x59 -> x81, local copies, waits for them, and re-layouts: 13.1 us -> 13.1 us
  transfers between devices with their start and end apart: 39 -> 41, of which waited for: 22 -> 18; matrix products, arithmetic and copies ran while one was open for 6% -> 5% of each run, Pallas kernels for 13% -> 22%
where the time goes in v1:
time: 285 us; the launch traced here: 284 us
  waiting for transfers between devices  114 us (40%)
  Pallas kernels  69.7 us (24%)
  starting transfers between devices  53.8 us (19%)
  blocking collectives  20.1 us (7%)
  local copies, waits for them, and re-layouts  19.1 us (7%)
  other arithmetic  6.59 us (2%)
    pallas_call x14, Pallas kernels, run(): pl.pallas_call(kernel, out_shape=out_shape, in_specs=specs, out_specs=[VM...  69.7 us
    ppermute x32, waiting for transfers between devices, swap(): return lax.ppermute(x, axis, [(i, i ^ bit) for i in range(size)])  48.1 us
    ppermute x3, waiting for transfers between devices, body(): lax.ppermute(d_parts[k], 'ctx', [(i + k, i) for i in range(n_ctx - k)])  45.1 us
    ppermute x32, starting transfers between devices, swap(): return lax.ppermute(x, axis, [(i, i ^ bit) for i in range(size)])  32.7 us
    ppermute x4, waiting for transfers between devices, gather_keys(): out.append(lax.ppermute(kv, 'ctx', [(i, i + k) for i in range(n_ctx - k)]))  20.7 us
    ppermute x4, starting transfers between devices, gather_keys(): out.append(lax.ppermute(kv, 'ctx', [(i, i + k) for i in range(n_ctx - k)]))  15.9 us
    unnamed x81, local copies, waits for them, and re-layouts  13.1 us
    all_gather x1, blocking collectives, body(): every = lax.all_gather(t_att.reshape(total, cols), 'tp', axis=0)  10.8 us
  transfers between devices with their start and end apart: 41, of which 18 were waited for; matrix products, arithmetic and copies ran while one was open for 5% of the time, Pallas kernels for 22%

profile of v1, /device:TPU:0, one launch (start us, length us, event | category | flops | bytes accessed | tf_op | source)
XLA Modules:
  0.0 284.4 jit_solution(13324769500601348257)
XLA Ops:
  9.5 5.4 %collective-permute-done.peer = bf16[3,192,384]{2,1,0:T(8,128)(2,1)S(1)} collective-permute-done((bf16[3,192,384]{2,1,0:T(8,128)(2,1)}, bf16[3,192,384]{2,1,0:T(8,128)(2,1)S(1)}, u32[]{:S(2)}, u32[]{:S(2)}) %collective-permute-start) | collective-permute-done | bytes 442400 | tf_op jit(solution)/shard_map/ppermute | solution.py:649
  18.6 4.0 %collective-permute-start.1 = (bf16[2,128,384]{2,1,0:T(8,128)(2,1)}, bf16[2,128,384]{2,1,0:T(8,128)(2,1)S(1)}, u32[]{:S(2)}, u32[]{:S(2)}) collective-permute-start(bf16[2,128,384]{2,1,0:T(8,128)(2,1)} %bitcast.64), channel_id=1, source_target_pairs={{0,4},{4,8},{8,12},{1,5},{5,9},{9,13},{2,6},{6,10},{10,14},{3,7},{... | collective-permute-start | bytes 589832 | tf_op jit(solution)/shard_map/ppermute | solution.py:665
  24.7 4.7 %collective-permute-done.2.peer_ref = bf16[192,384]{1,0:T(8,128)(2,1)S(1)} collective-permute-done((bf16[192,384]{1,0:T(8,128)(2,1)S(1)}, bf16[192,384]{1,0:T(8,128)(2,1)S(1)}, u32[]{:S(2)}, u32[]{:S(2)}) %collective-permute-start.2) | collective-permute-done | bytes 147488 | tf_op jit(solution)/shard_map/ppermute | solution.py:649
  30.2 7.5 %teacher_qkv.1 = (bf16[256,1408]{1,0:T(8,128)(2,1)}, f32[256,1408]{1,0:T(8,128)}, bf16[800,512]{1,0:T(8,128)(2,1)}) custom-call(s32[7]{0:T(128)} %concatenate.3.info, bf16[256,800]{1,0:T(8,128)(2,1)} %get-tuple-element.93.mine, bf16[256,800]{1,0:T(8,128)(2,1)} %copy-done.28, bf16[3,800,1600]{2,1,0:T(8,128)(2,1)} %w_hbm.1, bf16[800,1600]{1,0:T(8,128)(2,1)} %w.1), custom_call_target="tpu_custom_call" | custom-call | flops 1 | bytes 1 | tf_op jit(solution)/shard_map/teacher_qkv/pallas_call | solution.py:93
  39.3 4.6 %collective-permute-start.6 = (bf16[2,128,384]{2,1,0:T(8,128)(2,1)S(1)}, bf16[2,128,384]{2,1,0:T(8,128)(2,1)S(1)}, u32[]{:S(2)}, u32[]{:S(2)}) collective-permute-start(bf16[2,128,384]{2,1,0:T(8,128)(2,1)S(1)} %bitcast.67), channel_id=1, source_target_pairs={{0,12},{1,13},{2,14},{3,15},{16,28},{17,29},{18,30},{19,31}} | collective-permute-start | bytes 589832 | tf_op jit(solution)/shard_map/ppermute | solution.py:665
  48.4 4.6 %student_attend.1 = (bf16[2,128,192]{2,1,0:T(8,128)(2,1)}, bf16[128,768]{1,0:T(8,128)(2,1)}, f32[128,768]{1,0:T(8,128)}) custom-call(s32[7]{0:T(128)} %concatenate.3.info, bf16[2,128,256]{2,1,0:T(8,128)(2,1)} %bitcast.68, bf16[192,384]{1,0:T(8,128)(2,1)} %own_ref.3, bf16[192,384]{1,0:T(8,128)(2,1)} %copy-done.21, bf16[2,128,384]{2,1,0:T(8,128)(2,1)} %bitcast.65, ...), custom_call_target="tpu_custom_call" | custom-call | flops 1 | bytes 1 | tf_op jit(solution)/shard_map/student_attend/pallas_call | solution.py:93
  62.5 6.0 %collective-permute-start.8 = (bf16[2,128,896]{2,1,0:T(8,128)(2,1)}, bf16[2,128,896]{2,1,0:T(8,128)(2,1)S(1)}, u32[]{:S(2)}, u32[]{:S(2)}) collective-permute-start(bf16[2,128,896]{2,1,0:T(8,128)(2,1)} %bitcast.70), channel_id=1, source_target_pairs={{0,12},{1,13},{2,14},{3,15},{16,28},{17,29},{18,30},{19,31}} | collective-permute-start | bytes 1376264 | tf_op jit(solution)/shard_map/ppermute | solution.py:665
  70.1 9.7 %collective-permute-done.8.refs_3_ = bf16[2,128,896]{2,1,0:T(8,128)(2,1)S(1)} collective-permute-done((bf16[2,128,896]{2,1,0:T(8,128)(2,1)}, bf16[2,128,896]{2,1,0:T(8,128)(2,1)S(1)}, u32[]{:S(2)}, u32[]{:S(2)}) %collective-permute-start.8) | collective-permute-done | bytes 458784 | tf_op jit(solution)/shard_map/ppermute | solution.py:665
  79.7 8.5 %collective-permute-done.9.refs_1_ = bf16[2,128,896]{2,1,0:T(8,128)(2,1)S(1)} collective-permute-done((bf16[2,128,896]{2,1,0:T(8,128)(2,1)}, bf16[2,128,896]{2,1,0:T(8,128)(2,1)S(1)}, u32[]{:S(2)}, u32[]{:S(2)}) %collective-permute-start.9) | collective-permute-done | bytes 458784 | tf_op jit(solution)/shard_map/ppermute | solution.py:665
  89.9 5.0 %student_ffn.1 = (f32[256,768]{1,0:T(8,128)}, bf16[256,768]{1,0:T(8,128)(2,1)}, bf16[256,768]{1,0:T(8,128)(2,1)}, bf16[256,768]{1,0:T(8,128)(2,1)}, bf16[128,768]{1,0:T(8,128)(2,1)}, /*index=5*/f32[128,768]{1,0:T(8,128)}) custom-call(s32[7]{0:T(128)} %concatenate.3.info, bf16[256,768]{1,0:T(8,128)(2,1)} %bitcast.54, bf16[768]{0:T(1024)(128)(2,1)} %out_bias.2, ...), custom_call_target="tpu_custom_call" | custom-call | flops 1 | bytes 1 | tf_op jit(solution)/shard_map/student_ffn/pallas_call | solution.py:93
  107.5 6.3 %teacher_attend.1 = (bf16[2,128,384]{2,1,0:T(8,128)(2,1)}, bf16[2,128,64]{2,1,0:T(8,128)(2,1)}) custom-call(s32[7]{0:T(128)} %concatenate.3.info, bf16[2,128,512]{2,1,0:T(8,128)(2,1)} %bitcast.74, bf16[2,128,896]{2,1,0:T(8,128)(2,1)} %bitcast.72, bf16[2,128,896]{2,1,0:T(8,128)(2,1)} %copy-done.25, bf16[2,128,896]{2,1,0:T(8,128)(2,1)} %copy-done.27, ...), custom_call_target="tpu_custom_call" | custom-call | flops 1 | bytes 1 | tf_op jit(solution)/shard_map/teacher_attend/pallas_call | solution.py:93
  113.8 10.8 %all_gather.9.every = bf16[4,256,384]{2,1,0:T(8,128)(2,1)} all-gather(bf16[1,256,384]{2,1,0:T(8,128)(2,1)} %bitcast.78), channel_id=1, replica_groups=mesh['dp'=2,'ctx'=4,'tp'=4] {'tp'}, dimensions={0}, use_global_device_ids=true | all-gather | bytes 983040 | tf_op jit(solution)/shard_map/all_gather | solution.py:876
  125.2 7.7 %student_back.1 = (f32[256,768]{1,0:T(8,128)}, bf16[256,768]{1,0:T(8,128)(2,1)}, bf16[2,128,192]{2,1,0:T(8,128)(2,1)}, f32[3,768]{1,0:T(4,128)}, f32[2,128,384]{...) custom-call(s32[7]{0:T(128)} %concatenate.3.info, ...), custom_call_target="tpu_custom_call" | custom-call | flops 1 | bytes 1 | tf_op jit(solution)/shard_map/student_back/pallas_call | solution.py:93
  132.9 4.4 %collective-permute-start.22 = (bf16[400,1600]{1,0:T(8,128)(2,1)S(1)}, bf16[400,1600]{1,0:T(8,128)(2,1)S(1)}, u32[]{:S(2)}, u32[]{:S(2)}) collective-permute-start(bf16[400,1600]{1,0:T(8,128)(2,1)S(1)} %collective-permute-done.14.up_near), channel_id=1, source_target_pairs={{0,4},{4,0},{8,12},{12,8},{1,5},{5,1},{9,13},{13,9},{2,6},{6,2},{1... | collective-permute-start | bytes 3840008 | tf_op jit(solution)/shard_map/ppermute | solution.py:649
  139.9 35.6 %collective-permute-done.23 = bf16[2,128,384]{2,1,0:T(8,128)(2,1)S(1)} collective-permute-done((bf16[2,128,384]{2,1,0:T(8,128)(2,1)}, bf16[2,128,384]{2,1,0:T(8,128)(2,1)S(1)}, u32[]{:S(2)}, u32[]{:S(2)}) %collective-permute-start.23) | collective-permute-done | bytes 196640 | tf_op jit(solution)/shard_map/ppermute | solution.py:906
  176.7 9.5 %collective-permute-done.25 = bf16[2,128,384]{2,1,0:T(8,128)(2,1)S(1)} collective-permute-done((bf16[2,128,384]{2,1,0:T(8,128)(2,1)}, bf16[2,128,384]{2,1,0:T(8,128)(2,1)S(1)}, u32[]{:S(2)}, u32[]{:S(2)}) %collective-permute-start.25) | collective-permute-done | bytes 196640 | tf_op jit(solution)/shard_map/ppermute | solution.py:906
  186.3 4.3 %student_ffn_grads.1 = (bf16[384,1536]{1,0:T(8,128)(2,1)}, f32[384,1536]{1,0:T(8,128)}, f32[2,768]{1,0:T(2,128)}) custom-call(s32[7]{0:T(128)} %concatenate.3.info, bf16[256,768]{1,0:T(8,128)(2,1)} %get-tuple-element.120.normed, bf16[256,768]{1,0:T(8,128)(2,1)} %get-tuple-element.121.act, bf16[256,768]{1,0:T(8,128)(2,1)} %get-tuple-element.122.d_upper, ...), custom_call_target="tpu_custom_call" | custom-call | flops 1 | bytes 1 | tf_op jit(solution)/shard_map/student_ffn_grads/pallas_call | solution.py:93
  191.5 4.0 %teacher_out.1 = (bf16[256,384]{1,0:T(8,128)(2,1)}, bf16[256,64]{1,0:T(8,128)(2,1)}) custom-call(s32[7]{0:T(128)} %concatenate.3.info, bf16[4,256,384]{2,1,0:T(8,128)(2,1)} %all_gather.9.every, bf16[256,64]{1,0:T(8,128)(2,1)} %bitcast.81, bf16[800,1600]{1,0:T(8,128)(2,1)} %w.1, bf16[800,512]{1,0:T(8,128)(2,1)} %copy-done.12), custom_call_target="tpu_custom_call" | custom-call | flops 1 | bytes 1 | tf_op jit(solution)/shard_map/teacher_out/pallas_call | solution.py:93
  195.5 9.3 %all-gather = bf16[1024,384]{1,0:T(8,128)(2,1)} all-gather(bf16[256,384]{1,0:T(8,128)(2,1)} %get-tuple-element.133), channel_id=2, replica_groups=mesh['dp'=2,'ctx'=4,'tp'=4] {'tp'}, dimensions={0}, use_global_device_ids=true | all-gather | bytes 983040 | tf_op jit(solution)/shard_map/all_gather | solution.py:941
  204.8 5.2 %student_in.1 = (bf16[128,1536]{1,0:T(8,128)(2,1)}, f32[128,1536]{1,0:T(8,128)}, bf16[384,768]{1,0:T(8,128)(2,1)}, f32[384,768]{1,0:T(8,128)}, f32[2,192]{1,0:T(2,128)}) custom-call(s32[7]{0:T(128)} %concatenate.3.info, bf16[256,192]{1,0:T(8,128)(2,1)} %bitcast.80, bf16[256,768]{1,0:T(8,128)(2,1)} %get-tuple-element.134.normed, ...), custom_call_target="tpu_custom_call" | custom-call | flops 1 | bytes 1 | tf_op jit(solution)/shard_map/student_in/pallas_call | solution.py:93
  210.4 7.0 %collective-permute-done.21 = bf16[384,1536]{1,0:T(8,128)(2,1)} collective-permute-done((bf16[384,1536]{1,0:T(8,128)(2,1)}, bf16[384,1536]{1,0:T(8,128)(2,1)}, u32[]{:S(2)}, u32[]{:S(2)}) %collective-permute-start.21) | collective-permute-done | bytes 1179680 | tf_op jit(solution)/shard_map/ppermute | solution.py:649
  227.6 7.6 %collective-permute-done.31 = bf16[192,1536]{1,0:T(8,128)(2,1)S(1)} collective-permute-done((bf16[192,1536]{1,0:T(8,128)(2,1)S(1)}, bf16[192,1536]{1,0:T(8,128)(2,1)S(1)}, u32[]{:S(2)}, u32[]{:S(2)}) %collective-permute-start.31) | collective-permute-done | bytes 589856 | tf_op jit(solution)/shard_map/ppermute | solution.py:649
  239.8 10.2 %teacher_ffn.1 = (f32[256,1600]{1,0:T(8,128)}, bf16[128,1664]{1,0:T(8,128)(2,1)}, f32[128,1664]{1,0:T(8,128)}) custom-call(s32[7]{0:T(128)} %concatenate.3.info, bf16[256,1600]{1,0:T(8,128)(2,1)} %bitcast.51, bf16[1600]{0:T(1024)(128)(2,1)} %out_bias.3, bf16[1600]{0:T(1024)(128)(2,1)} %gain.11, bf16[1600]{0:T(1024)(128)(2,1)} %shift.7, ...), custom_call_target="tpu_custom_call" | custom-call | flops 1 | bytes 1 | tf_op jit(solution)/shard_map/teacher_ffn/pallas_call | solution.py:93
  271.2 3.6 %collective-permute-done.33 = bf16[128,1664]{1,0:T(8,128)(2,1)S(1)} collective-permute-done((bf16[128,1664]{1,0:T(8,128)(2,1)S(1)}, bf16[128,1664]{1,0:T(8,128)(2,1)S(1)}, u32[]{:S(2)}, u32[]{:S(2)}) %collective-permute-start.33) | collective-permute-done | bytes 426016 | tf_op jit(solution)/shard_map/ppermute | solution.py:649
  (188 shorter events, 97.7 us)
Async XLA Ops:
  0.7 14.3 %collective-permute-start = (bf16[3,192,384]{2,1,0:T(8,128)(2,1)}, bf16[3,192,384]{2,1,0:T(8,128)(2,1)S(1)}, u32[]{:S(2)}, u32[]{:S(2)}) collective-permute-start(bf16[3,192,384]{2,1,0:T(8,128)(2,1)} %bitcast.61), channel_id=1, source_target_pairs={{0,16},{16,0},{1,17},{17,1},{2,18},{18,2},{3,19},{19,3},{4,20},{20... | collective-permute-start | bytes 1327112 | tf_op jit(solution)/shard_map/ppermute | solution.py:649
  9.5 19.9 %collective-permute-start.3 = (bf16[256,800]{1,0:T(8,128)(2,1)}, bf16[256,800]{1,0:T(8,128)(2,1)S(1)}, u32[]{:S(2)}, u32[]{:S(2)}) collective-permute-start(bf16[256,800]{1,0:T(8,128)(2,1)} %get-tuple-element.88), channel_id=1, source_target_pairs={{0,16},{16,0},{1,17},{17,1},{2,18},{18,2},{3,19},{19,3},{4,20},{20... | collective-permute-start | bytes 1228808 | tf_op jit(solution)/shard_map/ppermute | solution.py:649
  18.6 10.8 %collective-permute-start.1 = (bf16[2,128,384]{2,1,0:T(8,128)(2,1)}, bf16[2,128,384]{2,1,0:T(8,128)(2,1)S(1)}, u32[]{:S(2)}, u32[]{:S(2)}) collective-permute-start(bf16[2,128,384]{2,1,0:T(8,128)(2,1)} %bitcast.64), channel_id=1, source_target_pairs={{0,4},{4,8},{8,12},{1,5},{5,9},{9,13},{2,6},{6,10},{10,14},{3,7},{... | collective-permute-start | bytes 589832 | tf_op jit(solution)/shard_map/ppermute | solution.py:665
  24.1 20.4 %collective-permute-start.4 = (bf16[384,768]{1,0:T(8,128)(2,1)S(1)}, bf16[384,768]{1,0:T(8,128)(2,1)S(1)}, u32[]{:S(2)}, u32[]{:S(2)}) collective-permute-start(bf16[384,768]{1,0:T(8,128)(2,1)S(1)} %copy-done.22), channel_id=1, source_target_pairs={{0,16},{16,0},{1,17},{17,1},{2,18},{18,2},{3,19},{19,3},{4,20},{20... | collective-permute-start | bytes 1769480 | tf_op jit(solution)/shard_map/ppermute | solution.py:649
  37.7 17.4 %collective-permute-start.7 = (bf16[256,1408]{1,0:T(8,128)(2,1)}, bf16[256,1408]{1,0:T(8,128)(2,1)S(1)}, u32[]{:S(2)}, u32[]{:S(2)}) collective-permute-start(bf16[256,1408]{1,0:T(8,128)(2,1)} %get-tuple-element.96), channel_id=1, source_target_pairs={{0,16},{16,0},{1,17},{17,1},{2,18},{18,2},{3,19},{19,3},{4,20},{20... | collective-permute-start | bytes 2162696 | tf_op jit(solution)/shard_map/ppermute | solution.py:649
  56.4 13.4 %collective-permute-start.11 = (bf16[128,768]{1,0:T(8,128)(2,1)S(1)}, bf16[128,768]{1,0:T(8,128)(2,1)S(1)}, u32[]{:S(2)}, u32[]{:S(2)}) collective-permute-start(bf16[128,768]{1,0:T(8,128)(2,1)S(1)} %add_convert_fusion.7), channel_id=1, source_target_pairs={{0,2},{1,3},{2,0},{3,1},{4,6},{5,7},{6,4},{7,5},{8,10},{9,11},{10,... | collective-permute-start | bytes 589832 | tf_op jit(solution)/shard_map/ppermute | solution.py:649
  58.3 29.9 %collective-permute-start.13 = (bf16[768,384]{1,0:T(8,128)(2,1)S(1)}, bf16[768,384]{1,0:T(8,128)(2,1)S(1)}, u32[]{:S(2)}, u32[]{:S(2)}) collective-permute-start(bf16[768,384]{1,0:T(8,128)(2,1)S(1)} %copy-done.2), channel_id=1, source_target_pairs={{0,16},{16,0},{1,17},{17,1},{2,18},{18,2},{3,19},{19,3},{4,20},{20... | collective-permute-start | bytes 1769480 | tf_op jit(solution)/shard_map/ppermute | solution.py:649
  62.5 17.2 %collective-permute-start.8 = (bf16[2,128,896]{2,1,0:T(8,128)(2,1)}, bf16[2,128,896]{2,1,0:T(8,128)(2,1)S(1)}, u32[]{:S(2)}, u32[]{:S(2)}) collective-permute-start(bf16[2,128,896]{2,1,0:T(8,128)(2,1)} %bitcast.70), channel_id=1, source_target_pairs={{0,12},{1,13},{2,14},{3,15},{16,28},{17,29},{18,30},{19,31}} | collective-permute-start | bytes 1376264 | tf_op jit(solution)/shard_map/ppermute | solution.py:665
  68.6 19.7 %collective-permute-start.9 = (bf16[2,128,896]{2,1,0:T(8,128)(2,1)}, bf16[2,128,896]{2,1,0:T(8,128)(2,1)S(1)}, u32[]{:S(2)}, u32[]{:S(2)}) collective-permute-start(bf16[2,128,896]{2,1,0:T(8,128)(2,1)} %bitcast.71), channel_id=1, source_target_pairs={{0,4},{4,8},{8,12},{1,5},{5,9},{9,13},{2,6},{6,10},{10,14},{3,7},{... | collective-permute-start | bytes 1376264 | tf_op jit(solution)/shard_map/ppermute | solution.py:665
  70.0 18.3 %collective-permute-start.12 = (bf16[128,768]{1,0:T(8,128)(2,1)S(1)}, bf16[128,768]{1,0:T(8,128)(2,1)S(1)}, u32[]{:S(2)}, u32[]{:S(2)}) collective-permute-start(bf16[128,768]{1,0:T(8,128)(2,1)S(1)} %add_convert_fusion.6.r_ref), channel_id=1, source_target_pairs={{0,1},{1,0},{2,3},{3,2},{4,5},{5,4},{6,7},{7,6},{8,9},{9,8},{10,11... | collective-permute-start | bytes 589832 | tf_op jit(solution)/shard_map/ppermute | solution.py:649
  96.2 36.7 %collective-permute-start.14 = (bf16[400,1600]{1,0:T(8,128)(2,1)}, bf16[400,1600]{1,0:T(8,128)(2,1)S(1)}, u32[]{:S(2)}, u32[]{:S(2)}) collective-permute-start(bf16[400,1600]{1,0:T(8,128)(2,1)} %constant_dynamic-slice_fusion.1), channel_id=1, source_target_pairs={{0,16},{16,0},{1,17},{17,1},{2,18},{18,2},{3,19},{19,3},{4,20},{20... | collective-permute-start | bytes 3840008 | tf_op jit(solution)/shard_map/ppermute | solution.py:649
  101.2 85.0 %collective-permute-start.19 = (bf16[400,1600]{1,0:T(8,128)(2,1)}, bf16[400,1600]{1,0:T(8,128)(2,1)}, u32[]{:S(2)}, u32[]{:S(2)}) collective-permute-start(bf16[400,1600]{1,0:T(8,128)(2,1)} %dynamic-slice_bitcast_fusion), channel_id=1, source_target_pairs={{0,16},{16,0},{1,17},{17,1},{2,18},{18,2},{3,19},{19,3},{4,20},{20... | collective-permute-start | bytes 3840008 | tf_op jit(solution)/shard_map/ppermute | solution.py:649
  101.8 88.8 %collective-permute-start.20 = (bf16[800,512]{1,0:T(8,128)(2,1)}, bf16[800,512]{1,0:T(8,128)(2,1)S(1)}, u32[]{:S(2)}, u32[]{:S(2)}) collective-permute-start(bf16[800,512]{1,0:T(8,128)(2,1)} %get-tuple-element.125), channel_id=1, source_target_pairs={{0,16},{16,0},{1,17},{17,1},{2,18},{18,2},{3,19},{19,3},{4,20},{20... | collective-permute-start | bytes 2457608 | tf_op jit(solution)/shard_map/ppermute | solution.py:649
  106.6 17.9 %collective-permute-start.18 = (bf16[128,768]{1,0:T(8,128)(2,1)S(1)}, bf16[128,768]{1,0:T(8,128)(2,1)S(1)}, u32[]{:S(2)}, u32[]{:S(2)}) collective-permute-start(bf16[128,768]{1,0:T(8,128)(2,1)S(1)} %add_convert_fusion.4.r_ref), channel_id=1, source_target_pairs={{0,1},{1,0},{2,3},{3,2},{4,5},{5,4},{6,7},{7,6},{8,9},{9,8},{10,11... | collective-permute-start | bytes 589832 | tf_op jit(solution)/shard_map/ppermute | solution.py:649
  132.9 58.3 %collective-permute-start.22 = (bf16[400,1600]{1,0:T(8,128)(2,1)S(1)}, bf16[400,1600]{1,0:T(8,128)(2,1)S(1)}, u32[]{:S(2)}, u32[]{:S(2)}) collective-permute-start(bf16[400,1600]{1,0:T(8,128)(2,1)S(1)} %collective-permute-done.14.up_near), channel_id=1, source_target_pairs={{0,4},{4,0},{8,12},{12,8},{1,5},{5,1},{9,13},{13,9},{2,6},{6,2},{1... | collective-permute-start | bytes 3840008 | tf_op jit(solution)/shard_map/ppermute | solution.py:649
  137.3 38.2 %collective-permute-start.23 = (bf16[2,128,384]{2,1,0:T(8,128)(2,1)}, bf16[2,128,384]{2,1,0:T(8,128)(2,1)S(1)}, u32[]{:S(2)}, u32[]{:S(2)}) collective-permute-start(bf16[2,128,384]{2,1,0:T(8,128)(2,1)} %get-tuple-element.128), channel_id=1, source_target_pairs={{4,0},{8,4},{12,8},{5,1},{9,5},{13,9},{6,2},{10,6},{14,10},{7,3},{... | collective-permute-start | bytes 589832 | tf_op jit(solution)/shard_map/ppermute | solution.py:906
  138.6 38.2 %collective-permute-start.24 = (bf16[2,128,384]{2,1,0:T(8,128)(2,1)}, bf16[2,128,384]{2,1,0:T(8,128)(2,1)S(1)}, u32[]{:S(2)}, u32[]{:S(2)}) collective-permute-start(bf16[2,128,384]{2,1,0:T(8,128)(2,1)} %get-tuple-element.129), channel_id=1, source_target_pairs={{8,0},{12,4},{9,1},{13,5},{10,2},{14,6},{11,3},{15,7},{24,16},{28,... | collective-permute-start | bytes 589832 | tf_op jit(solution)/shard_map/ppermute | solution.py:906
  175.4 10.8 %collective-permute-start.25 = (bf16[2,128,384]{2,1,0:T(8,128)(2,1)}, bf16[2,128,384]{2,1,0:T(8,128)(2,1)S(1)}, u32[]{:S(2)}, u32[]{:S(2)}) collective-permute-start(bf16[2,128,384]{2,1,0:T(8,128)(2,1)} %get-tuple-element.130), channel_id=1, source_target_pairs={{12,0},{13,1},{14,2},{15,3},{28,16},{29,17},{30,18},{31,19}} | collective-permute-start | bytes 589832 | tf_op jit(solution)/shard_map/ppermute | solution.py:906
  186.3 31.1 %collective-permute-start.30 = (bf16[400,1600]{1,0:T(8,128)(2,1)}, bf16[400,1600]{1,0:T(8,128)(2,1)}, u32[]{:S(2)}, u32[]{:S(2)}) collective-permute-start(bf16[400,1600]{1,0:T(8,128)(2,1)} %collective-permute-done.19.down_near), channel_id=1, source_target_pairs={{0,4},{4,0},{8,12},{12,8},{1,5},{5,1},{9,13},{13,9},{2,6},{6,2},{1... | collective-permute-start | bytes 3840008 | tf_op jit(solution)/shard_map/ppermute | solution.py:649
  190.6 26.8 %collective-permute-start.21 = (bf16[384,1536]{1,0:T(8,128)(2,1)}, bf16[384,1536]{1,0:T(8,128)(2,1)}, u32[]{:S(2)}, u32[]{:S(2)}) collective-permute-start(bf16[384,1536]{1,0:T(8,128)(2,1)} %get-tuple-element.126), channel_id=1, source_target_pairs={{0,16},{16,0},{1,17},{17,1},{2,18},{18,2},{3,19},{19,3},{4,20},{20... | collective-permute-start | bytes 3538952 | tf_op jit(solution)/shard_map/ppermute | solution.py:649
  221.8 13.3 %collective-permute-start.31 = (bf16[192,1536]{1,0:T(8,128)(2,1)S(1)}, bf16[192,1536]{1,0:T(8,128)(2,1)S(1)}, u32[]{:S(2)}, u32[]{:S(2)}) collective-permute-start(bf16[192,1536]{1,0:T(8,128)(2,1)S(1)} %slice.129), channel_id=1, source_target_pairs={{0,4},{4,0},{8,12},{12,8},{1,5},{5,1},{9,13},{13,9},{2,6},{6,2},{1... | collective-permute-start | bytes 1769480 | tf_op jit(solution)/shard_map/ppermute | solution.py:649
  223.6 16.2 %collective-permute-start.26 = (bf16[384,768]{1,0:T(8,128)(2,1)}, bf16[384,768]{1,0:T(8,128)(2,1)S(1)}, u32[]{:S(2)}, u32[]{:S(2)}) collective-permute-start(bf16[384,768]{1,0:T(8,128)(2,1)} %get-tuple-element.138), channel_id=1, source_target_pairs={{0,16},{16,0},{1,17},{17,1},{2,18},{18,2},{3,19},{19,3},{4,20},{20... | collective-permute-start | bytes 1769480 | tf_op jit(solution)/shard_map/ppermute | solution.py:649
  235.3 15.2 %collective-permute-start.40 = (bf16[96,1536]{1,0:T(8,128)(2,1)S(1)}, bf16[96,1536]{1,0:T(8,128)(2,1)S(1)}, u32[]{:S(2)}, u32[]{:S(2)}) collective-permute-start(bf16[96,1536]{1,0:T(8,128)(2,1)S(1)} %slice.130), channel_id=1, source_target_pairs={{0,12},{4,8},{8,4},{12,0},{1,13},{5,9},{9,5},{13,1},{2,14},{6,10},... | collective-permute-start | bytes 884744 | tf_op jit(solution)/shard_map/ppermute | solution.py:649
  264.8 10.0 %collective-permute-start.33 = (bf16[128,1664]{1,0:T(8,128)(2,1)S(1)}, bf16[128,1664]{1,0:T(8,128)(2,1)S(1)}, u32[]{:S(2)}, u32[]{:S(2)}) collective-permute-start(bf16[128,1664]{1,0:T(8,128)(2,1)S(1)} %add_convert_fusion.1), channel_id=1, source_target_pairs={{0,2},{1,3},{2,0},{3,1},{4,6},{5,7},{6,4},{7,5},{8,10},{9,11},{10,... | collective-permute-start | bytes 1277960 | tf_op jit(solution)/shard_map/ppermute | solution.py:649
  (56 other events, 507.2 us)

commit v2 on v1

--- a/solution.py
+++ b/solution.py
@@ -912,7 +912,7 @@
         up_near = after(up_near, d_q)
         up_far = swap(up_near, "ctx", n_ctx, 1)
         down_near = half_of(t_down_t, peer_up, peer_down)
-        b_normed = after(b_normed, up_near, down_near, d_q)
+        b_normed = after(b_normed, up_near, d_q)
 
         g_give, g_keep, sums_f = run(
             functools.partial(student_ffn_grads_kernel, n_ctx),
@@ -926,9 +926,9 @@
             scratch=[pltpu.VMEM((narrow, 2 * hidden), F32)],
             flops=4 * total * narrow * hidden,
         )
-        down_far = swap(after(down_near, *gots), "ctx", n_ctx, 1)
+        down_far = swap(down_near, "ctx", n_ctx, 1)
         w_out_peer = swap(after(w_out_give, peer_up, peer_down), "dp", n_dp, 1)
-        every = after(every, g_give, up_far, *gots)
+        every = after(every, g_give, down_near)
         pieces = [up_near, up_far, down_near, down_far]
         o_cols, o_tail = run(
             teacher_out_kernel,
@@ -974,27 +974,6 @@
         g_got = swap(after(g_give, w_out_peer), "dp", n_dp, 1)
         ga_got = swap(after(ga_give, w_out_peer), "dp", n_dp, 1)
         g_near = halve(g_keep + after(g_got, down_far).astype(F32), 1)
-        d_mid = after(d_mid, g_got, down_far)
-        in_grad, s_result, sums = run(
-            student_last_kernel,
-            "student_last",
-            [((total, narrow), F32), ((total, narrow), BF), ((8, narrow), F32)],
-            [
-                info,
-                s_x,
-                student_gain_a,
-                s_mid,
-                student_down_bias,
-                r3,
-                other3,
-                d_mid,
-                sums_b,
-                sums_f,
-                sums_q,
-            ],
-            scratch=[pltpu.VMEM((total, narrow), F32)],
-        )
-
         t_hidden = teacher_up.shape[1]
         packed = -(-wide // 128) * 128
         t_mid, f_give, f_keep = run(
@@ -1003,7 +982,7 @@
             [((total, wide), F32), ((rows, packed), BF), ((rows, packed), F32)],
             [
                 info,
-                after(t_x, g_got, ga_got, sums),
+                after(t_x, g_got),
                 teacher_out_bias,
                 teacher_gain_b,
                 teacher_shift_b,
@@ -1024,10 +1003,33 @@
             ],
             flops=4 * total * wide * t_hidden,
         )
-        r4, other4 = tp_sum(f_give, after(f_keep, g_near))
-        g_ffn = over_rings(halve(g_near, 3))
-        ga_got = after(ga_got, f_give)
+        part = (after(f_keep, g_near) + swap(f_give, "tp", n_tp, 1).astype(F32)).astype(BF)
+        r4 = (part.astype(F32) + swap(part, "tp", n_tp, 2).astype(F32)).astype(BF)
+        other4 = swap(r4, "tp", n_tp, 1)
+        g_ffn = over_rings(halve(after(g_near, part), 3))
+        ga_got = after(ga_got, part)
         g_att = over_rings(halve(halve(ga_keep + ga_got.astype(F32), 1), 3))
+        d_mid = after(d_mid, part)
+        in_grad, s_result, sums = run(
+            student_last_kernel,
+            "student_last",
+            [((total, narrow), F32), ((total, narrow), BF), ((8, narrow), F32)],
+            [
+                info,
+                s_x,
+                student_gain_a,
+                s_mid,
+                student_down_bias,
+                r3,
+                other3,
+                d_mid,
+                sums_b,
+                sums_f,
+                sums_q,
+            ],
+            scratch=[pltpu.VMEM((total, narrow), F32)],
+        )
+
         t_result = run(
             last_kernel,
             "last",
@@ -1035,7 +1037,7 @@
             [info, t_mid, teacher_down_bias, r4, other4],
         )[0]
 
-        small = small_sum(after(sums, f_give))
+        small = small_sum(after(sums, r4))
         piece = narrow // (n_dp * n_ctx)
         shards = lax.dynamic_slice_in_dim(small, (dp * n_ctx + ctx) * piece, piece, axis=1)
 

time: 285 us -> 260 us (0.912)
  waiting for transfers between devices: 114 us -> 78.9 us
  other arithmetic: 6.59 us -> 11.8 us
  starting transfers between devices: 53.8 us -> 58.6 us
    ppermute x3, waiting for transfers between devices: 45.1 us -> 2.26 us  [body(): lax.ppermute(d_parts[k], 'ctx', [(i + k, i) for i in range(n_ctx - k)])]
    ppermute x32, waiting for transfers between devices: 48.1 us -> 59.6 us  [swap(): return lax.ppermute(x, axis, [(i, i ^ bit) for i in range(size)])]
    ppermute x32, starting transfers between devices: 32.7 us -> 37.4 us  [swap(): return lax.ppermute(x, axis, [(i, i ^ bit) for i in range(size)])]
    ppermute x4, waiting for transfers between devices: 20.7 us -> 17 us  [gather_keys(): out.append(lax.ppermute(kv, 'ctx', [(i, i + k) for i in range(n_ctx - k)]))]
    add x4, other arithmetic: 0.27 us -> 3.23 us  [halve(): return keep[:half] + got.astype(F32)]
    unnamed x81 -> x63, local copies, waits for them, and re-layouts: 13.1 us -> 14.7 us
  transfers between devices with their start and end apart: 41 -> 41, of which waited for: 18 -> 19; matrix products, arithmetic and copies ran while one was open for 5% -> 8% of each run, Pallas kernels for 22% -> 26%
where the time goes in v2:
time: 260 us; the launch traced here: 259 us
  waiting for transfers between devices  78.9 us (30%)
  Pallas kernels  69.5 us (27%)
  starting transfers between devices  58.6 us (23%)
  local copies, waits for them, and re-layouts  21.5 us (8%)
  blocking collectives  17.6 us (7%)
  other arithmetic  11.8 us (5%)
    pallas_call x14, Pallas kernels, run(): pl.pallas_call(kernel, out_shape=out_shape, in_specs=specs, out_specs=[VM...  69.5 us
    ppermute x32, waiting for transfers between devices, swap(): return lax.ppermute(x, axis, [(i, i ^ bit) for i in range(size)])  59.6 us
    ppermute x32, starting transfers between devices, swap(): return lax.ppermute(x, axis, [(i, i ^ bit) for i in range(size)])  37.4 us
    ppermute x4, waiting for transfers between devices, gather_keys(): out.append(lax.ppermute(kv, 'ctx', [(i, i + k) for i in range(n_ctx - k)]))  17 us
    ppermute x4, starting transfers between devices, gather_keys(): out.append(lax.ppermute(kv, 'ctx', [(i, i + k) for i in range(n_ctx - k)]))  15.3 us
    unnamed x63, local copies, waits for them, and re-layouts  14.7 us
    all_gather x1, blocking collectives, body(): every = lax.all_gather(t_att.reshape(total, cols), 'tp', axis=0)  9.3 us
    all_gather x1, blocking collectives, body(): o_every = lax.all_gather(o_cols, 'tp', axis=0)  8.26 us
  transfers between devices with their start and end apart: 41, of which 19 were waited for; matrix products, arithmetic and copies ran while one was open for 8% of the time, Pallas kernels for 26%

profile of v2, /device:TPU:0, one launch (start us, length us, event | category | flops | bytes accessed | tf_op | source)
XLA Modules:
  0.0 259.0 jit_solution(17836870038193907627)
XLA Ops:
  9.5 5.4 %collective-permute-done.peer = bf16[3,192,384]{2,1,0:T(8,128)(2,1)S(1)} collective-permute-done((bf16[3,192,384]{2,1,0:T(8,128)(2,1)}, bf16[3,192,384]{2,1,0:T(8,128)(2,1)S(1)}, u32[]{:S(2)}, u32[]{:S(2)}) %collective-permute-start) | collective-permute-done | bytes 442400 | tf_op jit(solution)/shard_map/ppermute | solution.py:649
  18.5 4.0 %collective-permute-start.1 = (bf16[2,128,384]{2,1,0:T(8,128)(2,1)}, bf16[2,128,384]{2,1,0:T(8,128)(2,1)S(1)}, u32[]{:S(2)}, u32[]{:S(2)}) collective-permute-start(bf16[2,128,384]{2,1,0:T(8,128)(2,1)} %bitcast.64), channel_id=1, source_target_pairs={{0,4},{4,8},{8,12},{1,5},{5,9},{9,13},{2,6},{6,10},{10,14},{3,7},{... | collective-permute-start | bytes 589832 | tf_op jit(solution)/shard_map/ppermute | solution.py:665
  24.7 4.7 %collective-permute-done.2.peer_ref = bf16[192,384]{1,0:T(8,128)(2,1)S(1)} collective-permute-done((bf16[192,384]{1,0:T(8,128)(2,1)S(1)}, bf16[192,384]{1,0:T(8,128)(2,1)S(1)}, u32[]{:S(2)}, u32[]{:S(2)}) %collective-permute-start.2) | collective-permute-done | bytes 147488 | tf_op jit(solution)/shard_map/ppermute | solution.py:649
  29.4 7.7 %teacher_qkv.1 = (bf16[256,1408]{1,0:T(8,128)(2,1)}, f32[256,1408]{1,0:T(8,128)}, bf16[800,512]{1,0:T(8,128)(2,1)}) custom-call(s32[7]{0:T(128)} %concatenate.3.info, bf16[256,800]{1,0:T(8,128)(2,1)} %get-tuple-element.93.mine, bf16[256,800]{1,0:T(8,128)(2,1)} %collective-permute-done.3.other, bf16[3,800,1600]{2,1,0:T(8,128)(2,1)} %w_hbm.1, bf16[800,1600]{1,0:T(8,128)(2,1)} %w.1), custom_call_target="tpu_custom_call" | custom-call | flops 1 | bytes 1 | tf_op jit(solution)/shard_map/teacher_qkv/pallas_call | solution.py:93
  38.7 4.6 %collective-permute-start.6 = (bf16[2,128,384]{2,1,0:T(8,128)(2,1)S(1)}, bf16[2,128,384]{2,1,0:T(8,128)(2,1)S(1)}, u32[]{:S(2)}, u32[]{:S(2)}) collective-permute-start(bf16[2,128,384]{2,1,0:T(8,128)(2,1)S(1)} %bitcast.67), channel_id=1, source_target_pairs={{0,12},{1,13},{2,14},{3,15},{16,28},{17,29},{18,30},{19,31}} | collective-permute-start | bytes 589832 | tf_op jit(solution)/shard_map/ppermute | solution.py:665
  47.1 4.7 %student_attend.1 = (bf16[2,128,192]{2,1,0:T(8,128)(2,1)}, bf16[128,768]{1,0:T(8,128)(2,1)}, f32[128,768]{1,0:T(8,128)}) custom-call(s32[7]{0:T(128)} %concatenate.3.info, bf16[2,128,256]{2,1,0:T(8,128)(2,1)} %bitcast.68, bf16[192,384]{1,0:T(8,128)(2,1)} %own_ref.3, bf16[192,384]{1,0:T(8,128)(2,1)} %copy-done.17, bf16[2,128,384]{2,1,0:T(8,128)(2,1)} %bitcast.65, ...), custom_call_target="tpu_custom_call" | custom-call | flops 1 | bytes 1 | tf_op jit(solution)/shard_map/student_attend/pallas_call | solution.py:93
  62.7 5.4 %collective-permute-start.8 = (bf16[2,128,896]{2,1,0:T(8,128)(2,1)}, bf16[2,128,896]{2,1,0:T(8,128)(2,1)S(1)}, u32[]{:S(2)}, u32[]{:S(2)}) collective-permute-start(bf16[2,128,896]{2,1,0:T(8,128)(2,1)} %bitcast.70), channel_id=1, source_target_pairs={{0,12},{1,13},{2,14},{3,15},{16,28},{17,29},{18,30},{19,31}} | collective-permute-start | bytes 1376264 | tf_op jit(solution)/shard_map/ppermute | solution.py:665
  72.9 6.4 %collective-permute-done.8.refs_3_ = bf16[2,128,896]{2,1,0:T(8,128)(2,1)S(1)} collective-permute-done((bf16[2,128,896]{2,1,0:T(8,128)(2,1)}, bf16[2,128,896]{2,1,0:T(8,128)(2,1)S(1)}, u32[]{:S(2)}, u32[]{:S(2)}) %collective-permute-start.8) | collective-permute-done | bytes 458784 | tf_op jit(solution)/shard_map/ppermute | solution.py:665
  79.3 8.8 %collective-permute-done.9.refs_1_ = bf16[2,128,896]{2,1,0:T(8,128)(2,1)S(1)} collective-permute-done((bf16[2,128,896]{2,1,0:T(8,128)(2,1)}, bf16[2,128,896]{2,1,0:T(8,128)(2,1)S(1)}, u32[]{:S(2)}, u32[]{:S(2)}) %collective-permute-start.9) | collective-permute-done | bytes 458784 | tf_op jit(solution)/shard_map/ppermute | solution.py:665
  89.6 4.9 %student_ffn.1 = (f32[256,768]{1,0:T(8,128)}, bf16[256,768]{1,0:T(8,128)(2,1)}, bf16[256,768]{1,0:T(8,128)(2,1)}, bf16[256,768]{1,0:T(8,128)(2,1)}, bf16[128,768]{1,0:T(8,128)(2,1)}, /*index=5*/f32[128,768]{1,0:T(8,128)}) custom-call(s32[7]{0:T(128)} %concatenate.3.info, bf16[256,768]{1,0:T(8,128)(2,1)} %bitcast.54, bf16[768]{0:T(1024)(128)(2,1)} %out_bias.2, ...), custom_call_target="tpu_custom_call" | custom-call | flops 1 | bytes 1 | tf_op jit(solution)/shard_map/student_ffn/pallas_call | solution.py:93
  97.8 6.4 %collective-permute-done.17 = bf16[128,768]{1,0:T(8,128)(2,1)S(1)} collective-permute-done((bf16[128,768]{1,0:T(8,128)(2,1)S(1)}, bf16[128,768]{1,0:T(8,128)(2,1)S(1)}, u32[]{:S(2)}, u32[]{:S(2)}) %collective-permute-start.17) | collective-permute-done | bytes 196640 | tf_op jit(solution)/shard_map/ppermute | solution.py:649
  105.1 6.3 %teacher_attend.1 = (bf16[2,128,384]{2,1,0:T(8,128)(2,1)}, bf16[2,128,64]{2,1,0:T(8,128)(2,1)}) custom-call(s32[7]{0:T(128)} %concatenate.3.info, bf16[2,128,512]{2,1,0:T(8,128)(2,1)} %bitcast.74, bf16[2,128,896]{2,1,0:T(8,128)(2,1)} %bitcast.72, bf16[2,128,896]{2,1,0:T(8,128)(2,1)} %copy-done.19, bf16[2,128,896]{2,1,0:T(8,128)(2,1)} %copy-done.21, ...), custom_call_target="tpu_custom_call" | custom-call | flops 1 | bytes 1 | tf_op jit(solution)/shard_map/teacher_attend/pallas_call | solution.py:93
  111.4 5.1 %collective-permute-start.23 = (bf16[400,1600]{1,0:T(8,128)(2,1)}, bf16[400,1600]{1,0:T(8,128)(2,1)S(1)}, u32[]{:S(2)}, u32[]{:S(2)}) collective-permute-start(bf16[400,1600]{1,0:T(8,128)(2,1)} %collective-permute-done.21.down_near), channel_id=1, source_target_pairs={{0,4},{4,0},{8,12},{12,8},{1,5},{5,1},{9,13},{13,9},{2,6},{6,2},{1... | collective-permute-start | bytes 3840008 | tf_op jit(solution)/shard_map/ppermute | solution.py:649
  116.6 9.3 %all_gather.9.every = bf16[4,256,384]{2,1,0:T(8,128)(2,1)} all-gather(bf16[1,256,384]{2,1,0:T(8,128)(2,1)} %bitcast.78), channel_id=1, replica_groups=mesh['dp'=2,'ctx'=4,'tp'=4] {'tp'}, dimensions={0}, use_global_device_ids=true | all-gather | bytes 983040 | tf_op jit(solution)/shard_map/all_gather | solution.py:876
  126.5 7.7 %student_back.1 = (f32[256,768]{1,0:T(8,128)}, bf16[256,768]{1,0:T(8,128)(2,1)}, bf16[2,128,192]{2,1,0:T(8,128)(2,1)}, f32[3,768]{1,0:T(4,128)}, f32[2,128,384]{...) custom-call(s32[7]{0:T(128)} %concatenate.3.info, ...), custom_call_target="tpu_custom_call" | custom-call | flops 1 | bytes 1 | tf_op jit(solution)/shard_map/student_back/pallas_call | solution.py:93
  138.1 4.2 %student_ffn_grads.1 = (bf16[384,1536]{1,0:T(8,128)(2,1)}, f32[384,1536]{1,0:T(8,128)}, f32[2,768]{1,0:T(2,128)}) custom-call(s32[7]{0:T(128)} %concatenate.3.info, bf16[256,768]{1,0:T(8,128)(2,1)} %get-tuple-element.119.normed, bf16[256,768]{1,0:T(8,128)(2,1)} %get-tuple-element.120.act, bf16[256,768]{1,0:T(8,128)(2,1)} %get-tuple-element.121.d_upper, ...), custom_call_target="tpu_custom_call" | custom-call | flops 1 | bytes 1 | tf_op jit(solution)/shard_map/student_ffn_grads/pallas_call | solution.py:93
  142.3 4.2 %collective-permute-done.19.peer = bf16[800,512]{1,0:T(8,128)(2,1)S(1)} collective-permute-done((bf16[800,512]{1,0:T(8,128)(2,1)}, bf16[800,512]{1,0:T(8,128)(2,1)S(1)}, u32[]{:S(2)}, u32[]{:S(2)}) %collective-permute-start.19) | collective-permute-done | bytes 819232 | tf_op jit(solution)/shard_map/ppermute | solution.py:649
  147.4 3.9 %teacher_out.1 = (bf16[256,384]{1,0:T(8,128)(2,1)}, bf16[256,64]{1,0:T(8,128)(2,1)}) custom-call(s32[7]{0:T(128)} %concatenate.3.info, bf16[4,256,384]{2,1,0:T(8,128)(2,1)} %all_gather.9.every, bf16[256,64]{1,0:T(8,128)(2,1)} %bitcast.81, bf16[800,1600]{1,0:T(8,128)(2,1)} %w.1, bf16[800,512]{1,0:T(8,128)(2,1)} %copy-done.10), custom_call_target="tpu_custom_call" | custom-call | flops 1 | bytes 1 | tf_op jit(solution)/shard_map/teacher_out/pallas_call | solution.py:93
  151.3 8.3 %all-gather = bf16[1024,384]{1,0:T(8,128)(2,1)} all-gather(bf16[256,384]{1,0:T(8,128)(2,1)} %get-tuple-element.130), channel_id=2, replica_groups=mesh['dp'=2,'ctx'=4,'tp'=4] {'tp'}, dimensions={0}, use_global_device_ids=true | all-gather | bytes 983040 | tf_op jit(solution)/shard_map/all_gather | solution.py:941
  162.5 5.1 %student_in.1 = (bf16[128,1536]{1,0:T(8,128)(2,1)}, f32[128,1536]{1,0:T(8,128)}, bf16[384,768]{1,0:T(8,128)(2,1)}, f32[384,768]{1,0:T(8,128)}, f32[2,192]{1,0:T(2,128)}) custom-call(s32[7]{0:T(128)} %concatenate.3.info, bf16[256,192]{1,0:T(8,128)(2,1)} %bitcast.80, bf16[256,768]{1,0:T(8,128)(2,1)} %get-tuple-element.139.normed, ...), custom_call_target="tpu_custom_call" | custom-call | flops 1 | bytes 1 | tf_op jit(solution)/shard_map/student_in/pallas_call | solution.py:93
  182.8 17.0 %collective-permute-done.22.up_far = bf16[400,1600]{1,0:T(8,128)(2,1)S(1)} collective-permute-done((bf16[400,1600]{1,0:T(8,128)(2,1)S(1)}, bf16[400,1600]{1,0:T(8,128)(2,1)S(1)}, u32[]{:S(2)}, u32[]{:S(2)}) %collective-permute-start.22) | collective-permute-done | bytes 1280032 | tf_op jit(solution)/shard_map/ppermute | solution.py:649
  200.9 10.2 %teacher_ffn.1 = (f32[256,1600]{1,0:T(8,128)}, bf16[128,1664]{1,0:T(8,128)(2,1)}, f32[128,1664]{1,0:T(8,128)}) custom-call(s32[7]{0:T(128)} %concatenate.3.info, bf16[256,1600]{1,0:T(8,128)(2,1)} %bitcast.51, bf16[1600]{0:T(1024)(128)(2,1)} %out_bias.3, bf16[1600]{0:T(1024)(128)(2,1)} %gain.10, bf16[1600]{0:T(1024)(128)(2,1)} %shift.7, ...), custom_call_target="tpu_custom_call" | custom-call | flops 1 | bytes 1 | tf_op jit(solution)/shard_map/teacher_ffn/pallas_call | solution.py:93
  225.5 9.7 %collective-permute-start.39 = (bf16[96,768]{1,0:T(8,128)(2,1)S(1)}, bf16[96,768]{1,0:T(8,128)(2,1)S(1)}, u32[]{:S(2)}, u32[]{:S(2)}) collective-permute-start(bf16[96,768]{1,0:T(8,128)(2,1)S(1)} %slice.131), channel_id=1, source_target_pairs={{0,12},{4,8},{8,4},{12,0},{1,13},{5,9},{9,5},{13,1},{2,14},{6,10},... | collective-permute-start | bytes 442376 | tf_op jit(solution)/shard_map/ppermute | solution.py:649
  247.6 3.8 %collective-permute-done.36 = f32[8,768]{1,0:T(8,128)S(1)} collective-permute-done((f32[8,768]{1,0:T(8,128)S(1)}, f32[8,768]{1,0:T(8,128)S(1)}, u32[]{:S(2)}, u32[]{:S(2)}) %collective-permute-start.36) | collective-permute-done | bytes 24608 | tf_op jit(solution)/shard_map/ppermute | solution.py:649
  (170 shorter events, 100.2 us)
Async XLA Ops:
  9.4 19.9 %collective-permute-start.3 = (bf16[256,800]{1,0:T(8,128)(2,1)}, bf16[256,800]{1,0:T(8,128)(2,1)}, u32[]{:S(2)}, u32[]{:S(2)}) collective-permute-start(bf16[256,800]{1,0:T(8,128)(2,1)} %get-tuple-element.88), channel_id=1, source_target_pairs={{0,16},{16,0},{1,17},{17,1},{2,18},{18,2},{3,19},{19,3},{4,20},{20... | collective-permute-start | bytes 1228808 | tf_op jit(solution)/shard_map/ppermute | solution.py:649
  24.1 20.5 %collective-permute-start.4 = (bf16[384,768]{1,0:T(8,128)(2,1)}, bf16[384,768]{1,0:T(8,128)(2,1)}, u32[]{:S(2)}, u32[]{:S(2)}) collective-permute-start(bf16[384,768]{1,0:T(8,128)(2,1)} %up_own.2), channel_id=1, source_target_pairs={{0,16},{16,0},{1,17},{17,1},{2,18},{18,2},{3,19},{19,3},{4,20},{20... | collective-permute-start | bytes 1769480 | tf_op jit(solution)/shard_map/ppermute | solution.py:649
  37.1 18.9 %collective-permute-start.7 = (bf16[256,1408]{1,0:T(8,128)(2,1)}, bf16[256,1408]{1,0:T(8,128)(2,1)}, u32[]{:S(2)}, u32[]{:S(2)}) collective-permute-start(bf16[256,1408]{1,0:T(8,128)(2,1)} %get-tuple-element.96), channel_id=1, source_target_pairs={{0,16},{16,0},{1,17},{17,1},{2,18},{18,2},{3,19},{19,3},{4,20},{20... | collective-permute-start | bytes 2162696 | tf_op jit(solution)/shard_map/ppermute | solution.py:649
  51.8 17.7 %collective-permute-start.13 = (bf16[768,384]{1,0:T(8,128)(2,1)S(1)}, bf16[768,384]{1,0:T(8,128)(2,1)}, u32[]{:S(2)}, u32[]{:S(2)}) collective-permute-start(bf16[768,384]{1,0:T(8,128)(2,1)S(1)} %copy-done.2), channel_id=1, source_target_pairs={{0,16},{16,0},{1,17},{17,1},{2,18},{18,2},{3,19},{19,3},{4,20},{20... | collective-permute-start | bytes 1769480 | tf_op jit(solution)/shard_map/ppermute | solution.py:649
  62.7 16.6 %collective-permute-start.8 = (bf16[2,128,896]{2,1,0:T(8,128)(2,1)}, bf16[2,128,896]{2,1,0:T(8,128)(2,1)S(1)}, u32[]{:S(2)}, u32[]{:S(2)}) collective-permute-start(bf16[2,128,896]{2,1,0:T(8,128)(2,1)} %bitcast.70), channel_id=1, source_target_pairs={{0,12},{1,13},{2,14},{3,15},{16,28},{17,29},{18,30},{19,31}} | collective-permute-start | bytes 1376264 | tf_op jit(solution)/shard_map/ppermute | solution.py:665
  68.2 19.9 %collective-permute-start.9 = (bf16[2,128,896]{2,1,0:T(8,128)(2,1)}, bf16[2,128,896]{2,1,0:T(8,128)(2,1)S(1)}, u32[]{:S(2)}, u32[]{:S(2)}) collective-permute-start(bf16[2,128,896]{2,1,0:T(8,128)(2,1)} %bitcast.71), channel_id=1, source_target_pairs={{0,4},{4,8},{8,12},{1,5},{5,9},{9,13},{2,6},{6,10},{10,14},{3,7},{... | collective-permute-start | bytes 1376264 | tf_op jit(solution)/shard_map/ppermute | solution.py:665
  69.5 41.9 %collective-permute-start.21 = (bf16[400,1600]{1,0:T(8,128)(2,1)}, bf16[400,1600]{1,0:T(8,128)(2,1)}, u32[]{:S(2)}, u32[]{:S(2)}) collective-permute-start(bf16[400,1600]{1,0:T(8,128)(2,1)} %dynamic-slice_bitcast_fusion), channel_id=1, source_target_pairs={{0,16},{16,0},{1,17},{17,1},{2,18},{18,2},{3,19},{19,3},{4,20},{20... | collective-permute-start | bytes 3840008 | tf_op jit(solution)/shard_map/ppermute | solution.py:649
  70.7 17.4 %collective-permute-start.12 = (bf16[128,768]{1,0:T(8,128)(2,1)S(1)}, bf16[128,768]{1,0:T(8,128)(2,1)S(1)}, u32[]{:S(2)}, u32[]{:S(2)}) collective-permute-start(bf16[128,768]{1,0:T(8,128)(2,1)S(1)} %add_convert_fusion.6.r_ref), channel_id=1, source_target_pairs={{0,1},{1,0},{2,3},{3,2},{4,5},{5,4},{6,7},{7,6},{8,9},{9,8},{10,11... | collective-permute-start | bytes 589832 | tf_op jit(solution)/shard_map/ppermute | solution.py:649
  72.0 64.8 %collective-permute-start.14 = (bf16[400,1600]{1,0:T(8,128)(2,1)}, bf16[400,1600]{1,0:T(8,128)(2,1)S(1)}, u32[]{:S(2)}, u32[]{:S(2)}) collective-permute-start(bf16[400,1600]{1,0:T(8,128)(2,1)} %constant_dynamic-slice_fusion.1), channel_id=1, source_target_pairs={{0,16},{16,0},{1,17},{17,1},{2,18},{18,2},{3,19},{19,3},{4,20},{20... | collective-permute-start | bytes 3840008 | tf_op jit(solution)/shard_map/ppermute | solution.py:649
  94.5 52.0 %collective-permute-start.19 = (bf16[800,512]{1,0:T(8,128)(2,1)}, bf16[800,512]{1,0:T(8,128)(2,1)S(1)}, u32[]{:S(2)}, u32[]{:S(2)}) collective-permute-start(bf16[800,512]{1,0:T(8,128)(2,1)} %get-tuple-element.124), channel_id=1, source_target_pairs={{0,16},{16,0},{1,17},{17,1},{2,18},{18,2},{3,19},{19,3},{4,20},{20... | collective-permute-start | bytes 2457608 | tf_op jit(solution)/shard_map/ppermute | solution.py:649
  104.3 21.6 %collective-permute-start.18 = (bf16[128,768]{1,0:T(8,128)(2,1)S(1)}, bf16[128,768]{1,0:T(8,128)(2,1)S(1)}, u32[]{:S(2)}, u32[]{:S(2)}) collective-permute-start(bf16[128,768]{1,0:T(8,128)(2,1)S(1)} %add_convert_fusion.4.r_ref), channel_id=1, source_target_pairs={{0,1},{1,0},{2,3},{3,2},{4,5},{5,4},{6,7},{7,6},{8,9},{9,8},{10,11... | collective-permute-start | bytes 589832 | tf_op jit(solution)/shard_map/ppermute | solution.py:649
  111.4 62.0 %collective-permute-start.23 = (bf16[400,1600]{1,0:T(8,128)(2,1)}, bf16[400,1600]{1,0:T(8,128)(2,1)S(1)}, u32[]{:S(2)}, u32[]{:S(2)}) collective-permute-start(bf16[400,1600]{1,0:T(8,128)(2,1)} %collective-permute-done.21.down_near), channel_id=1, source_target_pairs={{0,4},{4,0},{8,12},{12,8},{1,5},{5,1},{9,13},{13,9},{2,6},{6,2},{1... | collective-permute-start | bytes 3840008 | tf_op jit(solution)/shard_map/ppermute | solution.py:649
  134.2 25.3 %collective-permute-start.28 = (bf16[2,128,384]{2,1,0:T(8,128)(2,1)}, bf16[2,128,384]{2,1,0:T(8,128)(2,1)S(1)}, u32[]{:S(2)}, u32[]{:S(2)}) collective-permute-start(bf16[2,128,384]{2,1,0:T(8,128)(2,1)} %get-tuple-element.142), channel_id=1, source_target_pairs={{4,0},{8,4},{12,8},{5,1},{9,5},{13,9},{6,2},{10,6},{14,10},{7,3},{... | collective-permute-start | bytes 589832 | tf_op jit(solution)/shard_map/ppermute | solution.py:906
  135.5 24.1 %collective-permute-start.29 = (bf16[2,128,384]{2,1,0:T(8,128)(2,1)}, bf16[2,128,384]{2,1,0:T(8,128)(2,1)S(1)}, u32[]{:S(2)}, u32[]{:S(2)}) collective-permute-start(bf16[2,128,384]{2,1,0:T(8,128)(2,1)} %get-tuple-element.143), channel_id=1, source_target_pairs={{8,0},{12,4},{9,1},{13,5},{10,2},{14,6},{11,3},{15,7},{24,16},{28,... | collective-permute-start | bytes 589832 | tf_op jit(solution)/shard_map/ppermute | solution.py:906
  136.8 25.0 %collective-permute-start.30 = (bf16[2,128,384]{2,1,0:T(8,128)(2,1)}, bf16[2,128,384]{2,1,0:T(8,128)(2,1)S(1)}, u32[]{:S(2)}, u32[]{:S(2)}) collective-permute-start(bf16[2,128,384]{2,1,0:T(8,128)(2,1)} %get-tuple-element.144), channel_id=1, source_target_pairs={{12,0},{13,1},{14,2},{15,3},{28,16},{29,17},{30,18},{31,19}} | collective-permute-start | bytes 589832 | tf_op jit(solution)/shard_map/ppermute | solution.py:906
  146.6 26.9 %collective-permute-start.20 = (bf16[384,1536]{1,0:T(8,128)(2,1)}, bf16[384,1536]{1,0:T(8,128)(2,1)}, u32[]{:S(2)}, u32[]{:S(2)}) collective-permute-start(bf16[384,1536]{1,0:T(8,128)(2,1)} %get-tuple-element.125), channel_id=1, source_target_pairs={{0,16},{16,0},{1,17},{17,1},{2,18},{18,2},{3,19},{19,3},{4,20},{20... | collective-permute-start | bytes 3538952 | tf_op jit(solution)/shard_map/ppermute | solution.py:649
  167.6 32.2 %collective-permute-start.22 = (bf16[400,1600]{1,0:T(8,128)(2,1)S(1)}, bf16[400,1600]{1,0:T(8,128)(2,1)S(1)}, u32[]{:S(2)}, u32[]{:S(2)}) collective-permute-start(bf16[400,1600]{1,0:T(8,128)(2,1)S(1)} %collective-permute-done.14.up_near), channel_id=1, source_target_pairs={{0,4},{4,0},{8,12},{12,8},{1,5},{5,1},{9,13},{13,9},{2,6},{6,2},{1... | collective-permute-start | bytes 3840008 | tf_op jit(solution)/shard_map/ppermute | solution.py:649
  177.7 34.2 %collective-permute-start.24 = (bf16[192,1536]{1,0:T(8,128)(2,1)}, bf16[192,1536]{1,0:T(8,128)(2,1)}, u32[]{:S(2)}, u32[]{:S(2)}) collective-permute-start(bf16[192,1536]{1,0:T(8,128)(2,1)} %slice.128), channel_id=1, source_target_pairs={{0,4},{4,0},{8,12},{12,8},{1,5},{5,1},{9,13},{13,9},{2,6},{6,2},{1... | collective-permute-start | bytes 1769480 | tf_op jit(solution)/shard_map/ppermute | solution.py:649
  178.3 34.9 %collective-permute-start.37 = (bf16[384,768]{1,0:T(8,128)(2,1)}, bf16[384,768]{1,0:T(8,128)(2,1)}, u32[]{:S(2)}, u32[]{:S(2)}) collective-permute-start(bf16[384,768]{1,0:T(8,128)(2,1)} %get-tuple-element.158), channel_id=1, source_target_pairs={{0,16},{16,0},{1,17},{17,1},{2,18},{18,2},{3,19},{19,3},{4,20},{20... | collective-permute-start | bytes 1769480 | tf_op jit(solution)/shard_map/ppermute | solution.py:649
  182.8 36.8 %collective-permute-start.33 = (bf16[128,1536]{1,0:T(8,128)(2,1)}, bf16[128,1536]{1,0:T(8,128)(2,1)}, u32[]{:S(2)}, u32[]{:S(2)}) collective-permute-start(bf16[128,1536]{1,0:T(8,128)(2,1)} %add_convert_fusion.2.r_ref), channel_id=1, source_target_pairs={{0,1},{1,0},{2,3},{3,2},{4,5},{5,4},{6,7},{7,6},{8,9},{9,8},{10,11... | collective-permute-start | bytes 1179656 | tf_op jit(solution)/shard_map/ppermute | solution.py:649
  216.0 19.2 %collective-permute-start.40 = (bf16[96,1536]{1,0:T(8,128)(2,1)S(1)}, bf16[96,1536]{1,0:T(8,128)(2,1)}, u32[]{:S(2)}, u32[]{:S(2)}) collective-permute-start(bf16[96,1536]{1,0:T(8,128)(2,1)S(1)} %slice.129), channel_id=1, source_target_pairs={{0,12},{4,8},{8,4},{12,0},{1,13},{5,9},{9,5},{13,1},{2,14},{6,10},... | collective-permute-start | bytes 884744 | tf_op jit(solution)/shard_map/ppermute | solution.py:649
  219.1 18.0 %collective-permute-start.26 = (bf16[128,1664]{1,0:T(8,128)(2,1)S(1)}, bf16[128,1664]{1,0:T(8,128)(2,1)S(1)}, u32[]{:S(2)}, u32[]{:S(2)}) collective-permute-start(bf16[128,1664]{1,0:T(8,128)(2,1)S(1)} %add_convert_fusion.1), channel_id=1, source_target_pairs={{0,2},{1,3},{2,0},{3,1},{4,6},{5,7},{6,4},{7,5},{8,10},{9,11},{10,... | collective-permute-start | bytes 1277960 | tf_op jit(solution)/shard_map/ppermute | solution.py:649
  225.5 14.6 %collective-permute-start.39 = (bf16[96,768]{1,0:T(8,128)(2,1)S(1)}, bf16[96,768]{1,0:T(8,128)(2,1)S(1)}, u32[]{:S(2)}, u32[]{:S(2)}) collective-permute-start(bf16[96,768]{1,0:T(8,128)(2,1)S(1)} %slice.131), channel_id=1, source_target_pairs={{0,12},{4,8},{8,4},{12,0},{1,13},{5,9},{9,5},{13,1},{2,14},{6,10},... | collective-permute-start | bytes 442376 | tf_op jit(solution)/shard_map/ppermute | solution.py:649
  237.2 16.1 %collective-permute-start.27 = (bf16[128,1664]{1,0:T(8,128)(2,1)S(1)}, bf16[128,1664]{1,0:T(8,128)(2,1)S(1)}, u32[]{:S(2)}, u32[]{:S(2)}) collective-permute-start(bf16[128,1664]{1,0:T(8,128)(2,1)S(1)} %add_convert_fusion.r_ref), channel_id=1, source_target_pairs={{0,1},{1,0},{2,3},{3,2},{4,5},{5,4},{6,7},{7,6},{8,9},{9,8},{10,11... | collective-permute-start | bytes 1277960 | tf_op jit(solution)/shard_map/ppermute | solution.py:649
  (47 other events, 334.0 us)

commit v3 on v1

--- a/solution.py
+++ b/solution.py
@@ -912,7 +912,7 @@
         up_near = after(up_near, d_q)
         up_far = swap(up_near, "ctx", n_ctx, 1)
         down_near = half_of(t_down_t, peer_up, peer_down)
-        b_normed = after(b_normed, up_near, down_near, d_q)
+        b_normed = after(b_normed, up_near, d_q)
 
         g_give, g_keep, sums_f = run(
             functools.partial(student_ffn_grads_kernel, n_ctx),
@@ -926,9 +926,9 @@
             scratch=[pltpu.VMEM((narrow, 2 * hidden), F32)],
             flops=4 * total * narrow * hidden,
         )
-        down_far = swap(after(down_near, *gots), "ctx", n_ctx, 1)
+        down_far = swap(down_near, "ctx", n_ctx, 1)
         w_out_peer = swap(after(w_out_give, peer_up, peer_down), "dp", n_dp, 1)
-        every = after(every, g_give, up_far, *gots)
+        every = after(every, g_give, down_near)
         pieces = [up_near, up_far, down_near, down_far]
         o_cols, o_tail = run(
             teacher_out_kernel,
@@ -974,7 +974,7 @@
         g_got = swap(after(g_give, w_out_peer), "dp", n_dp, 1)
         ga_got = swap(after(ga_give, w_out_peer), "dp", n_dp, 1)
         g_near = halve(g_keep + after(g_got, down_far).astype(F32), 1)
-        d_mid = after(d_mid, g_got, down_far)
+        d_mid = after(d_mid, g_got)
         in_grad, s_result, sums = run(
             student_last_kernel,
             "student_last",
@@ -1003,7 +1003,7 @@
             [((total, wide), F32), ((rows, packed), BF), ((rows, packed), F32)],
             [
                 info,
-                after(t_x, g_got, ga_got, sums),
+                after(t_x, g_got, in_grad),
                 teacher_out_bias,
                 teacher_gain_b,
                 teacher_shift_b,
@@ -1024,10 +1024,13 @@
             ],
             flops=4 * total * wide * t_hidden,
         )
-        r4, other4 = tp_sum(f_give, after(f_keep, g_near))
-        g_ffn = over_rings(halve(g_near, 3))
-        ga_got = after(ga_got, f_give)
-        g_att = over_rings(halve(halve(ga_keep + ga_got.astype(F32), 1), 3))
+        part = (after(f_keep, g_near) + swap(f_give, "tp", n_tp, 1).astype(F32)).astype(BF)
+        r4 = (part.astype(F32) + swap(part, "tp", n_tp, 2).astype(F32)).astype(BF)
+        other4 = swap(r4, "tp", n_tp, 1)
+        g_ffn = over_rings(halve(after(g_near, part), 3))
+        ga_got = after(ga_got, part)
+        ga_near = halve(ga_keep + ga_got.astype(F32), 1)
+        g_att = over_rings(halve(after(ga_near, r4), 3))
         t_result = run(
             last_kernel,
             "last",
@@ -1035,7 +1038,7 @@
             [info, t_mid, teacher_down_bias, r4, other4],
         )[0]
 
-        small = small_sum(after(sums, f_give))
+        small = small_sum(after(sums, other4))
         piece = narrow // (n_dp * n_ctx)
         shards = lax.dynamic_slice_in_dim(small, (dp * n_ctx + ctx) * piece, piece, axis=1)
 

time: 285 us -> 255 us (0.89)
  waiting for transfers between devices: 114 us -> 84.1 us
    ppermute x3, waiting for transfers between devices: 45.1 us -> 2.41 us  [body(): lax.ppermute(d_parts[k], 'ctx', [(i + k, i) for i in range(n_ctx - k)])]
    ppermute x32, waiting for transfers between devices: 48.1 us -> 64.7 us  [swap(): return lax.ppermute(x, axis, [(i, i ^ bit) for i in range(size)])]
    ppermute x4, waiting for transfers between devices: 20.7 us -> 17 us  [gather_keys(): out.append(lax.ppermute(kv, 'ctx', [(i, i + k) for i in range(n_ctx - k)]))]
    unnamed x81 -> x63, local copies, waits for them, and re-layouts: 13.1 us -> 11.7 us
  transfers between devices with their start and end apart: 41 -> 41, of which waited for: 18 -> 20; matrix products, arithmetic and copies ran while one was open for 5% -> 7% of each run, Pallas kernels for 22% -> 28%
where the time goes in v3:
time: 255 us; the launch traced here: 254 us
  waiting for transfers between devices  84.1 us (33%)
  Pallas kernels  69.8 us (27%)
  starting transfers between devices  54.3 us (21%)
  local copies, waits for them, and re-layouts  17.8 us (7%)
  blocking collectives  17.5 us (7%)
  other arithmetic  8.86 us (3%)
    pallas_call x14, Pallas kernels, run(): pl.pallas_call(kernel, out_shape=out_shape, in_specs=specs, out_specs=[VM...  69.8 us
    ppermute x32, waiting for transfers between devices, swap(): return lax.ppermute(x, axis, [(i, i ^ bit) for i in range(size)])  64.7 us
    ppermute x32, starting transfers between devices, swap(): return lax.ppermute(x, axis, [(i, i ^ bit) for i in range(size)])  33 us
    ppermute x4, waiting for transfers between devices, gather_keys(): out.append(lax.ppermute(kv, 'ctx', [(i, i + k) for i in range(n_ctx - k)]))  17 us
    ppermute x4, starting transfers between devices, gather_keys(): out.append(lax.ppermute(kv, 'ctx', [(i, i + k) for i in range(n_ctx - k)]))  15.5 us
    unnamed x63, local copies, waits for them, and re-layouts  11.7 us
    all_gather x1, blocking collectives, body(): every = lax.all_gather(t_att.reshape(total, cols), 'tp', axis=0)  9.28 us
    all_gather x1, blocking collectives, body(): o_every = lax.all_gather(o_cols, 'tp', axis=0)  8.26 us
  transfers between devices with their start and end apart: 41, of which 20 were waited for; matrix products, arithmetic and copies ran while one was open for 7% of the time, Pallas kernels for 28%

profile of v3, /device:TPU:0, one launch (start us, length us, event | category | flops | bytes accessed | tf_op | source)
XLA Modules:
  0.0 253.6 jit_solution(16866211418734362629)
XLA Ops:
  9.5 5.4 %collective-permute-done.peer = bf16[3,192,384]{2,1,0:T(8,128)(2,1)S(1)} collective-permute-done((bf16[3,192,384]{2,1,0:T(8,128)(2,1)}, bf16[3,192,384]{2,1,0:T(8,128)(2,1)S(1)}, u32[]{:S(2)}, u32[]{:S(2)}) %collective-permute-start) | collective-permute-done | bytes 442400 | tf_op jit(solution)/shard_map/ppermute | solution.py:649
  18.6 4.0 %collective-permute-start.1 = (bf16[2,128,384]{2,1,0:T(8,128)(2,1)}, bf16[2,128,384]{2,1,0:T(8,128)(2,1)S(1)}, u32[]{:S(2)}, u32[]{:S(2)}) collective-permute-start(bf16[2,128,384]{2,1,0:T(8,128)(2,1)} %bitcast.64), channel_id=1, source_target_pairs={{0,4},{4,8},{8,12},{1,5},{5,9},{9,13},{2,6},{6,10},{10,14},{3,7},{... | collective-permute-start | bytes 589832 | tf_op jit(solution)/shard_map/ppermute | solution.py:665
  24.7 4.7 %collective-permute-done.2.peer_ref = bf16[192,384]{1,0:T(8,128)(2,1)S(1)} collective-permute-done((bf16[192,384]{1,0:T(8,128)(2,1)S(1)}, bf16[192,384]{1,0:T(8,128)(2,1)S(1)}, u32[]{:S(2)}, u32[]{:S(2)}) %collective-permute-start.2) | collective-permute-done | bytes 147488 | tf_op jit(solution)/shard_map/ppermute | solution.py:649
  29.4 7.7 %teacher_qkv.1 = (bf16[256,1408]{1,0:T(8,128)(2,1)}, f32[256,1408]{1,0:T(8,128)}, bf16[800,512]{1,0:T(8,128)(2,1)}) custom-call(s32[7]{0:T(128)} %concatenate.3.info, bf16[256,800]{1,0:T(8,128)(2,1)} %get-tuple-element.94.mine, bf16[256,800]{1,0:T(8,128)(2,1)} %collective-permute-done.3.other, bf16[3,800,1600]{2,1,0:T(8,128)(2,1)} %w_hbm.1, bf16[800,1600]{1,0:T(8,128)(2,1)} %w.1), custom_call_target="tpu_custom_call" | custom-call | flops 1 | bytes 1 | tf_op jit(solution)/shard_map/teacher_qkv/pallas_call | solution.py:93
  38.7 4.6 %collective-permute-start.6 = (bf16[2,128,384]{2,1,0:T(8,128)(2,1)S(1)}, bf16[2,128,384]{2,1,0:T(8,128)(2,1)S(1)}, u32[]{:S(2)}, u32[]{:S(2)}) collective-permute-start(bf16[2,128,384]{2,1,0:T(8,128)(2,1)S(1)} %bitcast.67), channel_id=1, source_target_pairs={{0,12},{1,13},{2,14},{3,15},{16,28},{17,29},{18,30},{19,31}} | collective-permute-start | bytes 589832 | tf_op jit(solution)/shard_map/ppermute | solution.py:665
  47.1 4.7 %student_attend.1 = (bf16[2,128,192]{2,1,0:T(8,128)(2,1)}, bf16[128,768]{1,0:T(8,128)(2,1)}, f32[128,768]{1,0:T(8,128)}) custom-call(s32[7]{0:T(128)} %concatenate.3.info, bf16[2,128,256]{2,1,0:T(8,128)(2,1)} %bitcast.68, bf16[192,384]{1,0:T(8,128)(2,1)} %own_ref.3, bf16[192,384]{1,0:T(8,128)(2,1)} %copy-done.16, bf16[2,128,384]{2,1,0:T(8,128)(2,1)} %bitcast.65, ...), custom_call_target="tpu_custom_call" | custom-call | flops 1 | bytes 1 | tf_op jit(solution)/shard_map/student_attend/pallas_call | solution.py:93
  62.6 5.6 %collective-permute-start.8 = (bf16[2,128,896]{2,1,0:T(8,128)(2,1)}, bf16[2,128,896]{2,1,0:T(8,128)(2,1)S(1)}, u32[]{:S(2)}, u32[]{:S(2)}) collective-permute-start(bf16[2,128,896]{2,1,0:T(8,128)(2,1)} %bitcast.70), channel_id=1, source_target_pairs={{0,12},{1,13},{2,14},{3,15},{16,28},{17,29},{18,30},{19,31}} | collective-permute-start | bytes 1376264 | tf_op jit(solution)/shard_map/ppermute | solution.py:665
  73.0 6.4 %collective-permute-done.8.refs_3_ = bf16[2,128,896]{2,1,0:T(8,128)(2,1)S(1)} collective-permute-done((bf16[2,128,896]{2,1,0:T(8,128)(2,1)}, bf16[2,128,896]{2,1,0:T(8,128)(2,1)S(1)}, u32[]{:S(2)}, u32[]{:S(2)}) %collective-permute-start.8) | collective-permute-done | bytes 458784 | tf_op jit(solution)/shard_map/ppermute | solution.py:665
  79.4 8.8 %collective-permute-done.9.refs_1_ = bf16[2,128,896]{2,1,0:T(8,128)(2,1)S(1)} collective-permute-done((bf16[2,128,896]{2,1,0:T(8,128)(2,1)}, bf16[2,128,896]{2,1,0:T(8,128)(2,1)S(1)}, u32[]{:S(2)}, u32[]{:S(2)}) %collective-permute-start.9) | collective-permute-done | bytes 458784 | tf_op jit(solution)/shard_map/ppermute | solution.py:665
  89.6 5.0 %student_ffn.1 = (f32[256,768]{1,0:T(8,128)}, bf16[256,768]{1,0:T(8,128)(2,1)}, bf16[256,768]{1,0:T(8,128)(2,1)}, bf16[256,768]{1,0:T(8,128)(2,1)}, bf16[128,768]{1,0:T(8,128)(2,1)}, /*index=5*/f32[128,768]{1,0:T(8,128)}) custom-call(s32[7]{0:T(128)} %concatenate.3.info, bf16[256,768]{1,0:T(8,128)(2,1)} %bitcast.54, bf16[768]{0:T(1024)(128)(2,1)} %out_bias.2, ...), custom_call_target="tpu_custom_call" | custom-call | flops 1 | bytes 1 | tf_op jit(solution)/shard_map/student_ffn/pallas_call | solution.py:93
  97.9 6.4 %collective-permute-done.17 = bf16[128,768]{1,0:T(8,128)(2,1)S(1)} collective-permute-done((bf16[128,768]{1,0:T(8,128)(2,1)S(1)}, bf16[128,768]{1,0:T(8,128)(2,1)S(1)}, u32[]{:S(2)}, u32[]{:S(2)}) %collective-permute-start.17) | collective-permute-done | bytes 196640 | tf_op jit(solution)/shard_map/ppermute | solution.py:649
  105.2 6.3 %teacher_attend.1 = (bf16[2,128,384]{2,1,0:T(8,128)(2,1)}, bf16[2,128,64]{2,1,0:T(8,128)(2,1)}) custom-call(s32[7]{0:T(128)} %concatenate.3.info, bf16[2,128,512]{2,1,0:T(8,128)(2,1)} %bitcast.74, bf16[2,128,896]{2,1,0:T(8,128)(2,1)} %bitcast.72, bf16[2,128,896]{2,1,0:T(8,128)(2,1)} %copy-done.18, bf16[2,128,896]{2,1,0:T(8,128)(2,1)} %copy-done.20, ...), custom_call_target="tpu_custom_call" | custom-call | flops 1 | bytes 1 | tf_op jit(solution)/shard_map/teacher_attend/pallas_call | solution.py:93
  111.5 5.1 %collective-permute-start.29 = (bf16[400,1600]{1,0:T(8,128)(2,1)}, bf16[400,1600]{1,0:T(8,128)(2,1)S(1)}, u32[]{:S(2)}, u32[]{:S(2)}) collective-permute-start(bf16[400,1600]{1,0:T(8,128)(2,1)} %collective-permute-done.21.down_near), channel_id=1, source_target_pairs={{0,4},{4,0},{8,12},{12,8},{1,5},{5,1},{9,13},{13,9},{2,6},{6,2},{1... | collective-permute-start | bytes 3840008 | tf_op jit(solution)/shard_map/ppermute | solution.py:649
  116.7 9.3 %all_gather.9.every = bf16[4,256,384]{2,1,0:T(8,128)(2,1)} all-gather(bf16[1,256,384]{2,1,0:T(8,128)(2,1)} %bitcast.78), channel_id=1, replica_groups=mesh['dp'=2,'ctx'=4,'tp'=4] {'tp'}, dimensions={0}, use_global_device_ids=true | all-gather | bytes 983040 | tf_op jit(solution)/shard_map/all_gather | solution.py:876
  126.6 7.7 %student_back.1 = (f32[256,768]{1,0:T(8,128)}, bf16[256,768]{1,0:T(8,128)(2,1)}, bf16[2,128,192]{2,1,0:T(8,128)(2,1)}, f32[3,768]{1,0:T(4,128)}, f32[2,128,384]{...) custom-call(s32[7]{0:T(128)} %concatenate.3.info, ...), custom_call_target="tpu_custom_call" | custom-call | flops 1 | bytes 1 | tf_op jit(solution)/shard_map/student_back/pallas_call | solution.py:93
  138.2 4.3 %student_ffn_grads.1 = (bf16[384,1536]{1,0:T(8,128)(2,1)}, f32[384,1536]{1,0:T(8,128)}, f32[2,768]{1,0:T(2,128)}) custom-call(s32[7]{0:T(128)} %concatenate.3.info, bf16[256,768]{1,0:T(8,128)(2,1)} %get-tuple-element.120.normed, bf16[256,768]{1,0:T(8,128)(2,1)} %get-tuple-element.121.act, bf16[256,768]{1,0:T(8,128)(2,1)} %get-tuple-element.122.d_upper, ...), custom_call_target="tpu_custom_call" | custom-call | flops 1 | bytes 1 | tf_op jit(solution)/shard_map/student_ffn_grads/pallas_call | solution.py:93
  142.5 4.1 %collective-permute-done.19.peer = bf16[800,512]{1,0:T(8,128)(2,1)S(1)} collective-permute-done((bf16[800,512]{1,0:T(8,128)(2,1)S(1)}, bf16[800,512]{1,0:T(8,128)(2,1)S(1)}, u32[]{:S(2)}, u32[]{:S(2)}) %collective-permute-start.19) | collective-permute-done | bytes 819232 | tf_op jit(solution)/shard_map/ppermute | solution.py:649
  151.3 8.3 %all-gather = bf16[1024,384]{1,0:T(8,128)(2,1)} all-gather(bf16[256,384]{1,0:T(8,128)(2,1)} %get-tuple-element.131), channel_id=2, replica_groups=mesh['dp'=2,'ctx'=4,'tp'=4] {'tp'}, dimensions={0}, use_global_device_ids=true | all-gather | bytes 983040 | tf_op jit(solution)/shard_map/all_gather | solution.py:941
  162.7 5.1 %student_in.1 = (bf16[128,1536]{1,0:T(8,128)(2,1)}, f32[128,1536]{1,0:T(8,128)}, bf16[384,768]{1,0:T(8,128)(2,1)}, f32[384,768]{1,0:T(8,128)}, f32[2,192]{1,0:T(2,128)}) custom-call(s32[7]{0:T(128)} %concatenate.3.info, bf16[256,192]{1,0:T(8,128)(2,1)} %bitcast.80, bf16[256,768]{1,0:T(8,128)(2,1)} %get-tuple-element.132.normed, ...), custom_call_target="tpu_custom_call" | custom-call | flops 1 | bytes 1 | tf_op jit(solution)/shard_map/student_in/pallas_call | solution.py:93
  177.3 4.8 %collective-permute-done.26 = bf16[128,1536]{1,0:T(8,128)(2,1)S(1)} collective-permute-done((bf16[128,1536]{1,0:T(8,128)(2,1)S(1)}, bf16[128,1536]{1,0:T(8,128)(2,1)S(1)}, u32[]{:S(2)}, u32[]{:S(2)}) %collective-permute-start.26) | collective-permute-done | bytes 393248 | tf_op jit(solution)/shard_map/ppermute | solution.py:649
  187.7 12.5 %collective-permute-done.28.up_far = bf16[400,1600]{1,0:T(8,128)(2,1)} collective-permute-done((bf16[400,1600]{1,0:T(8,128)(2,1)}, bf16[400,1600]{1,0:T(8,128)(2,1)}, u32[]{:S(2)}, u32[]{:S(2)}) %collective-permute-start.28) | collective-permute-done | bytes 1280032 | tf_op jit(solution)/shard_map/ppermute | solution.py:649
  200.2 10.2 %teacher_ffn.1 = (f32[256,1600]{1,0:T(8,128)}, bf16[128,1664]{1,0:T(8,128)(2,1)}, f32[128,1664]{1,0:T(8,128)}) custom-call(s32[7]{0:T(128)} %concatenate.3.info, bf16[256,1600]{1,0:T(8,128)(2,1)} %bitcast.51, bf16[1600]{0:T(1024)(128)(2,1)} %out_bias.3, bf16[1600]{0:T(1024)(128)(2,1)} %gain.11, bf16[1600]{0:T(1024)(128)(2,1)} %shift.7, ...), custom_call_target="tpu_custom_call" | custom-call | flops 1 | bytes 1 | tf_op jit(solution)/shard_map/teacher_ffn/pallas_call | solution.py:93
  218.5 7.5 %collective-permute-done.40 = bf16[96,1536]{1,0:T(8,128)(2,1)S(1)} collective-permute-done((bf16[96,1536]{1,0:T(8,128)(2,1)S(1)}, bf16[96,1536]{1,0:T(8,128)(2,1)S(1)}, u32[]{:S(2)}, u32[]{:S(2)}) %collective-permute-start.40) | collective-permute-done | bytes 294944 | tf_op jit(solution)/shard_map/ppermute | solution.py:649
  226.3 4.4 %collective-permute-done.38 = bf16[192,768]{1,0:T(8,128)(2,1)S(1)} collective-permute-done((bf16[192,768]{1,0:T(8,128)(2,1)S(1)}, bf16[192,768]{1,0:T(8,128)(2,1)S(1)}, u32[]{:S(2)}, u32[]{:S(2)}) %collective-permute-start.38) | collective-permute-done | bytes 294944 | tf_op jit(solution)/shard_map/ppermute | solution.py:649
  (170 shorter events, 99.6 us)
Async XLA Ops:
  0.7 14.3 %collective-permute-start = (bf16[3,192,384]{2,1,0:T(8,128)(2,1)}, bf16[3,192,384]{2,1,0:T(8,128)(2,1)S(1)}, u32[]{:S(2)}, u32[]{:S(2)}) collective-permute-start(bf16[3,192,384]{2,1,0:T(8,128)(2,1)} %bitcast.61), channel_id=1, source_target_pairs={{0,16},{16,0},{1,17},{17,1},{2,18},{18,2},{3,19},{19,3},{4,20},{20... | collective-permute-start | bytes 1327112 | tf_op jit(solution)/shard_map/ppermute | solution.py:649
  9.4 19.9 %collective-permute-start.3 = (bf16[256,800]{1,0:T(8,128)(2,1)}, bf16[256,800]{1,0:T(8,128)(2,1)}, u32[]{:S(2)}, u32[]{:S(2)}) collective-permute-start(bf16[256,800]{1,0:T(8,128)(2,1)} %get-tuple-element.89), channel_id=1, source_target_pairs={{0,16},{16,0},{1,17},{17,1},{2,18},{18,2},{3,19},{19,3},{4,20},{20... | collective-permute-start | bytes 1228808 | tf_op jit(solution)/shard_map/ppermute | solution.py:649
  24.1 20.5 %collective-permute-start.4 = (bf16[384,768]{1,0:T(8,128)(2,1)}, bf16[384,768]{1,0:T(8,128)(2,1)}, u32[]{:S(2)}, u32[]{:S(2)}) collective-permute-start(bf16[384,768]{1,0:T(8,128)(2,1)} %up_own.2), channel_id=1, source_target_pairs={{0,16},{16,0},{1,17},{17,1},{2,18},{18,2},{3,19},{19,3},{4,20},{20... | collective-permute-start | bytes 1769480 | tf_op jit(solution)/shard_map/ppermute | solution.py:649
  37.1 18.8 %collective-permute-start.7 = (bf16[256,1408]{1,0:T(8,128)(2,1)}, bf16[256,1408]{1,0:T(8,128)(2,1)}, u32[]{:S(2)}, u32[]{:S(2)}) collective-permute-start(bf16[256,1408]{1,0:T(8,128)(2,1)} %get-tuple-element.97), channel_id=1, source_target_pairs={{0,16},{16,0},{1,17},{17,1},{2,18},{18,2},{3,19},{19,3},{4,20},{20... | collective-permute-start | bytes 2162696 | tf_op jit(solution)/shard_map/ppermute | solution.py:649
  51.8 17.7 %collective-permute-start.13 = (bf16[768,384]{1,0:T(8,128)(2,1)S(1)}, bf16[768,384]{1,0:T(8,128)(2,1)}, u32[]{:S(2)}, u32[]{:S(2)}) collective-permute-start(bf16[768,384]{1,0:T(8,128)(2,1)S(1)} %copy-done.2), channel_id=1, source_target_pairs={{0,16},{16,0},{1,17},{17,1},{2,18},{18,2},{3,19},{19,3},{4,20},{20... | collective-permute-start | bytes 1769480 | tf_op jit(solution)/shard_map/ppermute | solution.py:649
  57.0 13.7 %collective-permute-start.11 = (bf16[128,768]{1,0:T(8,128)(2,1)S(1)}, bf16[128,768]{1,0:T(8,128)(2,1)S(1)}, u32[]{:S(2)}, u32[]{:S(2)}) collective-permute-start(bf16[128,768]{1,0:T(8,128)(2,1)S(1)} %add_convert_fusion.7), channel_id=1, source_target_pairs={{0,2},{1,3},{2,0},{3,1},{4,6},{5,7},{6,4},{7,5},{8,10},{9,11},{10,... | collective-permute-start | bytes 589832 | tf_op jit(solution)/shard_map/ppermute | solution.py:649
  62.6 16.8 %collective-permute-start.8 = (bf16[2,128,896]{2,1,0:T(8,128)(2,1)}, bf16[2,128,896]{2,1,0:T(8,128)(2,1)S(1)}, u32[]{:S(2)}, u32[]{:S(2)}) collective-permute-start(bf16[2,128,896]{2,1,0:T(8,128)(2,1)} %bitcast.70), channel_id=1, source_target_pairs={{0,12},{1,13},{2,14},{3,15},{16,28},{17,29},{18,30},{19,31}} | collective-permute-start | bytes 1376264 | tf_op jit(solution)/shard_map/ppermute | solution.py:665
  68.2 19.9 %collective-permute-start.9 = (bf16[2,128,896]{2,1,0:T(8,128)(2,1)}, bf16[2,128,896]{2,1,0:T(8,128)(2,1)S(1)}, u32[]{:S(2)}, u32[]{:S(2)}) collective-permute-start(bf16[2,128,896]{2,1,0:T(8,128)(2,1)} %bitcast.71), channel_id=1, source_target_pairs={{0,4},{4,8},{8,12},{1,5},{5,9},{9,13},{2,6},{6,10},{10,14},{3,7},{... | collective-permute-start | bytes 1376264 | tf_op jit(solution)/shard_map/ppermute | solution.py:665
  69.5 42.0 %collective-permute-start.21 = (bf16[400,1600]{1,0:T(8,128)(2,1)}, bf16[400,1600]{1,0:T(8,128)(2,1)}, u32[]{:S(2)}, u32[]{:S(2)}) collective-permute-start(bf16[400,1600]{1,0:T(8,128)(2,1)} %dynamic-slice_bitcast_fusion), channel_id=1, source_target_pairs={{0,16},{16,0},{1,17},{17,1},{2,18},{18,2},{3,19},{19,3},{4,20},{20... | collective-permute-start | bytes 3840008 | tf_op jit(solution)/shard_map/ppermute | solution.py:649
  70.7 17.5 %collective-permute-start.12 = (bf16[128,768]{1,0:T(8,128)(2,1)S(1)}, bf16[128,768]{1,0:T(8,128)(2,1)S(1)}, u32[]{:S(2)}, u32[]{:S(2)}) collective-permute-start(bf16[128,768]{1,0:T(8,128)(2,1)S(1)} %add_convert_fusion.6.r_ref), channel_id=1, source_target_pairs={{0,1},{1,0},{2,3},{3,2},{4,5},{5,4},{6,7},{7,6},{8,9},{9,8},{10,11... | collective-permute-start | bytes 589832 | tf_op jit(solution)/shard_map/ppermute | solution.py:649
  72.0 64.9 %collective-permute-start.14 = (bf16[400,1600]{1,0:T(8,128)(2,1)}, bf16[400,1600]{1,0:T(8,128)(2,1)}, u32[]{:S(2)}, u32[]{:S(2)}) collective-permute-start(bf16[400,1600]{1,0:T(8,128)(2,1)} %constant_dynamic-slice_fusion.1), channel_id=1, source_target_pairs={{0,16},{16,0},{1,17},{17,1},{2,18},{18,2},{3,19},{19,3},{4,20},{20... | collective-permute-start | bytes 3840008 | tf_op jit(solution)/shard_map/ppermute | solution.py:649
  94.6 52.0 %collective-permute-start.19 = (bf16[800,512]{1,0:T(8,128)(2,1)S(1)}, bf16[800,512]{1,0:T(8,128)(2,1)S(1)}, u32[]{:S(2)}, u32[]{:S(2)}) collective-permute-start(bf16[800,512]{1,0:T(8,128)(2,1)S(1)} %copy-done.28), channel_id=1, source_target_pairs={{0,16},{16,0},{1,17},{17,1},{2,18},{18,2},{3,19},{19,3},{4,20},{20... | collective-permute-start | bytes 2457608 | tf_op jit(solution)/shard_map/ppermute | solution.py:649
  104.4 21.6 %collective-permute-start.18 = (bf16[128,768]{1,0:T(8,128)(2,1)S(1)}, bf16[128,768]{1,0:T(8,128)(2,1)S(1)}, u32[]{:S(2)}, u32[]{:S(2)}) collective-permute-start(bf16[128,768]{1,0:T(8,128)(2,1)S(1)} %add_convert_fusion.4.r_ref), channel_id=1, source_target_pairs={{0,1},{1,0},{2,3},{3,2},{4,5},{5,4},{6,7},{7,6},{8,9},{9,8},{10,11... | collective-permute-start | bytes 589832 | tf_op jit(solution)/shard_map/ppermute | solution.py:649
  111.5 61.9 %collective-permute-start.29 = (bf16[400,1600]{1,0:T(8,128)(2,1)}, bf16[400,1600]{1,0:T(8,128)(2,1)S(1)}, u32[]{:S(2)}, u32[]{:S(2)}) collective-permute-start(bf16[400,1600]{1,0:T(8,128)(2,1)} %collective-permute-done.21.down_near), channel_id=1, source_target_pairs={{0,4},{4,0},{8,12},{12,8},{1,5},{5,1},{9,13},{13,9},{2,6},{6,2},{1... | collective-permute-start | bytes 3840008 | tf_op jit(solution)/shard_map/ppermute | solution.py:649
  134.3 25.3 %collective-permute-start.22 = (bf16[2,128,384]{2,1,0:T(8,128)(2,1)}, bf16[2,128,384]{2,1,0:T(8,128)(2,1)S(1)}, u32[]{:S(2)}, u32[]{:S(2)}) collective-permute-start(bf16[2,128,384]{2,1,0:T(8,128)(2,1)} %get-tuple-element.135), channel_id=1, source_target_pairs={{4,0},{8,4},{12,8},{5,1},{9,5},{13,9},{6,2},{10,6},{14,10},{7,3},{... | collective-permute-start | bytes 589832 | tf_op jit(solution)/shard_map/ppermute | solution.py:906
  135.6 24.0 %collective-permute-start.23 = (bf16[2,128,384]{2,1,0:T(8,128)(2,1)}, bf16[2,128,384]{2,1,0:T(8,128)(2,1)S(1)}, u32[]{:S(2)}, u32[]{:S(2)}) collective-permute-start(bf16[2,128,384]{2,1,0:T(8,128)(2,1)} %get-tuple-element.136), channel_id=1, source_target_pairs={{8,0},{12,4},{9,1},{13,5},{10,2},{14,6},{11,3},{15,7},{24,16},{28,... | collective-permute-start | bytes 589832 | tf_op jit(solution)/shard_map/ppermute | solution.py:906
  136.9 25.1 %collective-permute-start.24 = (bf16[2,128,384]{2,1,0:T(8,128)(2,1)}, bf16[2,128,384]{2,1,0:T(8,128)(2,1)S(1)}, u32[]{:S(2)}, u32[]{:S(2)}) collective-permute-start(bf16[2,128,384]{2,1,0:T(8,128)(2,1)} %get-tuple-element.137), channel_id=1, source_target_pairs={{12,0},{13,1},{14,2},{15,3},{28,16},{29,17},{30,18},{31,19}} | collective-permute-start | bytes 589832 | tf_op jit(solution)/shard_map/ppermute | solution.py:906
  146.6 26.8 %collective-permute-start.20 = (bf16[384,1536]{1,0:T(8,128)(2,1)}, bf16[384,1536]{1,0:T(8,128)(2,1)S(1)}, u32[]{:S(2)}, u32[]{:S(2)}) collective-permute-start(bf16[384,1536]{1,0:T(8,128)(2,1)} %get-tuple-element.126), channel_id=1, source_target_pairs={{0,16},{16,0},{1,17},{17,1},{2,18},{18,2},{3,19},{19,3},{4,20},{20... | collective-permute-start | bytes 3538952 | tf_op jit(solution)/shard_map/ppermute | solution.py:649
  167.8 32.5 %collective-permute-start.28 = (bf16[400,1600]{1,0:T(8,128)(2,1)}, bf16[400,1600]{1,0:T(8,128)(2,1)}, u32[]{:S(2)}, u32[]{:S(2)}) collective-permute-start(bf16[400,1600]{1,0:T(8,128)(2,1)} %collective-permute-done.14.up_near), channel_id=1, source_target_pairs={{0,4},{4,0},{8,12},{12,8},{1,5},{5,1},{9,13},{13,9},{2,6},{6,2},{1... | collective-permute-start | bytes 3840008 | tf_op jit(solution)/shard_map/ppermute | solution.py:649
  176.6 35.7 %collective-permute-start.30 = (bf16[192,1536]{1,0:T(8,128)(2,1)S(1)}, bf16[192,1536]{1,0:T(8,128)(2,1)}, u32[]{:S(2)}, u32[]{:S(2)}) collective-permute-start(bf16[192,1536]{1,0:T(8,128)(2,1)S(1)} %slice.127), channel_id=1, source_target_pairs={{0,4},{4,0},{8,12},{12,8},{1,5},{5,1},{9,13},{13,9},{2,6},{6,2},{1... | collective-permute-start | bytes 1769480 | tf_op jit(solution)/shard_map/ppermute | solution.py:649
  182.3 31.9 %collective-permute-start.37 = (bf16[384,768]{1,0:T(8,128)(2,1)}, bf16[384,768]{1,0:T(8,128)(2,1)}, u32[]{:S(2)}, u32[]{:S(2)}) collective-permute-start(bf16[384,768]{1,0:T(8,128)(2,1)} %get-tuple-element.159), channel_id=1, source_target_pairs={{0,16},{16,0},{1,17},{17,1},{2,18},{18,2},{3,19},{19,3},{4,20},{20... | collective-permute-start | bytes 1769480 | tf_op jit(solution)/shard_map/ppermute | solution.py:649
  213.6 12.4 %collective-permute-start.32 = (bf16[128,1664]{1,0:T(8,128)(2,1)S(1)}, bf16[128,1664]{1,0:T(8,128)(2,1)S(1)}, u32[]{:S(2)}, u32[]{:S(2)}) collective-permute-start(bf16[128,1664]{1,0:T(8,128)(2,1)S(1)} %add_convert_fusion.1), channel_id=1, source_target_pairs={{0,2},{1,3},{2,0},{3,1},{4,6},{5,7},{6,4},{7,5},{8,10},{9,11},{10,... | collective-permute-start | bytes 1277960 | tf_op jit(solution)/shard_map/ppermute | solution.py:649
  214.2 11.8 %collective-permute-start.40 = (bf16[96,1536]{1,0:T(8,128)(2,1)S(1)}, bf16[96,1536]{1,0:T(8,128)(2,1)S(1)}, u32[]{:S(2)}, u32[]{:S(2)}) collective-permute-start(bf16[96,1536]{1,0:T(8,128)(2,1)S(1)} %slice.128), channel_id=1, source_target_pairs={{0,12},{4,8},{8,4},{12,0},{1,13},{5,9},{9,5},{13,1},{2,14},{6,10},... | collective-permute-start | bytes 884744 | tf_op jit(solution)/shard_map/ppermute | solution.py:649
  218.4 12.3 %collective-permute-start.38 = (bf16[192,768]{1,0:T(8,128)(2,1)S(1)}, bf16[192,768]{1,0:T(8,128)(2,1)S(1)}, u32[]{:S(2)}, u32[]{:S(2)}) collective-permute-start(bf16[192,768]{1,0:T(8,128)(2,1)S(1)} %slice.129), channel_id=1, source_target_pairs={{0,4},{4,0},{8,12},{12,8},{1,5},{5,1},{9,13},{13,9},{2,6},{6,2},{1... | collective-permute-start | bytes 884744 | tf_op jit(solution)/shard_map/ppermute | solution.py:649
  (47 other events, 309.0 us)
